TPU v7x, 32 devices: a whole 2x2x4 slice. The times are simulated.
32 devices in a mesh: groups: 2 (over y), tile: 8 (over z, x), cuts: 2 (over core).
Axes of the slice: x: 2, y: 2, z: 4, core: 2. Of those that a mesh axis runs over, the one named last changes fastest.
Arguments:
- slice_rows: float32 [8192, 512], P(('groups', 'tile', 'cuts')), parts along dimension 0, may hold values from -0.025625 to 0.025625
- row_owner: int32 [8192, 1], P(('groups', 'tile', 'cuts')), parts along dimension 0, may hold values from 0 to 7; in each aligned block of 256 rows (0 to 255, 256 to 511, ...) at most 48 rows name the same one
- leaf_row: int32 [8192], P(('groups', 'tile', 'cuts')), parts along dimension 0, may hold values from 0 to 511
- exponent: int32 [8192], P(('groups', 'tile', 'cuts')), parts along dimension 0, may hold values from -1 to 1
- environment: float32 [16384, 512], P(('groups', 'tile', 'cuts')), parts along dimension 0, may hold values from -0.25 to 0.25
- ordering: int32 [32, 512], P(('groups', 'tile', 'cuts')), parts along dimension 0, may hold values from 0 to 511, each once within a row
- sign_mask: int32 [32, 512], P(('groups', 'tile', 'cuts')), parts along dimension 0, may hold values 0 or 1
Outputs:
- partition: float32 [1024, 512], P(('groups', 'tile'), 'cuts'), parts along dimension 0
- log_scale: float32 [2], P('groups'), parts along dimension 0
There are 2 independent parts, one for each index of `groups`. A program takes and returns all parts, laid end to end along the dimension named above; each array names one. Nothing has to cross between parts.
Inputs may be any that keep to these rules, and one draw needn't show every extreme that they name: `row_owner`: of the rows of one device at most 48 name the same owner, and in some device exactly 48 do.
All inputs are finite; a program needn't handle non-finite values. No bound on the sum of `sign_mask` on one device may be relied on, other than what follows from the above.
Results may differ from a plain program's by a relative error of at most 0.0003.
Values sent between devices are 32-bit elements; how exact they have to be, the bound alone decides.
No kernel may reach another device: no remote copies, remote signals or barrier semaphores. Data moves between devices by JAX's collectives and lax.ppermute only.
A program may use at most 64 MiB of HBM per device.

v0:
```python
import jax
import jax.numpy as jnp
from jax import lax
from jax.sharding import PartitionSpec as P


def from_partner(x, axis, bit):
    return lax.ppermute(x, axis, [(i, i ^ 1 << bit) for i in range(lax.axis_size(axis))])


def multiply(left_factor, right_factor):
    return jnp.dot(
        left_factor,
        right_factor,
        precision=lax.Precision.HIGHEST,
        preferred_element_type=jnp.float32,
    )


def body(slice_rows, row_owner, leaf_row, exponent, environment, ordering, sign_mask):
    tiles = lax.axis_size("tile")
    cut_count = lax.axis_size("cuts")
    width = slice_rows.shape[1]
    row_count = slice_rows.shape[0]
    capacity = max(2, (3 * row_count + 2 * tiles - 1) // (2 * tiles))
    factor = jnp.where(exponent == -1, 0.5, jnp.where(exponent == 1, 2.0, 1.0)).astype(jnp.float32)
    scaled = slice_rows * factor[:, None]
    owners = row_owner[:, 0]
    hits = (owners[:, None] == jnp.arange(tiles, dtype=jnp.int32)[None, :]).astype(jnp.int32)
    before = jnp.cumsum(hits, axis=0) - hits
    position = jnp.sum(before * hits, axis=1)
    placed = owners * capacity + position
    outgoing = jnp.zeros((tiles * capacity, width), jnp.float32).at[placed].set(scaled)
    outgoing_rows = jnp.zeros((tiles * capacity,), jnp.int32).at[placed].set(leaf_row)
    arrived, arrived_rows = (
        lax.all_to_all(outgoing, "tile", split_axis=0, concat_axis=0, tiled=True),
        lax.all_to_all(outgoing_rows, "tile", split_axis=0, concat_axis=0, tiled=True),
    )
    collected = jnp.zeros((width, width), jnp.float32).at[arrived_rows].add(arrived)
    contracted = multiply(collected, environment)
    columns = jnp.arange(width, dtype=jnp.int32)
    signs = 1.0 - 2.0 * sign_mask[0].astype(jnp.float32)
    signed = (ordering[0][:, None] == columns[None, :]).astype(jnp.float32) * signs[:, None]
    product = contracted + signed
    for level in range(tiles.bit_length() - 1):
        partner = from_partner(product, "tile", level)
        upper = lax.axis_index("tile") >> level & 1 == 1
        first_part = jnp.where(upper, partner, product)
        second_part = jnp.where(upper, product, partner)
        product = multiply(first_part, second_part)
    level = 0
    partner = from_partner(product, "cuts", level)
    upper = lax.axis_index("cuts") >> level & 1 == 1
    first_part = jnp.where(upper, partner, product)
    second_part = jnp.where(upper, product, partner)
    product = multiply(first_part, second_part)
    spread = jnp.sqrt(jnp.mean(product * product) + 1e-06)
    rows_each = width // tiles
    cols_each = width // cut_count
    row_start = lax.axis_index("tile") * rows_each
    col_start = lax.axis_index("cuts") * cols_each
    own_block = lax.dynamic_slice(product, (row_start, col_start), (rows_each, cols_each))
    return (own_block / spread, jnp.log(spread).reshape(1))


def solution(mesh):
    return jax.shard_map(
        body,
        mesh=mesh,
        in_specs=(
            P(("groups", "tile", "cuts"), None),
            P(("groups", "tile", "cuts"), None),
            P(("groups", "tile", "cuts")),
            P(("groups", "tile", "cuts")),
            P(("groups", "tile", "cuts"), None),
            P(("groups", "tile", "cuts"), None),
            P(("groups", "tile", "cuts"), None),
        ),
        out_specs=(P(("groups", "tile"), "cuts"), P("groups")),
        check_vma=False,
    )
```

profile of v0, /device:TPU:0, one launch (start us, length us, event | category | flops | bytes accessed | tf_op | source)
XLA Modules:
  0.0 158.7 jit_solution(14111099245107817277)
XLA Ops:
  0.6 0.0 copy-start
  0.6 0.0 copy-start.2
  0.7 0.8 copy-done.2
  1.4 0.6 reduce-window.6
  2.0 0.2 slice_reduce_fusion
  2.2 0.1 fusion.23
  2.3 1.6 scatter_custom_fusion
  3.9 0.7 all_to_all.16
  4.6 0.0 copy-start.5
  4.6 7.4 %all-to-all-start = ((s32[8,48,1]{1,2,0:T(1,128)}), s32[8,48,1]{1,2,0:T(1,128)S(1)}, u32[]{:S(2)}, u32[]{:S(2)}) async-start(s32[8,48,1]{1,2,0:T(1,128)} %bitcast.6), calls=%async_computation | async-start | bytes 8192 | tf_op jit(solution)/shard_map/all_to_all | solution.py:37
  12.0 0.0 copy-done.5
  12.0 2.9 %scatter_custom_fusion.1 = f32[384,512]{1,0:T(8,128)} fusion(s32[256]{0:T(256)S(1)} %bitcast.28, f32[256,512]{1,0:T(8,128)} %param.7, f32[]{:T(128)} %constant.22.clone.1, f32[256]{0:T(256)S(1)} %compare_select_fusion.3), kind=kCustom, calls=%fused_computation.18 | custom fusion | flops 131072 | bytes 1311748 | tf_op jit(solution)/shard_map/scatter | solution.py:33
  14.9 3.5 %all-to-all-done = s32[8,48,1]{1,2,0:T(1,128)S(1)} async-done(((s32[8,48,1]{1,2,0:T(1,128)}), s32[8,48,1]{1,2,0:T(1,128)S(1)}, u32[]{:S(2)}, u32[]{:S(2)}) %all-to-all-start) | async-done | bytes 1568 | tf_op jit(solution)/shard_map/all_to_all | solution.py:37
  18.4 0.0 copy-start.4
  18.4 3.7 %all-to-all-start.1 = ((f32[8,48,512]{2,1,0:T(8,128)}), f32[8,48,512]{2,1,0:T(8,128)S(1)}, u32[]{:S(2)}, u32[]{:S(2)}) async-start(f32[8,48,512]{2,1,0:T(8,128)} %bitcast.7), calls=%async_computation.1 | async-start | bytes 1572864 | tf_op jit(solution)/shard_map/all_to_all | solution.py:36
  22.1 0.0 copy-done.4
  22.1 0.5 broadcast.74
  22.6 0.7 reduce.7
  23.3 0.1 all_to_all.18
  23.4 17.7 %all-to-all-done.1 = f32[8,48,512]{2,1,0:T(8,128)S(1)} async-done(((f32[8,48,512]{2,1,0:T(8,128)}), f32[8,48,512]{2,1,0:T(8,128)S(1)}, u32[]{:S(2)}, u32[]{:S(2)}) %all-to-all-start.1) | async-done | bytes 786464 | tf_op jit(solution)/shard_map/all_to_all | solution.py:36
  41.1 3.4 %scatter_custom_fusion.2 = f32[512,512]{1,0:T(8,128)S(1)} fusion(s32[384]{0:T(512)S(1)} %fusion.25, f32[384,512]{1,0:T(8,128)S(1)} %bitcast.21, f32[]{:T(128)} %constant.22.clone.1), kind=kCustom, calls=%fused_computation.20 | custom fusion | flops 196608 | bytes 1048580 | tf_op jit(solution)/shard_map/scatter-add | solution.py:39
  44.6 0.0 copy-start.3
  44.6 0.0 copy-done
  44.6 0.7 copy-done.3
  45.2 1.9 %convolution_add_fusion = f32[512,512]{1,0:T(8,128)S(1)} fusion(f32[512,512]{1,0:T(8,128)S(1)} %scatter_custom_fusion.2, f32[512,512]{1,0:T(8,128)S(1)} %copy-done, f32[512]{0:T(512)S(1)} %bitcast.24, s32[512]{0:T(512)S(1)} %bitcast.26), kind=kOutput, calls=%fused_computation.3 | convolution fusion | flops 1611399168 | bytes 3149824 | tf_op jit(solution)/shard_map/dot_general | solution.py:12
  47.1 1.3 collective-permute-start
  48.5 22.0 %collective-permute-done = f32[512,512]{1,0:T(8,128)} collective-permute-done((f32[512,512]{1,0:T(8,128)S(1)}, f32[512,512]{1,0:T(8,128)}, u32[]{:S(2)}, u32[]{:S(2)}) %collective-permute-start) | collective-permute-done | bytes 1048608 | tf_op jit(solution)/shard_map/ppermute | solution.py:8
  70.5 3.1 %fusion.9 = f32[512,512]{1,0:T(8,128)S(1)} fusion(f32[512,512]{1,0:T(8,128)S(1)} %convolution_add_fusion, f32[512,512]{1,0:T(8,128)} %collective-permute-done, pred[]{:T(512)S(6)} %eq.67), kind=kOutput, calls=%fused_computation.14 | convolution fusion | flops 1611137024 | bytes 3145729 | tf_op jit(solution)/shard_map/dot_general | solution.py:12
  73.6 0.0 copy-start.1
  73.6 0.1 collective-permute-start.1
  73.7 0.9 copy-done.1
  74.6 21.4 %collective-permute-done.1 = f32[512,512]{1,0:T(8,128)S(1)} collective-permute-done((f32[512,512]{1,0:T(8,128)S(1)}, f32[512,512]{1,0:T(8,128)S(1)}, u32[]{:S(2)}, u32[]{:S(2)}) %collective-permute-start.1) | collective-permute-done | bytes 1048608 | tf_op jit(solution)/shard_map/ppermute | solution.py:8
  96.0 3.1 %fusion.6 = f32[512,512]{1,0:T(8,128)S(1)} fusion(f32[512,512]{1,0:T(8,128)} %copy-done.1, f32[512,512]{1,0:T(8,128)S(1)} %collective-permute-done.1, pred[]{:T(512)S(6)} %eq.66), kind=kOutput, calls=%fused_computation.11 | convolution fusion | flops 1611137024 | bytes 3145729 | tf_op jit(solution)/shard_map/dot_general | solution.py:12
  99.2 2.8 %collective-permute-start.2 = (f32[512,512]{1,0:T(8,128)S(1)}, f32[512,512]{1,0:T(8,128)}, u32[]{:S(2)}, u32[]{:S(2)}) collective-permute-start(f32[512,512]{1,0:T(8,128)S(1)} %fusion.6), channel_id=1, source_target_pairs={{0,8},{2,10},{4,12},{6,14},{8,0},{10,2},{12,4},{14,6},{1,9},{3,11}... | collective-permute-start | bytes 3145736 | tf_op jit(solution)/shard_map/ppermute | solution.py:8
  102.0 44.1 %collective-permute-done.2 = f32[512,512]{1,0:T(8,128)} collective-permute-done((f32[512,512]{1,0:T(8,128)S(1)}, f32[512,512]{1,0:T(8,128)}, u32[]{:S(2)}, u32[]{:S(2)}) %collective-permute-start.2) | collective-permute-done | bytes 1048608 | tf_op jit(solution)/shard_map/ppermute | solution.py:8
  146.0 3.1 %fusion.3 = f32[512,512]{1,0:T(8,128)S(1)} fusion(f32[512,512]{1,0:T(8,128)S(1)} %fusion.6, f32[512,512]{1,0:T(8,128)} %collective-permute-done.2, pred[]{:T(512)S(6)} %eq.65), kind=kOutput, calls=%fused_computation.8 | convolution fusion | flops 1611137024 | bytes 3145729 | tf_op jit(solution)/shard_map/dot_general | solution.py:12
  149.1 0.1 collective-permute-start.3
  149.2 2.6 %collective-permute-done.3 = f32[512,512]{1,0:T(8,128)S(1)} collective-permute-done((f32[512,512]{1,0:T(8,128)S(1)}, f32[512,512]{1,0:T(8,128)S(1)}, u32[]{:S(2)}, u32[]{:S(2)}) %collective-permute-start.3) | collective-permute-done | bytes 1048608 | tf_op jit(solution)/shard_map/ppermute | solution.py:8
  151.9 3.5 %multiply_reduce_fusion = (f32[]{:T(128)}, f32[512,512]{1,0:T(8,128)}) fusion(f32[512,512]{1,0:T(8,128)S(1)} %fusion.3, f32[512,512]{1,0:T(8,128)S(1)} %collective-permute-done.3, pred[]{:T(512)S(6)} %eq.64), kind=kOutput, calls=%fused_computation.4 | convolution fusion | flops 1611661312 | bytes 3145733 | tf_op jit(solution)/shard_map/dot_general | solution.py:12
  156.1 1.5 dynamic-slice_divide_fusion
  (7 shorter events, 0.1 us)
Async XLA Ops:
  0.6 43.9 %copy-start = (f32[512,512]{1,0:T(8,128)S(1)}, f32[512,512]{1,0:T(8,128)}, u32[]{:S(2)}) copy-start(f32[512,512]{1,0:T(8,128)} %param.11) | copy-start | bytes 3145732
  0.6 0.8 copy-start.2
  4.6 7.4 %copy-start.5 = (s32[256]{0:T(256)S(1)}, s32[256]{0:T(256)}, u32[]{:S(2)}) copy-start(s32[256]{0:T(256)} %param.10) | copy-start | bytes 3076
  4.6 13.8 %all-to-all-start = ((s32[8,48,1]{1,2,0:T(1,128)}), s32[8,48,1]{1,2,0:T(1,128)S(1)}, u32[]{:S(2)}, u32[]{:S(2)}) async-start(s32[8,48,1]{1,2,0:T(1,128)} %bitcast.6), calls=%async_computation | async-start | bytes 8192 | tf_op jit(solution)/shard_map/all_to_all | solution.py:37
  18.4 3.7 %copy-start.4 = (s32[1,512]{1,0:T(1,128)S(1)}, s32[1,512]{1,0:T(1,128)}, u32[]{:S(2)}) copy-start(s32[1,512]{1,0:T(1,128)} %param.13) | copy-start | bytes 6148
  18.4 22.7 %all-to-all-start.1 = ((f32[8,48,512]{2,1,0:T(8,128)}), f32[8,48,512]{2,1,0:T(8,128)S(1)}, u32[]{:S(2)}, u32[]{:S(2)}) async-start(f32[8,48,512]{2,1,0:T(8,128)} %bitcast.7), calls=%async_computation.1 | async-start | bytes 1572864 | tf_op jit(solution)/shard_map/all_to_all | solution.py:36
  44.6 0.7 copy-start.3
  47.1 23.4 %collective-permute-start = (f32[512,512]{1,0:T(8,128)S(1)}, f32[512,512]{1,0:T(8,128)}, u32[]{:S(2)}, u32[]{:S(2)}) collective-permute-start(f32[512,512]{1,0:T(8,128)S(1)} %convolution_add_fusion), channel_id=1, source_target_pairs={{0,2},{2,0},{4,6},{6,4},{8,10},{10,8},{12,14},{14,12},{1,3},{3,1},... | collective-permute-start | bytes 3145736 | tf_op jit(solution)/shard_map/ppermute | solution.py:8
  73.6 1.0 copy-start.1
  73.6 22.4 %collective-permute-start.1 = (f32[512,512]{1,0:T(8,128)S(1)}, f32[512,512]{1,0:T(8,128)S(1)}, u32[]{:S(2)}, u32[]{:S(2)}) collective-permute-start(f32[512,512]{1,0:T(8,128)S(1)} %fusion.9), channel_id=1, source_target_pairs={{0,4},{2,6},{4,0},{6,2},{8,12},{10,14},{12,8},{14,10},{1,5},{3,7},... | collective-permute-start | bytes 3145736 | tf_op jit(solution)/shard_map/ppermute | solution.py:8
  99.2 46.8 %collective-permute-start.2 = (f32[512,512]{1,0:T(8,128)S(1)}, f32[512,512]{1,0:T(8,128)}, u32[]{:S(2)}, u32[]{:S(2)}) collective-permute-start(f32[512,512]{1,0:T(8,128)S(1)} %fusion.6), channel_id=1, source_target_pairs={{0,8},{2,10},{4,12},{6,14},{8,0},{10,2},{12,4},{14,6},{1,9},{3,11}... | collective-permute-start | bytes 3145736 | tf_op jit(solution)/shard_map/ppermute | solution.py:8
  149.1 2.7 %collective-permute-start.3 = (f32[512,512]{1,0:T(8,128)S(1)}, f32[512,512]{1,0:T(8,128)S(1)}, u32[]{:S(2)}, u32[]{:S(2)}) collective-permute-start(f32[512,512]{1,0:T(8,128)S(1)} %fusion.3), channel_id=1, source_target_pairs={{0,1},{1,0},{2,3},{3,2},{4,5},{5,4},{6,7},{7,6},{8,9},{9,8},{10,11... | collective-permute-start | bytes 3145736 | tf_op jit(solution)/shard_map/ppermute | solution.py:8
where the time goes:
time: 159 us
  waiting for transfers between devices  111 us (70%)
  starting transfers between devices  15.4 us (10%)
  matrix products  14.7 us (9%)
  other arithmetic  9.22 us (6%)
  local copies, waits for them, and re-layouts  5.38 us (3%)
  between operations  2.67 us (2%)
    ppermute x4, waiting for transfers between devices, from_partner(): lax.ppermute(x, axis, [(i, i ^ 1 << bit) for i in range(lax.axis_size(axi...  90.2 us
    all_to_all x1, waiting for transfers between devices, body(): lax.all_to_all(outgoing, 'tile', split_axis=0, concat_axis=0, tiled=True)  17.7 us
    dot_general x5, matrix products, multiply(): jnp.dot(left_factor, right_factor, precision=lax.Precision.HIGHEST, prefe...  14.7 us
    all_to_all x1, starting transfers between devices, body(): lax.all_to_all(outgoing_rows, 'tile', split_axis=0, concat_axis=0, tiled=...  7.41 us
    ppermute x4, starting transfers between devices, from_partner(): lax.ppermute(x, axis, [(i, i ^ 1 << bit) for i in range(lax.axis_size(axi...  4.27 us
    all_to_all x1, starting transfers between devices, body(): lax.all_to_all(outgoing, 'tile', split_axis=0, concat_axis=0, tiled=True)  3.68 us
    all_to_all x1, waiting for transfers between devices, body(): lax.all_to_all(outgoing_rows, 'tile', split_axis=0, concat_axis=0, tiled=...  3.5 us
    scatter-add x1, other arithmetic, body(): jnp.zeros((width, width), jnp.float32).at[arrived_rows].add(arrived)  3.43 us
  transfers between devices with their start and end apart: 6, of which 6 were waited for; matrix products, arithmetic and copies ran while one was open for 3% of the time, Pallas kernels for 0%

commit v1 on v0

v1 whole, which is shorter than its diff:
```python
import functools

import jax
import jax.numpy as jnp
from jax import lax
from jax.experimental import pallas as pl
from jax.experimental.pallas import tpu as pltpu
from jax.sharding import PartitionSpec as P

AXES = ("tile", "cuts")
VMEM = pl.BlockSpec(memory_space=pltpu.VMEM)
BF, F32 = jnp.bfloat16, jnp.float32
PAD = 8


def pairs(tiles, place):
    out = []
    for t in range(tiles):
        for c in range(2):
            to, core = place(t, c)
            out.append((t * 2 + c, to * 2 + core))
    return out


def moved(x, place):
    return lax.ppermute(x, AXES, pairs(lax.axis_size("tile"), place))


def routed(m):
    def place(t, c):
        to = t ^ (m << 1)
        return (to ^ 1, c ^ 1) if (t & 1) == c else (to, c)

    return place


def other_core(t, c):
    return t, c ^ 1


def across(level):
    return lambda t, c: (t ^ (1 << level), c)


def mul(a, b, dims=None):
    if dims is None:
        return jnp.dot(a, b, preferred_element_type=F32)
    return lax.dot_general(a, b, (dims, ((), ())), preferred_element_type=F32)


def split2(x):
    hi = x.astype(BF)
    return hi, (x - hi.astype(F32)).astype(BF)


def split3(x):
    hi = x.astype(BF)
    rest = x - hi.astype(F32)
    mid = rest.astype(BF)
    return hi, mid, (rest - mid.astype(F32)).astype(BF)


def product(a, b):
    ah, al = split2(a)
    bh, bl = split2(b)
    return mul(ah, bh) + (mul(ah, bl) + mul(al, bh))


def call(kernel, outs, args, scratch=(), flops=0):
    size = sum(a.size * 4 for a in args) + sum(o.size * 4 for o in outs)
    return pl.pallas_call(
        kernel,
        out_shape=tuple(outs),
        in_specs=[VMEM] * len(args),
        out_specs=tuple([VMEM] * len(outs)),
        scratch_shapes=list(scratch),
        cost_estimate=pl.CostEstimate(flops=flops, bytes_accessed=size, transcendentals=0),
    )(*args)


def like(*shape):
    return jax.ShapeDtypeStruct(shape, F32)


def pack_kernel(tiles, cap, rows_ref, owner_ref, leaf_ref, exp_ref, order_ref, sign_ref, *outs):
    count = rows_ref.shape[0]
    tile = lax.axis_index("tile")
    own = owner_ref[...]
    hits = own == lax.broadcasted_iota(jnp.int32, (tiles, count), 0)
    earlier = lax.broadcasted_iota(jnp.int32, (count, count), 0) < lax.broadcasted_iota(jnp.int32, (count, count), 1)
    before = mul(jnp.where(hits, 1.0, 0.0).astype(BF), jnp.where(earlier, 1.0, 0.0).astype(BF))
    position = jnp.sum(jnp.where(hits, before, 0.0), axis=0, keepdims=True).astype(jnp.int32)
    placed = (own ^ tile) * cap + position
    power = exp_ref[...]
    factor = jnp.where(power == -1, 0.5, jnp.where(power == 1, 2.0, 1.0))
    row = leaf_ref[...] + 1
    which = lax.broadcasted_iota(jnp.int32, (PAD, count), 0)
    digits = jnp.where(which == 0, row >> 4, jnp.where(which == 1, row & 15, 0)).astype(F32).astype(BF)
    hi, mid, lo = split3(rows_ref[...])
    for m, out in enumerate(outs):
        slots = lax.broadcasted_iota(jnp.int32, (2 * cap, count), 0) + m * 2 * cap
        hot = slots == placed
        pick = jnp.where(hot, factor, 0.0).astype(BF)
        out[0 : 2 * cap, :] = mul(pick, hi) + (mul(pick, mid) + mul(pick, lo))
        out[2 * cap : 2 * cap + PAD, :] = jnp.zeros((PAD, out.shape[1]), F32)
        out[2 * cap : 2 * cap + PAD, 0 : 2 * cap] = mul(digits, jnp.where(hot, 1.0, 0.0).astype(BF), ((1,), (1,)))
    signs = 1 - 2 * sign_ref[...]
    outs[0][2 * cap + 2 : 2 * cap + 3, :] = ((order_ref[...] + 1) * signs).astype(F32)


def leaf_kernel(cap, count, *refs):
    near, far, env_ref, leaf_ref = refs[:count], refs[count : 2 * count], refs[2 * count], refs[2 * count + 1]
    width = env_ref.shape[1]
    eh, el = split2(env_ref[...])
    lane = lax.broadcasted_iota(jnp.int32, (1, 128), 1)
    targets = lax.broadcasted_iota(jnp.int32, (width, 128), 0) + 1
    total = None
    for m in range(0, count, 2):
        spread, chosen = [], []
        for i in (m, m + 1):
            block = jnp.concatenate([near[i][0:cap, :], far[i][cap : 2 * cap, :]], axis=0)
            bh, bl = split2(block)
            spread.append(mul(bh, eh) + (mul(bh, el) + mul(bl, eh)))
            spread.append(jnp.zeros((128 - 2 * cap, width), F32))
            digits = jnp.where(lane < cap, near[i][2 * cap : 2 * cap + PAD, 0:128], far[i][2 * cap : 2 * cap + PAD, 0:128])
            to = (digits[0:1, :] * 16.0 + digits[1:2, :]).astype(jnp.int32)
            to = jnp.where(lane < 2 * cap, to, 0)
            chosen.append(jnp.where(targets == to, 1.0, 0.0).astype(BF))
        sh, sl = split2(jnp.concatenate(spread, axis=0))
        pick = jnp.concatenate(chosen, axis=1)
        part = mul(pick, sh) + mul(pick, sl)
        total = part if total is None else total + part
    code = near[0][2 * cap : 2 * cap + PAD, :]
    column = jnp.transpose(code)[:, 2:3]
    bond = (jnp.abs(column) - 1.0).astype(jnp.int32)
    sign = jnp.where(column < 0.0, -1.0, 1.0)
    spots = lax.broadcasted_iota(jnp.int32, (width, width), 1)
    leaf_ref[...] = total + jnp.where(spots == bond, sign, 0.0)


def half_of(core, value, half_ref):
    size = half_ref.shape[0]
    for k in range(2):

        @pl.when(core == k)
        def _(k=k):
            half_ref[...] = value[k * size : (k + 1) * size, :]


def pair_kernel(own_ref, other_ref, out_ref, half_ref):
    core = lax.axis_index("cuts")

    @pl.when(core == 1)
    def _():
        out_ref[...] = product(own_ref[...], other_ref[...])

    @pl.when(core == 0)
    def _():
        out_ref[...] = product(other_ref[...], own_ref[...])

    half_of(core, out_ref, half_ref)


def combine(bit, left_if, own_ref, near_ref, far_ref, out_ref):
    core = lax.axis_index("cuts")
    left = ((lax.axis_index("tile") >> bit) & 1) == left_if
    size = near_ref.shape[0]
    for k in range(2):
        mine, rest = slice(k * size, (k + 1) * size), slice((1 - k) * size, (2 - k) * size)

        @pl.when((core == k) & left)
        def _(mine=mine, rest=rest):
            out_ref[...] = product(own_ref[:, mine], near_ref[...]) + product(own_ref[:, rest], far_ref[...])

        @pl.when((core == k) & jnp.logical_not(left))
        def _(mine=mine, rest=rest):
            out_ref[mine, :] = product(near_ref[...], own_ref[...])
            out_ref[rest, :] = product(far_ref[...], own_ref[...])


def level_kernel(bit, own_ref, near_ref, far_ref, out_ref, half_ref):
    combine(bit, 0, own_ref, near_ref, far_ref, out_ref)
    half_of(lax.axis_index("cuts"), out_ref, half_ref)


def last_kernel(own_ref, near_ref, far_ref, block_ref, log_ref, whole_ref):
    combine(0, 1, own_ref, near_ref, far_ref, whole_ref)
    whole = whole_ref[...]
    square = jnp.sum(jnp.sum(whole * whole, axis=0, keepdims=True), axis=1, keepdims=True)
    spread = jnp.sqrt(square / whole.size + 1e-06)
    rows, cols = block_ref.shape
    start = pl.multiple_of(lax.axis_index("tile") * rows, 8)
    core = lax.axis_index("cuts")
    for k in range(whole.shape[1] // cols):

        @pl.when(core == k)
        def _(k=k):
            block_ref[...] = whole_ref[pl.ds(start, rows), k * cols : (k + 1) * cols] / spread

    log_ref[...] = jnp.log(spread)


def plain_leaf(slice_rows, row_owner, leaf_row, exponent, environment, ordering, sign_mask, tiles, cap):
    width = slice_rows.shape[1]
    factor = jnp.where(exponent == -1, 0.5, jnp.where(exponent == 1, 2.0, 1.0)).astype(F32)
    scaled = slice_rows * factor[:, None]
    owners = row_owner[:, 0]
    hits = (owners[:, None] == jnp.arange(tiles, dtype=jnp.int32)[None, :]).astype(jnp.int32)
    position = jnp.sum((jnp.cumsum(hits, axis=0) - hits) * hits, axis=1)
    placed = owners * cap + position
    outgoing = jnp.zeros((tiles * cap, width), F32).at[placed].set(scaled)
    outgoing_rows = jnp.zeros((tiles * cap,), jnp.int32).at[placed].set(leaf_row)
    arrived = lax.all_to_all(outgoing, "tile", split_axis=0, concat_axis=0, tiled=True)
    arrived_rows = lax.all_to_all(outgoing_rows, "tile", split_axis=0, concat_axis=0, tiled=True)
    collected = jnp.zeros((width, width), F32).at[arrived_rows].add(arrived)
    contracted = jnp.dot(collected, environment, precision=lax.Precision.HIGHEST, preferred_element_type=F32)
    columns = jnp.arange(width, dtype=jnp.int32)
    signs = 1.0 - 2.0 * sign_mask[0].astype(F32)
    leaf = contracted + (ordering[0][:, None] == columns[None, :]).astype(F32) * signs[:, None]
    return moved(leaf, routed(0))


def packed_leaf(slice_rows, row_owner, leaf_row, exponent, environment, ordering, sign_mask, tiles, cap):
    count, width = slice_rows.shape
    sets = tiles // 2
    env = moved(environment, routed(0))
    line = lambda a: a.reshape(1, count)
    outgoing = call(
        functools.partial(pack_kernel, tiles, cap),
        [like(2 * cap + PAD, width)] * sets,
        (slice_rows, line(row_owner), line(leaf_row), line(exponent), ordering, sign_mask),
        flops=6 * tiles * cap * count * width,
    )
    near = [None] * sets
    for m in sorted(range(sets), key=lambda m: -m):
        near[m] = moved(outgoing[m], routed(m))
    far = [moved(block, other_core) for block in near]
    (leaf,) = call(
        functools.partial(leaf_kernel, cap, sets),
        [like(width, width)],
        (*near, *far, env),
        flops=10 * width**3,
    )
    return leaf


def body(slice_rows, row_owner, leaf_row, exponent, environment, ordering, sign_mask):
    tiles = lax.axis_size("tile")
    count, width = slice_rows.shape
    cap = max(2, (3 * count + 2 * tiles - 1) // (2 * tiles))
    narrow = cap % 8 == 0 and 2 * cap <= 128 and 2 <= tiles // 2 <= 8 and width % 128 == 0
    make_leaf = packed_leaf if narrow else plain_leaf
    leaf = make_leaf(slice_rows, row_owner, leaf_row, exponent, environment, ordering, sign_mask, tiles, cap)
    whole, half = like(width, width), like(width // 2, width)
    cost = 6 * width**3
    own, part = call(pair_kernel, [whole, half], (leaf, moved(leaf, other_core)), flops=cost)
    for level in range(1, tiles.bit_length() - 1):
        near = moved(part, across(level))
        far = moved(near, other_core)
        own, part = call(functools.partial(level_kernel, level), [whole, half], (own, near, far), flops=cost)
    near = moved(part, across(0))
    far = moved(near, other_core)
    block, log = call(
        last_kernel,
        [like(width // tiles, width // 2), like(1, 1)],
        (own, near, far),
        scratch=[pltpu.VMEM((width, width), F32)],
        flops=cost,
    )
    return block, log.reshape(1)


def solution(mesh):
    return jax.shard_map(
        body,
        mesh=mesh,
        in_specs=(
            P(("groups", "tile", "cuts"), None),
            P(("groups", "tile", "cuts"), None),
            P(("groups", "tile", "cuts")),
            P(("groups", "tile", "cuts")),
            P(("groups", "tile", "cuts"), None),
            P(("groups", "tile", "cuts"), None),
            P(("groups", "tile", "cuts"), None),
        ),
        out_specs=(P(("groups", "tile"), "cuts"), P("groups")),
        check_vma=False,
    )
```

time: 159 us -> 122 us (0.77)
  waiting for transfers between devices: 111 us -> 74.6 us
  Pallas kernels: 0 us -> 21.8 us
  matrix products: 14.7 us -> 0 us
  other arithmetic: 9.22 us -> 0 us
  starting transfers between devices: 15.4 us -> 19.4 us
  between operations: 2.67 us -> 0.75 us
    pallas_call x0 -> x6, Pallas kernels: none -> 21.8 us  [call(): pl.pallas_call(kernel, out_shape=tuple(outs), in_specs=[VMEM] * len(args)...]
    all_to_all x2 -> x0, waiting for transfers between devices: 21.2 us -> none  [the longest x1 17.7 us: body(): lax.all_to_all(outgoing, 'tile', split_axis=0, concat_axis=0, tiled=True)]
    ppermute x4 -> x16, waiting for transfers between devices: 90.2 us -> 74.6 us  [moved(): return lax.ppermute(x, AXES, pairs(lax.axis_size('tile'), place))]
    ppermute x4 -> x16, starting transfers between devices: 4.27 us -> 19.4 us  [moved(): return lax.ppermute(x, AXES, pairs(lax.axis_size('tile'), place))]
    dot_general x5 -> x0, matrix products: 14.7 us -> none  [multiply(): jnp.dot(left_factor, right_factor, precision=lax.Precision.HIGHEST, prefe...]
    all_to_all x2 -> x0, starting transfers between devices: 11.1 us -> none  [the longest x1 7.41 us: body(): lax.all_to_all(outgoing_rows, 'tile', split_axis=0, concat_axis=0, tiled=...]
    scatter-add x1 -> x0, other arithmetic: 3.43 us -> none  [body(): jnp.zeros((width, width), jnp.float32).at[arrived_rows].add(arrived)]
    scatter x1 -> x0, other arithmetic: 2.9 us -> none  [body(): jnp.zeros((tiles * capacity, width), jnp.float32).at[placed].set(scaled)]
  transfers between devices with their start and end apart: 6 -> 16, of which waited for: 6 -> 11; matrix products, arithmetic and copies ran while one was open for 3% -> 0% of each run, Pallas kernels for 0% -> 2%
where the time goes in v1:
time: 122 us
  waiting for transfers between devices  74.6 us (61%)
  Pallas kernels  21.8 us (18%)
  starting transfers between devices  19.4 us (16%)
  local copies, waits for them, and re-layouts  4.95 us (4%)
    ppermute x16, waiting for transfers between devices, moved(): return lax.ppermute(x, AXES, pairs(lax.axis_size('tile'), place))  74.6 us
    pallas_call x6, Pallas kernels, call(): pl.pallas_call(kernel, out_shape=tuple(outs), in_specs=[VMEM] * len(args)...  21.8 us
    ppermute x16, starting transfers between devices, moved(): return lax.ppermute(x, AXES, pairs(lax.axis_size('tile'), place))  19.4 us
    unnamed x32, local copies, waits for them, and re-layouts  4.95 us
  transfers between devices with their start and end apart: 16, of which 11 were waited for; matrix products, arithmetic and copies ran while one was open for 0% of the time, Pallas kernels for 2%

profile of v1, /device:TPU:0, one launch (start us, length us, event | category | flops | bytes accessed | tf_op | source)
XLA Modules:
  0.0 121.6 jit_solution(17732273827287920000)
XLA Ops:
  0.6 4.3 %collective-permute-start.8 = (f32[512,512]{1,0:T(8,128)}, f32[512,512]{1,0:T(8,128)S(1)}, u32[]{:S(2)}, u32[]{:S(2)}) collective-permute-start(f32[512,512]{1,0:T(8,128)} %param.11), channel_id=1, source_target_pairs={{0,3},{1,1},{2,2},{3,0},{4,7},{5,5},{6,6},{7,4},{8,11},{9,9},{10,1... | collective-permute-start | bytes 3145736 | tf_op jit(solution)/shard_map/ppermute | solution.py:26
  5.0 2.6 %shard_map.86 = (f32[104,512]{1,0:T(8,128)}, f32[104,512]{1,0:T(8,128)}, f32[104,512]{1,0:T(8,128)}, f32[104,512]{1,0:T(8,128)}) custom-call(f32[256,512]{1,0:T(8,128)} %rows_ref.1, s32[1,256]{1,0:T(1,128)} %bitcast.4, s32[1,256]{1,0:T(1,128)} %bitcast.5, s32[1,256]{1,0:T(1,128)} %bitcast.6, s32[1,512]{1,0:T(1,128)} %order_ref.1, s32[1,512]{1,0:T(1,128)} %sign_ref.1), custom_call_target="tpu_custom_call" | custom-call | flops 301989888 | bytes 1383424 | tf_op jit(solution)/shard_map/pallas_call | solution.py:71
  7.5 1.9 %collective-permute-start = (f32[104,512]{1,0:T(8,128)}, f32[104,512]{1,0:T(8,128)S(1)}, u32[]{:S(2)}, u32[]{:S(2)}) collective-permute-start(f32[104,512]{1,0:T(8,128)} %get-tuple-element.14), channel_id=1, source_target_pairs={{0,3},{1,1},{2,2},{3,0},{4,7},{5,5},{6,6},{7,4},{8,11},{9,9},{10,1... | collective-permute-start | bytes 638984 | tf_op jit(solution)/shard_map/ppermute | solution.py:26
  9.4 2.8 %collective-permute-start.1 = (f32[104,512]{1,0:T(8,128)}, f32[104,512]{1,0:T(8,128)S(1)}, u32[]{:S(2)}, u32[]{:S(2)}) collective-permute-start(f32[104,512]{1,0:T(8,128)} %get-tuple-element.15), channel_id=1, source_target_pairs={{0,7},{1,5},{2,6},{3,4},{4,3},{5,1},{6,2},{7,0},{8,15},{9,13},{10,... | collective-permute-start | bytes 638984 | tf_op jit(solution)/shard_map/ppermute | solution.py:26
  12.2 2.8 %collective-permute-start.2 = (f32[104,512]{1,0:T(8,128)}, f32[104,512]{1,0:T(8,128)S(1)}, u32[]{:S(2)}, u32[]{:S(2)}) collective-permute-start(f32[104,512]{1,0:T(8,128)} %get-tuple-element.16), channel_id=1, source_target_pairs={{0,11},{1,9},{2,10},{3,8},{4,15},{5,13},{6,14},{7,12},{8,3},{9,1},... | collective-permute-start | bytes 638984 | tf_op jit(solution)/shard_map/ppermute | solution.py:26
  15.1 0.6 collective-permute-start.3
  15.7 7.7 %collective-permute-done.refs_0_ = f32[104,512]{1,0:T(8,128)S(1)} collective-permute-done((f32[104,512]{1,0:T(8,128)}, f32[104,512]{1,0:T(8,128)S(1)}, u32[]{:S(2)}, u32[]{:S(2)}) %collective-permute-start) | collective-permute-done | bytes 213024 | tf_op jit(solution)/shard_map/ppermute | solution.py:26
  23.3 0.0 copy-start.8
  23.3 0.0 collective-permute-start.4
  23.3 0.0 collective-permute-done.1.refs_1_
  23.3 0.0 copy-start.9
  23.4 0.5 collective-permute-start.5
  23.9 7.1 %collective-permute-done.2.refs_2_ = f32[104,512]{1,0:T(8,128)S(1)} collective-permute-done((f32[104,512]{1,0:T(8,128)}, f32[104,512]{1,0:T(8,128)S(1)}, u32[]{:S(2)}, u32[]{:S(2)}) %collective-permute-start.2) | collective-permute-done | bytes 213024 | tf_op jit(solution)/shard_map/ppermute | solution.py:26
  30.9 0.0 copy-start.10
  30.9 0.0 collective-permute-start.6
  30.9 0.0 collective-permute-done.3.refs_3_
  30.9 0.0 copy-start.11
  31.0 0.5 collective-permute-start.7
  31.4 0.0 collective-permute-done.4.refs_4_
  31.5 0.0 copy-start.12
  31.5 0.0 collective-permute-done.5.refs_5_
  31.5 0.0 copy-start.13
  31.5 0.9 collective-permute-done.6.refs_6_
  32.4 0.0 copy-start.14
  32.4 0.3 collective-permute-done.7.refs_7_
  32.7 0.0 copy-start.15
  32.7 0.0 collective-permute-done.8.refs_8_
  32.7 0.0 copy-done.8
  32.7 0.0 copy-done.9
  32.7 0.0 copy-done.10
  32.7 0.0 copy-done.11
  32.7 0.0 copy-done.12
  32.8 0.0 copy-done.13
  32.8 0.3 copy-done.14
  33.1 0.3 copy-done.15
  33.4 0.0 copy-start
  33.4 1.0 copy-done
  34.3 4.8 %shard_map.87.own_ref = f32[512,512]{1,0:T(8,128)} custom-call(f32[104,512]{1,0:T(8,128)} %copy-done.8, f32[104,512]{1,0:T(8,128)} %copy-done.9, f32[104,512]{1,0:T(8,128)} %copy-done.10, f32[104,512]{1,0:T(8,128)} %copy-done.11, f32[104,512]{1,0:T(8,128)} %copy-done.12, f32[104,512]{1,0:T(8,128)} %copy-done.13, f32[104,512]{1,0:T(8,128)} %copy-done.14, ...), custom_call_target="tpu_custom_call" | custom-call | flops 1342177280 | bytes 3801088 | tf_op jit(solution)/shard_map/pallas_call | solution.py:71
  39.2 0.2 collective-permute-start.9
  39.4 2.7 %collective-permute-done.9.other_ref = f32[512,512]{1,0:T(8,128)S(1)} collective-permute-done((f32[512,512]{1,0:T(8,128)}, f32[512,512]{1,0:T(8,128)S(1)}, u32[]{:S(2)}, u32[]{:S(2)}) %collective-permute-start.9) | collective-permute-done | bytes 1048608 | tf_op jit(solution)/shard_map/ppermute | solution.py:26
  42.0 0.0 copy-start.1
  42.0 1.0 copy-done.1
  43.0 3.7 %shard_map.88 = (f32[512,512]{1,0:T(8,128)}, f32[256,512]{1,0:T(8,128)}) custom-call(f32[512,512]{1,0:T(8,128)} %shard_map.87.own_ref, f32[512,512]{1,0:T(8,128)} %copy-done.1), custom_call_target="tpu_custom_call" | custom-call | flops 805306368 | bytes 3670016 | tf_op jit(solution)/shard_map/pallas_call | solution.py:71
  46.7 2.9 %collective-permute-start.10 = (f32[256,512]{1,0:T(8,128)}, f32[256,512]{1,0:T(8,128)S(1)}, u32[]{:S(2)}, u32[]{:S(2)}) collective-permute-start(f32[256,512]{1,0:T(8,128)} %get-tuple-element.19), channel_id=1, source_target_pairs={{0,4},{1,5},{2,6},{3,7},{4,0},{5,1},{6,2},{7,3},{8,12},{9,13},{10,... | collective-permute-start | bytes 1572872 | tf_op jit(solution)/shard_map/ppermute | solution.py:26
  49.6 12.5 %collective-permute-done.10.near_ref = f32[256,512]{1,0:T(8,128)S(1)} collective-permute-done((f32[256,512]{1,0:T(8,128)}, f32[256,512]{1,0:T(8,128)S(1)}, u32[]{:S(2)}, u32[]{:S(2)}) %collective-permute-start.10) | collective-permute-done | bytes 524320 | tf_op jit(solution)/shard_map/ppermute | solution.py:26
  62.1 0.0 collective-permute-start.11
  62.1 1.9 %collective-permute-done.11.far_ref = f32[256,512]{1,0:T(8,128)S(1)} collective-permute-done((f32[256,512]{1,0:T(8,128)S(1)}, f32[256,512]{1,0:T(8,128)S(1)}, u32[]{:S(2)}, u32[]{:S(2)}) %collective-permute-start.11) | collective-permute-done | bytes 524320 | tf_op jit(solution)/shard_map/ppermute | solution.py:26
  64.0 0.0 copy-done.2
  64.0 0.8 copy-done.5
  64.8 3.7 %shard_map.89 = (f32[512,512]{1,0:T(8,128)}, f32[256,512]{1,0:T(8,128)}) custom-call(f32[512,512]{1,0:T(8,128)} %get-tuple-element.18.own_ref, f32[256,512]{1,0:T(8,128)} %copy-done.2, f32[256,512]{1,0:T(8,128)} %copy-done.5), custom_call_target="tpu_custom_call" | custom-call | flops 805306368 | bytes 3670016 | tf_op jit(solution)/shard_map/pallas_call | solution.py:71
  68.5 2.8 %collective-permute-start.12 = (f32[256,512]{1,0:T(8,128)}, f32[256,512]{1,0:T(8,128)S(1)}, u32[]{:S(2)}, u32[]{:S(2)}) collective-permute-start(f32[256,512]{1,0:T(8,128)} %get-tuple-element.21), channel_id=1, source_target_pairs={{0,8},{1,9},{2,10},{3,11},{4,12},{5,13},{6,14},{7,15},{8,0},{9,1},... | collective-permute-start | bytes 1572872 | tf_op jit(solution)/shard_map/ppermute | solution.py:26
  71.3 23.6 %collective-permute-done.12.near_ref = f32[256,512]{1,0:T(8,128)S(1)} collective-permute-done((f32[256,512]{1,0:T(8,128)}, f32[256,512]{1,0:T(8,128)S(1)}, u32[]{:S(2)}, u32[]{:S(2)}) %collective-permute-start.12) | collective-permute-done | bytes 524320 | tf_op jit(solution)/shard_map/ppermute | solution.py:26
  94.9 0.0 collective-permute-start.13
  94.9 1.9 %collective-permute-done.13.far_ref = f32[256,512]{1,0:T(8,128)S(1)} collective-permute-done((f32[256,512]{1,0:T(8,128)S(1)}, f32[256,512]{1,0:T(8,128)S(1)}, u32[]{:S(2)}, u32[]{:S(2)}) %collective-permute-start.13) | collective-permute-done | bytes 524320 | tf_op jit(solution)/shard_map/ppermute | solution.py:26
  96.8 0.0 copy-done.3
  96.8 0.8 copy-done.6
  97.6 3.7 %shard_map.90 = (f32[512,512]{1,0:T(8,128)}, f32[256,512]{1,0:T(8,128)}) custom-call(f32[512,512]{1,0:T(8,128)} %get-tuple-element.20.own_ref, f32[256,512]{1,0:T(8,128)} %copy-done.3, f32[256,512]{1,0:T(8,128)} %copy-done.6), custom_call_target="tpu_custom_call" | custom-call | flops 805306368 | bytes 3670016 | tf_op jit(solution)/shard_map/pallas_call | solution.py:71
  101.3 0.0 collective-permute-start.14
  101.3 14.2 %collective-permute-done.14.near_ref = f32[256,512]{1,0:T(8,128)S(1)} collective-permute-done((f32[256,512]{1,0:T(8,128)}, f32[256,512]{1,0:T(8,128)S(1)}, u32[]{:S(2)}, u32[]{:S(2)}) %collective-permute-start.14) | collective-permute-done | bytes 524320 | tf_op jit(solution)/shard_map/ppermute | solution.py:26
  115.5 0.0 collective-permute-start.15
  115.5 1.9 %collective-permute-done.15.far_ref = f32[256,512]{1,0:T(8,128)S(1)} collective-permute-done((f32[256,512]{1,0:T(8,128)S(1)}, f32[256,512]{1,0:T(8,128)S(1)}, u32[]{:S(2)}, u32[]{:S(2)}) %collective-permute-start.15) | collective-permute-done | bytes 524320 | tf_op jit(solution)/shard_map/ppermute | solution.py:26
  117.4 0.0 copy-done.4
  117.4 0.8 copy-done.7
  118.2 3.4 %shard_map.91 = (f32[64,256]{1,0:T(8,128)}, f32[1,1]{1,0:T(1,128)}) custom-call(f32[512,512]{1,0:T(8,128)} %get-tuple-element.22.own_ref, f32[256,512]{1,0:T(8,128)} %copy-done.4, f32[256,512]{1,0:T(8,128)} %copy-done.7), custom_call_target="tpu_custom_call" | custom-call | flops 805306368 | bytes 2162692 | tf_op jit(solution)/shard_map/pallas_call | solution.py:71
  (6 shorter events, 0.0 us)
Async XLA Ops:
  0.6 32.1 %collective-permute-start.8 = (f32[512,512]{1,0:T(8,128)}, f32[512,512]{1,0:T(8,128)S(1)}, u32[]{:S(2)}, u32[]{:S(2)}) collective-permute-start(f32[512,512]{1,0:T(8,128)} %param.11), channel_id=1, source_target_pairs={{0,3},{1,1},{2,2},{3,0},{4,7},{5,5},{6,6},{7,4},{8,11},{9,9},{10,1... | collective-permute-start | bytes 3145736 | tf_op jit(solution)/shard_map/ppermute | solution.py:26
  7.5 15.8 %collective-permute-start = (f32[104,512]{1,0:T(8,128)}, f32[104,512]{1,0:T(8,128)S(1)}, u32[]{:S(2)}, u32[]{:S(2)}) collective-permute-start(f32[104,512]{1,0:T(8,128)} %get-tuple-element.14), channel_id=1, source_target_pairs={{0,3},{1,1},{2,2},{3,0},{4,7},{5,5},{6,6},{7,4},{8,11},{9,9},{10,1... | collective-permute-start | bytes 638984 | tf_op jit(solution)/shard_map/ppermute | solution.py:26
  9.4 13.9 %collective-permute-start.1 = (f32[104,512]{1,0:T(8,128)}, f32[104,512]{1,0:T(8,128)S(1)}, u32[]{:S(2)}, u32[]{:S(2)}) collective-permute-start(f32[104,512]{1,0:T(8,128)} %get-tuple-element.15), channel_id=1, source_target_pairs={{0,7},{1,5},{2,6},{3,4},{4,3},{5,1},{6,2},{7,0},{8,15},{9,13},{10,... | collective-permute-start | bytes 638984 | tf_op jit(solution)/shard_map/ppermute | solution.py:26
  12.2 18.7 %collective-permute-start.2 = (f32[104,512]{1,0:T(8,128)}, f32[104,512]{1,0:T(8,128)S(1)}, u32[]{:S(2)}, u32[]{:S(2)}) collective-permute-start(f32[104,512]{1,0:T(8,128)} %get-tuple-element.16), channel_id=1, source_target_pairs={{0,11},{1,9},{2,10},{3,8},{4,15},{5,13},{6,14},{7,12},{8,3},{9,1},... | collective-permute-start | bytes 638984 | tf_op jit(solution)/shard_map/ppermute | solution.py:26
  15.1 15.9 %collective-permute-start.3 = (f32[104,512]{1,0:T(8,128)}, f32[104,512]{1,0:T(8,128)S(1)}, u32[]{:S(2)}, u32[]{:S(2)}) collective-permute-start(f32[104,512]{1,0:T(8,128)} %get-tuple-element.17), channel_id=1, source_target_pairs={{0,15},{1,13},{2,14},{3,12},{4,11},{5,9},{6,10},{7,8},{8,7},{9,5},... | collective-permute-start | bytes 638984 | tf_op jit(solution)/shard_map/ppermute | solution.py:26
  23.3 9.4 %copy-start.8 = (f32[104,512]{1,0:T(8,128)}, f32[104,512]{1,0:T(8,128)S(1)}, u32[]{:S(2)}) copy-start(f32[104,512]{1,0:T(8,128)S(1)} %collective-permute-done.refs_0_) | copy-start | bytes 638980
  23.3 8.1 %collective-permute-start.4 = (f32[104,512]{1,0:T(8,128)S(1)}, f32[104,512]{1,0:T(8,128)S(1)}, u32[]{:S(2)}, u32[]{:S(2)}) collective-permute-start(f32[104,512]{1,0:T(8,128)S(1)} %collective-permute-done.refs_0_), channel_id=1, source_target_pairs={{0,1},{1,0},{2,3},{3,2},{4,5},{5,4},{6,7},{7,6},{8,9},{9,8},{10,11... | collective-permute-start | bytes 638984 | tf_op jit(solution)/shard_map/ppermute | solution.py:26
  23.3 9.4 %copy-start.9 = (f32[104,512]{1,0:T(8,128)}, f32[104,512]{1,0:T(8,128)S(1)}, u32[]{:S(2)}) copy-start(f32[104,512]{1,0:T(8,128)S(1)} %collective-permute-done.1.refs_1_) | copy-start | bytes 638980
  23.4 8.1 %collective-permute-start.5 = (f32[104,512]{1,0:T(8,128)S(1)}, f32[104,512]{1,0:T(8,128)S(1)}, u32[]{:S(2)}, u32[]{:S(2)}) collective-permute-start(f32[104,512]{1,0:T(8,128)S(1)} %collective-permute-done.1.refs_1_), channel_id=1, source_target_pairs={{0,1},{1,0},{2,3},{3,2},{4,5},{5,4},{6,7},{7,6},{8,9},{9,8},{10,11... | collective-permute-start | bytes 638984 | tf_op jit(solution)/shard_map/ppermute | solution.py:26
  30.9 1.8 %copy-start.10 = (f32[104,512]{1,0:T(8,128)}, f32[104,512]{1,0:T(8,128)S(1)}, u32[]{:S(2)}) copy-start(f32[104,512]{1,0:T(8,128)S(1)} %collective-permute-done.2.refs_2_) | copy-start | bytes 638980
  30.9 1.5 %collective-permute-start.6 = (f32[104,512]{1,0:T(8,128)S(1)}, f32[104,512]{1,0:T(8,128)S(1)}, u32[]{:S(2)}, u32[]{:S(2)}) collective-permute-start(f32[104,512]{1,0:T(8,128)S(1)} %collective-permute-done.2.refs_2_), channel_id=1, source_target_pairs={{0,1},{1,0},{2,3},{3,2},{4,5},{5,4},{6,7},{7,6},{8,9},{9,8},{10,11... | collective-permute-start | bytes 638984 | tf_op jit(solution)/shard_map/ppermute | solution.py:26
  30.9 1.8 %copy-start.11 = (f32[104,512]{1,0:T(8,128)}, f32[104,512]{1,0:T(8,128)S(1)}, u32[]{:S(2)}) copy-start(f32[104,512]{1,0:T(8,128)S(1)} %collective-permute-done.3.refs_3_) | copy-start | bytes 638980
  31.0 1.8 %collective-permute-start.7 = (f32[104,512]{1,0:T(8,128)S(1)}, f32[104,512]{1,0:T(8,128)S(1)}, u32[]{:S(2)}, u32[]{:S(2)}) collective-permute-start(f32[104,512]{1,0:T(8,128)S(1)} %collective-permute-done.3.refs_3_), channel_id=1, source_target_pairs={{0,1},{1,0},{2,3},{3,2},{4,5},{5,4},{6,7},{7,6},{8,9},{9,8},{10,11... | collective-permute-start | bytes 638984 | tf_op jit(solution)/shard_map/ppermute | solution.py:26
  31.5 1.3 %copy-start.12 = (f32[104,512]{1,0:T(8,128)}, f32[104,512]{1,0:T(8,128)S(1)}, u32[]{:S(2)}) copy-start(f32[104,512]{1,0:T(8,128)S(1)} %collective-permute-done.4.refs_4_) | copy-start | bytes 638980
  31.5 1.3 %copy-start.13 = (f32[104,512]{1,0:T(8,128)}, f32[104,512]{1,0:T(8,128)S(1)}, u32[]{:S(2)}) copy-start(f32[104,512]{1,0:T(8,128)S(1)} %collective-permute-done.5.refs_5_) | copy-start | bytes 638980
  32.4 0.7 copy-start.14
  32.7 0.7 copy-start.15
  33.4 1.0 copy-start
  39.2 2.9 %collective-permute-start.9 = (f32[512,512]{1,0:T(8,128)}, f32[512,512]{1,0:T(8,128)S(1)}, u32[]{:S(2)}, u32[]{:S(2)}) collective-permute-start(f32[512,512]{1,0:T(8,128)} %shard_map.87.own_ref), channel_id=1, source_target_pairs={{0,1},{1,0},{2,3},{3,2},{4,5},{5,4},{6,7},{7,6},{8,9},{9,8},{10,11... | collective-permute-start | bytes 3145736 | tf_op jit(solution)/shard_map/ppermute | solution.py:26
  42.0 1.0 copy-start.1
  46.7 15.4 %collective-permute-start.10 = (f32[256,512]{1,0:T(8,128)}, f32[256,512]{1,0:T(8,128)S(1)}, u32[]{:S(2)}, u32[]{:S(2)}) collective-permute-start(f32[256,512]{1,0:T(8,128)} %get-tuple-element.19), channel_id=1, source_target_pairs={{0,4},{1,5},{2,6},{3,7},{4,0},{5,1},{6,2},{7,3},{8,12},{9,13},{10,... | collective-permute-start | bytes 1572872 | tf_op jit(solution)/shard_map/ppermute | solution.py:26
  62.1 1.9 %copy-start.2 = (f32[256,512]{1,0:T(8,128)}, f32[256,512]{1,0:T(8,128)S(1)}, u32[]{:S(2)}) copy-start(f32[256,512]{1,0:T(8,128)S(1)} %collective-permute-done.10.near_ref) | copy-start | bytes 1572868
  62.1 1.9 %collective-permute-start.11 = (f32[256,512]{1,0:T(8,128)S(1)}, f32[256,512]{1,0:T(8,128)S(1)}, u32[]{:S(2)}, u32[]{:S(2)}) collective-permute-start(f32[256,512]{1,0:T(8,128)S(1)} %collective-permute-done.10.near_ref), channel_id=1, source_target_pairs={{0,1},{1,0},{2,3},{3,2},{4,5},{5,4},{6,7},{7,6},{8,9},{9,8},{10,11... | collective-permute-start | bytes 1572872 | tf_op jit(solution)/shard_map/ppermute | solution.py:26
  64.0 0.8 copy-start.5
  68.5 26.4 %collective-permute-start.12 = (f32[256,512]{1,0:T(8,128)}, f32[256,512]{1,0:T(8,128)S(1)}, u32[]{:S(2)}, u32[]{:S(2)}) collective-permute-start(f32[256,512]{1,0:T(8,128)} %get-tuple-element.21), channel_id=1, source_target_pairs={{0,8},{1,9},{2,10},{3,11},{4,12},{5,13},{6,14},{7,15},{8,0},{9,1},... | collective-permute-start | bytes 1572872 | tf_op jit(solution)/shard_map/ppermute | solution.py:26
  94.9 1.9 %copy-start.3 = (f32[256,512]{1,0:T(8,128)}, f32[256,512]{1,0:T(8,128)S(1)}, u32[]{:S(2)}) copy-start(f32[256,512]{1,0:T(8,128)S(1)} %collective-permute-done.12.near_ref) | copy-start | bytes 1572868
  94.9 1.9 %collective-permute-start.13 = (f32[256,512]{1,0:T(8,128)S(1)}, f32[256,512]{1,0:T(8,128)S(1)}, u32[]{:S(2)}, u32[]{:S(2)}) collective-permute-start(f32[256,512]{1,0:T(8,128)S(1)} %collective-permute-done.12.near_ref), channel_id=1, source_target_pairs={{0,1},{1,0},{2,3},{3,2},{4,5},{5,4},{6,7},{7,6},{8,9},{9,8},{10,11... | collective-permute-start | bytes 1572872 | tf_op jit(solution)/shard_map/ppermute | solution.py:26
  96.8 0.8 copy-start.6
  101.3 14.2 %collective-permute-start.14 = (f32[256,512]{1,0:T(8,128)}, f32[256,512]{1,0:T(8,128)S(1)}, u32[]{:S(2)}, u32[]{:S(2)}) collective-permute-start(f32[256,512]{1,0:T(8,128)} %get-tuple-element.23), channel_id=1, source_target_pairs={{0,2},{1,3},{2,0},{3,1},{4,6},{5,7},{6,4},{7,5},{8,10},{9,11},{10,... | collective-permute-start | bytes 1572872 | tf_op jit(solution)/shard_map/ppermute | solution.py:26
  115.5 1.9 %copy-start.4 = (f32[256,512]{1,0:T(8,128)}, f32[256,512]{1,0:T(8,128)S(1)}, u32[]{:S(2)}) copy-start(f32[256,512]{1,0:T(8,128)S(1)} %collective-permute-done.14.near_ref) | copy-start | bytes 1572868
  115.5 1.9 %collective-permute-start.15 = (f32[256,512]{1,0:T(8,128)S(1)}, f32[256,512]{1,0:T(8,128)S(1)}, u32[]{:S(2)}, u32[]{:S(2)}) collective-permute-start(f32[256,512]{1,0:T(8,128)S(1)} %collective-permute-done.14.near_ref), channel_id=1, source_target_pairs={{0,1},{1,0},{2,3},{3,2},{4,5},{5,4},{6,7},{7,6},{8,9},{9,8},{10,11... | collective-permute-start | bytes 1572872 | tf_op jit(solution)/shard_map/ppermute | solution.py:26
  117.4 0.8 copy-start.7

commit v2 on v1

--- a/solution.py
+++ b/solution.py
@@ -11,6 +11,7 @@
 VMEM = pl.BlockSpec(memory_space=pltpu.VMEM)
 BF, F32 = jnp.bfloat16, jnp.float32
 PAD = 8
+GRANT = 16 << 20
 
 
 def pairs(tiles, place):
@@ -66,15 +67,18 @@
     return mul(ah, bh) + (mul(ah, bl) + mul(al, bh))
 
 
-def call(kernel, outs, args, scratch=(), flops=0):
+def call(kernel, outs, args, scratch=(), flops=0, held=True, kept=True):
     size = sum(a.size * 4 for a in args) + sum(o.size * 4 for o in outs)
+    if held:
+        args = [pltpu.with_memory_space_constraint(a, pltpu.VMEM) for a in args]
     return pl.pallas_call(
         kernel,
-        out_shape=tuple(outs),
+        out_shape=tuple(pltpu.VMEM(o.shape, o.dtype) if kept else o for o in outs),
         in_specs=[VMEM] * len(args),
         out_specs=tuple([VMEM] * len(outs)),
         scratch_shapes=list(scratch),
         cost_estimate=pl.CostEstimate(flops=flops, bytes_accessed=size, transcendentals=0),
+        compiler_params=pltpu.CompilerParams(vmem_limit_bytes=GRANT),
     )(*args)
 
 
@@ -230,6 +234,7 @@
         [like(2 * cap + PAD, width)] * sets,
         (slice_rows, line(row_owner), line(leaf_row), line(exponent), ordering, sign_mask),
         flops=6 * tiles * cap * count * width,
+        held=False,
     )
     near = [None] * sets
     for m in sorted(range(sets), key=lambda m: -m):
@@ -266,6 +271,7 @@
         (own, near, far),
         scratch=[pltpu.VMEM((width, width), F32)],
         flops=cost,
+        kept=False,
     )
     return block, log.reshape(1)
 

time: 122 us -> 104 us (0.85)
  Pallas kernels: 21.8 us -> 7.71 us
  local copies, waits for them, and re-layouts: 4.95 us -> 3.08 us
  waiting for transfers between devices: 74.6 us -> 73.1 us
    pallas_call x6, Pallas kernels: 21.8 us -> 7.71 us  [call(): pl.pallas_call(kernel, out_shape=tuple((pltpu.VMEM(o.shape, o.dtype) if k...]
    unnamed x32 -> x12, local copies, waits for them, and re-layouts: 4.95 us -> 3.08 us
    ppermute x16, waiting for transfers between devices: 74.6 us -> 73.1 us  [moved(): return lax.ppermute(x, AXES, pairs(lax.axis_size('tile'), place))]
  transfers between devices with their start and end apart: 16 -> 16, of which waited for: 11 -> 11; matrix products, arithmetic and copies ran while one was open for 0% -> 0% of each run, Pallas kernels for 2% -> 1%
where the time goes in v2:
time: 104 us
  waiting for transfers between devices  73.1 us (70%)
  starting transfers between devices  19.4 us (19%)
  Pallas kernels  7.71 us (7%)
  local copies, waits for them, and re-layouts  3.08 us (3%)
    ppermute x16, waiting for transfers between devices, moved(): return lax.ppermute(x, AXES, pairs(lax.axis_size('tile'), place))  73.1 us
    ppermute x16, starting transfers between devices, moved(): return lax.ppermute(x, AXES, pairs(lax.axis_size('tile'), place))  19.4 us
    pallas_call x6, Pallas kernels, call(): pl.pallas_call(kernel, out_shape=tuple((pltpu.VMEM(o.shape, o.dtype) if k...  7.71 us
    unnamed x12, local copies, waits for them, and re-layouts  3.08 us
  transfers between devices with their start and end apart: 16, of which 11 were waited for; matrix products, arithmetic and copies ran while one was open for 0% of the time, Pallas kernels for 1%

profile of v2, /device:TPU:0, one launch (start us, length us, event | category | flops | bytes accessed | tf_op | source)
XLA Modules:
  0.0 104.0 jit_solution(17966428633206495983)
XLA Ops:
  0.6 4.3 %collective-permute-start.8 = (f32[512,512]{1,0:T(8,128)}, f32[512,512]{1,0:T(8,128)S(1)}, u32[]{:S(2)}, u32[]{:S(2)}) collective-permute-start(f32[512,512]{1,0:T(8,128)} %param.11), channel_id=1, source_target_pairs={{0,3},{1,1},{2,2},{3,0},{4,7},{5,5},{6,6},{7,4},{8,11},{9,9},{10,1... | collective-permute-start | bytes 3145736 | tf_op jit(solution)/shard_map/ppermute | solution.py:27
  5.0 0.0 copy-start.2
  5.0 0.0 copy-start.1
  5.0 0.0 copy-start.3
  5.0 0.7 copy-done.2
  5.6 0.0 copy-done.1
  5.7 0.0 copy-done.3
  5.7 0.0 copy-start
  5.7 1.0 copy-done
  6.7 0.0 copy-start.4
  6.7 0.7 copy-done.4
  7.4 0.0 copy-start.5
  7.4 0.7 copy-done.5
  8.1 0.8 shard_map.86
  8.9 1.9 %collective-permute-start = (f32[104,512]{1,0:T(8,128)S(1)}, f32[104,512]{1,0:T(8,128)S(1)}, u32[]{:S(2)}, u32[]{:S(2)}) collective-permute-start(f32[104,512]{1,0:T(8,128)S(1)} %get-tuple-element.14), channel_id=1, source_target_pairs={{0,3},{1,1},{2,2},{3,0},{4,7},{5,5},{6,6},{7,4},{8,11},{9,9},{10,1... | collective-permute-start | bytes 638984 | tf_op jit(solution)/shard_map/ppermute | solution.py:27
  10.8 2.8 %collective-permute-start.1 = (f32[104,512]{1,0:T(8,128)S(1)}, f32[104,512]{1,0:T(8,128)S(1)}, u32[]{:S(2)}, u32[]{:S(2)}) collective-permute-start(f32[104,512]{1,0:T(8,128)S(1)} %get-tuple-element.15), channel_id=1, source_target_pairs={{0,7},{1,5},{2,6},{3,4},{4,3},{5,1},{6,2},{7,0},{8,15},{9,13},{10,... | collective-permute-start | bytes 638984 | tf_op jit(solution)/shard_map/ppermute | solution.py:27
  13.6 2.8 %collective-permute-start.2 = (f32[104,512]{1,0:T(8,128)S(1)}, f32[104,512]{1,0:T(8,128)S(1)}, u32[]{:S(2)}, u32[]{:S(2)}) collective-permute-start(f32[104,512]{1,0:T(8,128)S(1)} %get-tuple-element.16), channel_id=1, source_target_pairs={{0,11},{1,9},{2,10},{3,8},{4,15},{5,13},{6,14},{7,12},{8,3},{9,1},... | collective-permute-start | bytes 638984 | tf_op jit(solution)/shard_map/ppermute | solution.py:27
  16.4 0.6 collective-permute-start.3
  17.0 6.1 %collective-permute-done.refs_0_ = f32[104,512]{1,0:T(8,128)S(1)} collective-permute-done((f32[104,512]{1,0:T(8,128)S(1)}, f32[104,512]{1,0:T(8,128)S(1)}, u32[]{:S(2)}, u32[]{:S(2)}) %collective-permute-start) | collective-permute-done | bytes 213024 | tf_op jit(solution)/shard_map/ppermute | solution.py:27
  23.1 0.0 collective-permute-start.4
  23.1 0.0 collective-permute-done.1.refs_1_
  23.1 0.5 collective-permute-start.5
  23.6 7.9 %collective-permute-done.2.refs_2_ = f32[104,512]{1,0:T(8,128)S(1)} collective-permute-done((f32[104,512]{1,0:T(8,128)S(1)}, f32[104,512]{1,0:T(8,128)S(1)}, u32[]{:S(2)}, u32[]{:S(2)}) %collective-permute-start.2) | collective-permute-done | bytes 213024 | tf_op jit(solution)/shard_map/ppermute | solution.py:27
  31.6 0.0 collective-permute-start.6
  31.6 0.0 collective-permute-done.3.refs_3_
  31.6 0.5 collective-permute-start.7
  32.1 0.0 collective-permute-done.4.refs_4_
  32.1 0.0 collective-permute-done.5.refs_5_
  32.1 0.9 collective-permute-done.6.refs_6_
  33.0 0.3 collective-permute-done.7.refs_7_
  33.3 0.0 collective-permute-done.8.refs_8_
  33.3 2.0 %shard_map.87.own_ref = f32[512,512]{1,0:T(8,128)S(1)} custom-call(f32[104,512]{1,0:T(8,128)S(1)} %collective-permute-done.refs_0_, f32[104,512]{1,0:T(8,128)S(1)} %collective-permute-done.1.refs_1_, f32[104,512]{1,0:T(8,128)S(1)} %collective-permute-done.2.refs_2_, f32[104,512]{1,0:T(8,128)S(1)} %collective-permute-done.3.refs_3_, ...), custom_call_target="tpu_custom_call" | custom-call | flops 1342177280 | bytes 3801088 | tf_op jit(solution)/shard_map/pallas_call | solution.py:74
  35.3 0.3 collective-permute-start.9
  35.6 2.4 %collective-permute-done.9.other_ref = f32[512,512]{1,0:T(8,128)S(1)} collective-permute-done((f32[512,512]{1,0:T(8,128)S(1)}, f32[512,512]{1,0:T(8,128)S(1)}, u32[]{:S(2)}, u32[]{:S(2)}) %collective-permute-start.9) | collective-permute-done | bytes 1048608 | tf_op jit(solution)/shard_map/ppermute | solution.py:27
  38.0 1.0 shard_map.88
  39.0 2.7 %collective-permute-start.10 = (f32[256,512]{1,0:T(8,128)S(1)}, f32[256,512]{1,0:T(8,128)S(1)}, u32[]{:S(2)}, u32[]{:S(2)}) collective-permute-start(f32[256,512]{1,0:T(8,128)S(1)} %get-tuple-element.19), channel_id=1, source_target_pairs={{0,4},{1,5},{2,6},{3,7},{4,0},{5,1},{6,2},{7,3},{8,12},{9,13},{10,... | collective-permute-start | bytes 1572872 | tf_op jit(solution)/shard_map/ppermute | solution.py:27
  41.7 12.3 %collective-permute-done.10.near_ref = f32[256,512]{1,0:T(8,128)S(1)} collective-permute-done((f32[256,512]{1,0:T(8,128)S(1)}, f32[256,512]{1,0:T(8,128)S(1)}, u32[]{:S(2)}, u32[]{:S(2)}) %collective-permute-start.10) | collective-permute-done | bytes 524320 | tf_op jit(solution)/shard_map/ppermute | solution.py:27
  54.0 0.0 collective-permute-start.11
  54.0 1.9 %collective-permute-done.11.far_ref = f32[256,512]{1,0:T(8,128)S(1)} collective-permute-done((f32[256,512]{1,0:T(8,128)S(1)}, f32[256,512]{1,0:T(8,128)S(1)}, u32[]{:S(2)}, u32[]{:S(2)}) %collective-permute-start.11) | collective-permute-done | bytes 524320 | tf_op jit(solution)/shard_map/ppermute | solution.py:27
  55.9 1.0 %shard_map.89 = (f32[512,512]{1,0:T(8,128)S(1)}, f32[256,512]{1,0:T(8,128)S(1)}) custom-call(f32[512,512]{1,0:T(8,128)S(1)} %get-tuple-element.18.own_ref, f32[256,512]{1,0:T(8,128)S(1)} %collective-permute-done.10.near_ref, f32[256,512]{1,0:T(8,128)S(1)} %collective-permute-done.11.far_ref), custom_call_target="tpu_custom_call" | custom-call | flops 805306368 | bytes 3670016 | tf_op jit(solution)/shard_map/pallas_call | solution.py:74
  57.0 2.8 %collective-permute-start.12 = (f32[256,512]{1,0:T(8,128)S(1)}, f32[256,512]{1,0:T(8,128)S(1)}, u32[]{:S(2)}, u32[]{:S(2)}) collective-permute-start(f32[256,512]{1,0:T(8,128)S(1)} %get-tuple-element.21), channel_id=1, source_target_pairs={{0,8},{1,9},{2,10},{3,11},{4,12},{5,13},{6,14},{7,15},{8,0},{9,1},... | collective-permute-start | bytes 1572872 | tf_op jit(solution)/shard_map/ppermute | solution.py:27
  59.8 23.5 %collective-permute-done.12.near_ref = f32[256,512]{1,0:T(8,128)S(1)} collective-permute-done((f32[256,512]{1,0:T(8,128)S(1)}, f32[256,512]{1,0:T(8,128)S(1)}, u32[]{:S(2)}, u32[]{:S(2)}) %collective-permute-start.12) | collective-permute-done | bytes 524320 | tf_op jit(solution)/shard_map/ppermute | solution.py:27
  83.2 0.0 collective-permute-start.13
  83.2 1.9 %collective-permute-done.13.far_ref = f32[256,512]{1,0:T(8,128)S(1)} collective-permute-done((f32[256,512]{1,0:T(8,128)S(1)}, f32[256,512]{1,0:T(8,128)S(1)}, u32[]{:S(2)}, u32[]{:S(2)}) %collective-permute-start.13) | collective-permute-done | bytes 524320 | tf_op jit(solution)/shard_map/ppermute | solution.py:27
  85.1 1.0 %shard_map.90 = (f32[512,512]{1,0:T(8,128)S(1)}, f32[256,512]{1,0:T(8,128)S(1)}) custom-call(f32[512,512]{1,0:T(8,128)S(1)} %get-tuple-element.20.own_ref, f32[256,512]{1,0:T(8,128)S(1)} %collective-permute-done.12.near_ref, f32[256,512]{1,0:T(8,128)S(1)} %collective-permute-done.13.far_ref), custom_call_target="tpu_custom_call" | custom-call | flops 805306368 | bytes 3670016 | tf_op jit(solution)/shard_map/pallas_call | solution.py:74
  86.2 0.1 collective-permute-start.14
  86.3 13.9 %collective-permute-done.14.near_ref = f32[256,512]{1,0:T(8,128)S(1)} collective-permute-done((f32[256,512]{1,0:T(8,128)S(1)}, f32[256,512]{1,0:T(8,128)S(1)}, u32[]{:S(2)}, u32[]{:S(2)}) %collective-permute-start.14) | collective-permute-done | bytes 524320 | tf_op jit(solution)/shard_map/ppermute | solution.py:27
  100.2 0.0 collective-permute-start.15
  100.2 1.9 %collective-permute-done.15.far_ref = f32[256,512]{1,0:T(8,128)S(1)} collective-permute-done((f32[256,512]{1,0:T(8,128)S(1)}, f32[256,512]{1,0:T(8,128)S(1)}, u32[]{:S(2)}, u32[]{:S(2)}) %collective-permute-start.15) | collective-permute-done | bytes 524320 | tf_op jit(solution)/shard_map/ppermute | solution.py:27
  102.1 1.9 %shard_map.91 = (f32[64,256]{1,0:T(8,128)}, f32[1,1]{1,0:T(1,128)}) custom-call(f32[512,512]{1,0:T(8,128)S(1)} %get-tuple-element.22.own_ref, f32[256,512]{1,0:T(8,128)S(1)} %collective-permute-done.14.near_ref, f32[256,512]{1,0:T(8,128)S(1)} %collective-permute-done.15.far_ref), custom_call_target="tpu_custom_call" | custom-call | flops 805306368 | bytes 2162692 | tf_op jit(solution)/shard_map/pallas_call | solution.py:74
Async XLA Ops:
  0.6 32.7 %collective-permute-start.8 = (f32[512,512]{1,0:T(8,128)}, f32[512,512]{1,0:T(8,128)S(1)}, u32[]{:S(2)}, u32[]{:S(2)}) collective-permute-start(f32[512,512]{1,0:T(8,128)} %param.11), channel_id=1, source_target_pairs={{0,3},{1,1},{2,2},{3,0},{4,7},{5,5},{6,6},{7,4},{8,11},{9,9},{10,1... | collective-permute-start | bytes 3145736 | tf_op jit(solution)/shard_map/ppermute | solution.py:27
  5.0 0.7 copy-start.2
  5.0 0.7 copy-start.1
  5.0 0.7 copy-start.3
  5.7 1.0 %copy-start = (f32[256,512]{1,0:T(8,128)S(1)}, f32[256,512]{1,0:T(8,128)}, u32[]{:S(2)}) copy-start(f32[256,512]{1,0:T(8,128)} %rows_ref.1) | copy-start | bytes 1572868
  6.7 0.7 copy-start.4
  7.4 0.7 copy-start.5
  8.9 14.3 %collective-permute-start = (f32[104,512]{1,0:T(8,128)S(1)}, f32[104,512]{1,0:T(8,128)S(1)}, u32[]{:S(2)}, u32[]{:S(2)}) collective-permute-start(f32[104,512]{1,0:T(8,128)S(1)} %get-tuple-element.14), channel_id=1, source_target_pairs={{0,3},{1,1},{2,2},{3,0},{4,7},{5,5},{6,6},{7,4},{8,11},{9,9},{10,1... | collective-permute-start | bytes 638984 | tf_op jit(solution)/shard_map/ppermute | solution.py:27
  10.8 12.3 %collective-permute-start.1 = (f32[104,512]{1,0:T(8,128)S(1)}, f32[104,512]{1,0:T(8,128)S(1)}, u32[]{:S(2)}, u32[]{:S(2)}) collective-permute-start(f32[104,512]{1,0:T(8,128)S(1)} %get-tuple-element.15), channel_id=1, source_target_pairs={{0,7},{1,5},{2,6},{3,4},{4,3},{5,1},{6,2},{7,0},{8,15},{9,13},{10,... | collective-permute-start | bytes 638984 | tf_op jit(solution)/shard_map/ppermute | solution.py:27
  13.6 17.9 %collective-permute-start.2 = (f32[104,512]{1,0:T(8,128)S(1)}, f32[104,512]{1,0:T(8,128)S(1)}, u32[]{:S(2)}, u32[]{:S(2)}) collective-permute-start(f32[104,512]{1,0:T(8,128)S(1)} %get-tuple-element.16), channel_id=1, source_target_pairs={{0,11},{1,9},{2,10},{3,8},{4,15},{5,13},{6,14},{7,12},{8,3},{9,1},... | collective-permute-start | bytes 638984 | tf_op jit(solution)/shard_map/ppermute | solution.py:27
  16.4 15.1 %collective-permute-start.3 = (f32[104,512]{1,0:T(8,128)S(1)}, f32[104,512]{1,0:T(8,128)S(1)}, u32[]{:S(2)}, u32[]{:S(2)}) collective-permute-start(f32[104,512]{1,0:T(8,128)S(1)} %get-tuple-element.17), channel_id=1, source_target_pairs={{0,15},{1,13},{2,14},{3,12},{4,11},{5,9},{6,10},{7,8},{8,7},{9,5},... | collective-permute-start | bytes 638984 | tf_op jit(solution)/shard_map/ppermute | solution.py:27
  23.1 8.9 %collective-permute-start.4 = (f32[104,512]{1,0:T(8,128)S(1)}, f32[104,512]{1,0:T(8,128)S(1)}, u32[]{:S(2)}, u32[]{:S(2)}) collective-permute-start(f32[104,512]{1,0:T(8,128)S(1)} %collective-permute-done.refs_0_), channel_id=1, source_target_pairs={{0,1},{1,0},{2,3},{3,2},{4,5},{5,4},{6,7},{7,6},{8,9},{9,8},{10,11... | collective-permute-start | bytes 638984 | tf_op jit(solution)/shard_map/ppermute | solution.py:27
  23.1 8.9 %collective-permute-start.5 = (f32[104,512]{1,0:T(8,128)S(1)}, f32[104,512]{1,0:T(8,128)S(1)}, u32[]{:S(2)}, u32[]{:S(2)}) collective-permute-start(f32[104,512]{1,0:T(8,128)S(1)} %collective-permute-done.1.refs_1_), channel_id=1, source_target_pairs={{0,1},{1,0},{2,3},{3,2},{4,5},{5,4},{6,7},{7,6},{8,9},{9,8},{10,11... | collective-permute-start | bytes 638984 | tf_op jit(solution)/shard_map/ppermute | solution.py:27
  31.6 1.5 %collective-permute-start.6 = (f32[104,512]{1,0:T(8,128)S(1)}, f32[104,512]{1,0:T(8,128)S(1)}, u32[]{:S(2)}, u32[]{:S(2)}) collective-permute-start(f32[104,512]{1,0:T(8,128)S(1)} %collective-permute-done.2.refs_2_), channel_id=1, source_target_pairs={{0,1},{1,0},{2,3},{3,2},{4,5},{5,4},{6,7},{7,6},{8,9},{9,8},{10,11... | collective-permute-start | bytes 638984 | tf_op jit(solution)/shard_map/ppermute | solution.py:27
  31.6 1.8 %collective-permute-start.7 = (f32[104,512]{1,0:T(8,128)S(1)}, f32[104,512]{1,0:T(8,128)S(1)}, u32[]{:S(2)}, u32[]{:S(2)}) collective-permute-start(f32[104,512]{1,0:T(8,128)S(1)} %collective-permute-done.3.refs_3_), channel_id=1, source_target_pairs={{0,1},{1,0},{2,3},{3,2},{4,5},{5,4},{6,7},{7,6},{8,9},{9,8},{10,11... | collective-permute-start | bytes 638984 | tf_op jit(solution)/shard_map/ppermute | solution.py:27
  35.3 2.7 %collective-permute-start.9 = (f32[512,512]{1,0:T(8,128)S(1)}, f32[512,512]{1,0:T(8,128)S(1)}, u32[]{:S(2)}, u32[]{:S(2)}) collective-permute-start(f32[512,512]{1,0:T(8,128)S(1)} %shard_map.87.own_ref), channel_id=1, source_target_pairs={{0,1},{1,0},{2,3},{3,2},{4,5},{5,4},{6,7},{7,6},{8,9},{9,8},{10,11... | collective-permute-start | bytes 3145736 | tf_op jit(solution)/shard_map/ppermute | solution.py:27
  39.0 15.0 %collective-permute-start.10 = (f32[256,512]{1,0:T(8,128)S(1)}, f32[256,512]{1,0:T(8,128)S(1)}, u32[]{:S(2)}, u32[]{:S(2)}) collective-permute-start(f32[256,512]{1,0:T(8,128)S(1)} %get-tuple-element.19), channel_id=1, source_target_pairs={{0,4},{1,5},{2,6},{3,7},{4,0},{5,1},{6,2},{7,3},{8,12},{9,13},{10,... | collective-permute-start | bytes 1572872 | tf_op jit(solution)/shard_map/ppermute | solution.py:27
  54.0 1.9 %collective-permute-start.11 = (f32[256,512]{1,0:T(8,128)S(1)}, f32[256,512]{1,0:T(8,128)S(1)}, u32[]{:S(2)}, u32[]{:S(2)}) collective-permute-start(f32[256,512]{1,0:T(8,128)S(1)} %collective-permute-done.10.near_ref), channel_id=1, source_target_pairs={{0,1},{1,0},{2,3},{3,2},{4,5},{5,4},{6,7},{7,6},{8,9},{9,8},{10,11... | collective-permute-start | bytes 1572872 | tf_op jit(solution)/shard_map/ppermute | solution.py:27
  57.0 26.3 %collective-permute-start.12 = (f32[256,512]{1,0:T(8,128)S(1)}, f32[256,512]{1,0:T(8,128)S(1)}, u32[]{:S(2)}, u32[]{:S(2)}) collective-permute-start(f32[256,512]{1,0:T(8,128)S(1)} %get-tuple-element.21), channel_id=1, source_target_pairs={{0,8},{1,9},{2,10},{3,11},{4,12},{5,13},{6,14},{7,15},{8,0},{9,1},... | collective-permute-start | bytes 1572872 | tf_op jit(solution)/shard_map/ppermute | solution.py:27
  83.2 1.9 %collective-permute-start.13 = (f32[256,512]{1,0:T(8,128)S(1)}, f32[256,512]{1,0:T(8,128)S(1)}, u32[]{:S(2)}, u32[]{:S(2)}) collective-permute-start(f32[256,512]{1,0:T(8,128)S(1)} %collective-permute-done.12.near_ref), channel_id=1, source_target_pairs={{0,1},{1,0},{2,3},{3,2},{4,5},{5,4},{6,7},{7,6},{8,9},{9,8},{10,11... | collective-permute-start | bytes 1572872 | tf_op jit(solution)/shard_map/ppermute | solution.py:27
  86.2 14.0 %collective-permute-start.14 = (f32[256,512]{1,0:T(8,128)S(1)}, f32[256,512]{1,0:T(8,128)S(1)}, u32[]{:S(2)}, u32[]{:S(2)}) collective-permute-start(f32[256,512]{1,0:T(8,128)S(1)} %get-tuple-element.23), channel_id=1, source_target_pairs={{0,2},{1,3},{2,0},{3,1},{4,6},{5,7},{6,4},{7,5},{8,10},{9,11},{10,... | collective-permute-start | bytes 1572872 | tf_op jit(solution)/shard_map/ppermute | solution.py:27
  100.2 1.9 %collective-permute-start.15 = (f32[256,512]{1,0:T(8,128)S(1)}, f32[256,512]{1,0:T(8,128)S(1)}, u32[]{:S(2)}, u32[]{:S(2)}) collective-permute-start(f32[256,512]{1,0:T(8,128)S(1)} %collective-permute-done.14.near_ref), channel_id=1, source_target_pairs={{0,1},{1,0},{2,3},{3,2},{4,5},{5,4},{6,7},{7,6},{8,9},{9,8},{10,11... | collective-permute-start | bytes 1572872 | tf_op jit(solution)/shard_map/ppermute | solution.py:27

commit v3 on v2

--- a/solution.py
+++ b/solution.py
@@ -69,8 +69,7 @@
 
 def call(kernel, outs, args, scratch=(), flops=0, held=True, kept=True):
     size = sum(a.size * 4 for a in args) + sum(o.size * 4 for o in outs)
-    if held:
-        args = [pltpu.with_memory_space_constraint(a, pltpu.VMEM) for a in args]
+    args = [pltpu.with_memory_space_constraint(a, pltpu.VMEM if held else pltpu.HBM) for a in args]
     return pl.pallas_call(
         kernel,
         out_shape=tuple(pltpu.VMEM(o.shape, o.dtype) if kept else o for o in outs),
@@ -204,6 +203,89 @@
     log_ref[...] = jnp.log(spread)
 
 
+def product_nt(a, b):
+    ah, al = split2(a)
+    bh, bl = split2(b)
+    last = ((1,), (1,))
+    return mul(ah, bh, last) + (mul(ah, bl, last) + mul(al, bh, last))
+
+
+def fold_pair_kernel(own_ref, other_ref, out_ref, *parts):
+    core = lax.axis_index("cuts")
+    odd = (lax.axis_index("tile") >> 1) & 1
+    for k in range(2):
+
+        @pl.when(core == k)
+        def _(k=k):
+            left, right = (own_ref, other_ref) if k else (other_ref, own_ref)
+            out_ref[...] = product(left[...], right[...])
+
+    @pl.when(odd == 1)
+    def _():
+        out_ref[...] = jnp.transpose(out_ref[...])
+
+    rows = parts[0].shape[0]
+    start = core * (rows * len(parts))
+    for p, part in enumerate(parts):
+        part[...] = out_ref[pl.ds(pl.multiple_of(start + p * rows, 8), rows), :]
+
+
+def fold_kernel(near_ref, own_ref, out_ref):
+    out_ref[...] = product_nt(near_ref[...], own_ref[...])
+
+
+def fold_wide_kernel(near_ref, *refs):
+    out_ref, pieces = refs[-1], refs[:-1]
+    core = lax.axis_index("cuts")
+    half = len(pieces) // 2
+    size = out_ref.shape[1] // 2
+    near = near_ref[...]
+    for at, group in ((core, pieces[:half]), (1 - core, pieces[half:])):
+        rows = jnp.concatenate([piece[...] for piece in group], axis=0)
+        out_ref[:, pl.ds(pl.multiple_of(at * size, 128), size)] = product_nt(near, rows)
+
+
+def fold_last_kernel(count, *refs):
+    own, own_far = refs[:count], refs[count : 2 * count]
+    got, got_far = refs[2 * count : 3 * count], refs[3 * count : 4 * count]
+    block_ref, send_ref, own_ref, got_ref, whole_ref = refs[4 * count :]
+    core, tile = lax.axis_index("cuts"), lax.axis_index("tile")
+    side, column, group = (tile >> 2) & 1, tile & 1, tile >> 1
+    rows = own[0].shape[0]
+    for ref, near, far in ((own_ref, own, own_far), (got_ref, got, got_far)):
+        for at, part in ((core, near), (1 - core, far)):
+            for p, piece in enumerate(part):
+                start = pl.multiple_of(at * (rows * count) + p * rows, 8)
+                ref[pl.ds(start, rows), :] = piece[...]
+
+    @pl.when(side == column)
+    def _():
+        whole_ref[...] = product(own_ref[...], got_ref[...])
+
+    @pl.when(side != column)
+    def _():
+        whole_ref[...] = product(got_ref[...], own_ref[...])
+
+    whole = whole_ref[...]
+    square = jnp.sum(jnp.sum(whole * whole, axis=0, keepdims=True), axis=1, keepdims=True)
+    spread = jnp.sqrt(square / whole.size + 1e-06)
+    high, cols = block_ref.shape
+    for ref, place in ((block_ref, group), (send_ref, group ^ 1)):
+        rows_at = pl.multiple_of(place * 2 * high, 128)
+        cols_at = pl.multiple_of(core * cols, 128)
+
+        @pl.when(side == 1)
+        def _(rows_at=rows_at, cols_at=cols_at):
+            got_ref[0 : 2 * high, 0:cols] = whole_ref[pl.ds(rows_at, 2 * high), pl.ds(cols_at, cols)]
+
+        @pl.when(side == 0)
+        def _(rows_at=rows_at, cols_at=cols_at):
+            got_ref[0 : 2 * high, 0:cols] = jnp.transpose(whole_ref[pl.ds(cols_at, cols), pl.ds(rows_at, 2 * high)])
+
+        ref[0:high, :] = got_ref[pl.ds(pl.multiple_of(column * high, 8), high), 0:cols] / spread
+    send_ref[high : high + PAD, :] = jnp.broadcast_to(jnp.log(spread), (PAD, cols))
+
+
 def plain_leaf(slice_rows, row_owner, leaf_row, exponent, environment, ordering, sign_mask, tiles, cap):
     width = slice_rows.shape[1]
     factor = jnp.where(exponent == -1, 0.5, jnp.where(exponent == 1, 2.0, 1.0)).astype(F32)
@@ -256,6 +338,53 @@
     narrow = cap % 8 == 0 and 2 * cap <= 128 and 2 <= tiles // 2 <= 8 and width % 128 == 0
     make_leaf = packed_leaf if narrow else plain_leaf
     leaf = make_leaf(slice_rows, row_owner, leaf_row, exponent, environment, ordering, sign_mask, tiles, cap)
+    if tiles == 8 and width % 512 == 0:
+        return center_tree(leaf, tiles, width)
+    return plain_tree(leaf, tiles, width)
+
+
+def center(t, c):
+    return (t ^ 6 if t >> 1 in (1, 2) else t), c
+
+
+def center_tree(leaf, tiles, width):
+    count = 2
+    rows = width // 2 // count
+    cost = 6 * width**2
+    whole, piece = like(width, width), like(rows, width)
+    own, *parts = call(
+        fold_pair_kernel, [whole] + [piece] * count, (leaf, moved(leaf, other_core)), flops=cost * width
+    )
+    near = [moved(part, across(1)) for part in parts]
+    first, first_far, got = [], [], []
+    for p in range(count):
+        (done,) = call(fold_kernel, [piece], (near[p], own), flops=cost * rows)
+        first.append(done)
+        got.append(moved(done, center))
+        first_far.append(moved(done, other_core))
+    mine, mine_far, theirs, theirs_far = [], [], [], []
+    for p in range(count):
+        (done,) = call(fold_wide_kernel, [piece], (got[p], *first, *first_far), flops=cost * rows)
+        mine.append(done)
+        theirs.append(moved(done, across(0)))
+        mine_far.append(moved(done, other_core))
+    theirs_far = [moved(part, other_core) for part in theirs]
+    high, cols = width // tiles, width // 2
+    block, send = call(
+        functools.partial(fold_last_kernel, count),
+        [like(high, cols), like(high + PAD, cols)],
+        (*mine, *mine_far, *theirs, *theirs_far),
+        scratch=[pltpu.VMEM((width, width), F32)] * 3,
+        flops=cost * width,
+    )
+    got = moved(send, across(1))
+    group = lax.axis_index("tile") >> 1
+    inner = (group == 1) | (group == 2)
+    log = jnp.where(inner, send[high, 0], got[high, 0])
+    return jnp.where(inner, block, got[:high]), log.reshape(1)
+
+
+def plain_tree(leaf, tiles, width):
     whole, half = like(width, width), like(width // 2, width)
     cost = 6 * width**3
     own, part = call(pair_kernel, [whole, half], (leaf, moved(leaf, other_core)), flops=cost)

time: 104 us -> 84.3 us (0.81)
  waiting for transfers between devices: 73.1 us -> 43.5 us
  starting transfers between devices: 19.4 us -> 26.6 us
  between operations: 0.73 us -> 3.23 us
  local copies, waits for them, and re-layouts: 3.08 us -> 1.02 us
  Pallas kernels: 7.71 us -> 9.02 us
    ppermute x16 -> x23, waiting for transfers between devices: 73.1 us -> 43.5 us  [moved(): return lax.ppermute(x, AXES, pairs(lax.axis_size('tile'), place))]
    ppermute x16 -> x23, starting transfers between devices: 19.4 us -> 26.6 us  [moved(): return lax.ppermute(x, AXES, pairs(lax.axis_size('tile'), place))]
    unnamed x12 -> x0, local copies, waits for them, and re-layouts: 3.08 us -> none
    pallas_call x6 -> x8, Pallas kernels: 7.71 us -> 9.02 us  [call(): pl.pallas_call(kernel, out_shape=tuple((pltpu.VMEM(o.shape, o.dtype) if k...]
  transfers between devices with their start and end apart: 16 -> 23, of which waited for: 11 -> 12; matrix products, arithmetic and copies ran while one was open for 0% -> 1% of each run, Pallas kernels for 1% -> 5%
where the time goes in v3:
time: 84.3 us; the launch traced here: 84.1 us
  waiting for transfers between devices  43.5 us (52%)
  starting transfers between devices  26.6 us (32%)
  Pallas kernels  9.02 us (11%)
  between operations  3.23 us (4%)
  local copies, waits for them, and re-layouts  1.02 us (1%)
    ppermute x23, waiting for transfers between devices, moved(): return lax.ppermute(x, AXES, pairs(lax.axis_size('tile'), place))  43.5 us
    ppermute x23, starting transfers between devices, moved(): return lax.ppermute(x, AXES, pairs(lax.axis_size('tile'), place))  26.6 us
    pallas_call x8, Pallas kernels, call(): pl.pallas_call(kernel, out_shape=tuple((pltpu.VMEM(o.shape, o.dtype) if k...  9.02 us
  transfers between devices with their start and end apart: 23, of which 12 were waited for; matrix products, arithmetic and copies ran while one was open for 1% of the time, Pallas kernels for 5%

profile of v3, /device:TPU:0, one launch (start us, length us, event | category | flops | bytes accessed | tf_op | source)
XLA Modules:
  0.0 84.1 jit_solution(16139372166399844898)
XLA Ops:
  0.6 4.3 %collective-permute-start.8 = (f32[512,512]{1,0:T(8,128)}, f32[512,512]{1,0:T(8,128)S(1)}, u32[]{:S(2)}, u32[]{:S(2)}) collective-permute-start(f32[512,512]{1,0:T(8,128)} %param.11), channel_id=1, source_target_pairs={{0,3},{1,1},{2,2},{3,0},{4,7},{5,5},{6,6},{7,4},{8,11},{9,9},{10,1... | collective-permute-start | bytes 3145736 | tf_op jit(solution)/shard_map/ppermute | solution.py:27
  5.0 1.9 %shard_map.86 = (f32[104,512]{1,0:T(8,128)S(1)}, f32[104,512]{1,0:T(8,128)S(1)}, f32[104,512]{1,0:T(8,128)S(1)}, f32[104,512]{1,0:T(8,128)S(1)}) custom-call(f32[256,512]{1,0:T(8,128)} %rows_ref.1, s32[1,256]{1,0:T(1,128)} %bitcast.6, s32[1,256]{1,0:T(1,128)} %bitcast.7, s32[1,256]{1,0:T(1,128)} %bitcast.8, s32[1,512]{1,0:T(1,128)} %order_ref.1, ...), custom_call_target="tpu_custom_call" | custom-call | flops 301989888 | bytes 1383424 | tf_op jit(solution)/shard_map/pallas_call | solution.py:73
  6.8 1.9 %collective-permute-start = (f32[104,512]{1,0:T(8,128)S(1)}, f32[104,512]{1,0:T(8,128)S(1)}, u32[]{:S(2)}, u32[]{:S(2)}) collective-permute-start(f32[104,512]{1,0:T(8,128)S(1)} %get-tuple-element.11), channel_id=1, source_target_pairs={{0,3},{1,1},{2,2},{3,0},{4,7},{5,5},{6,6},{7,4},{8,11},{9,9},{10,1... | collective-permute-start | bytes 638984 | tf_op jit(solution)/shard_map/ppermute | solution.py:27
  8.8 2.8 %collective-permute-start.1 = (f32[104,512]{1,0:T(8,128)S(1)}, f32[104,512]{1,0:T(8,128)S(1)}, u32[]{:S(2)}, u32[]{:S(2)}) collective-permute-start(f32[104,512]{1,0:T(8,128)S(1)} %get-tuple-element.12), channel_id=1, source_target_pairs={{0,7},{1,5},{2,6},{3,4},{4,3},{5,1},{6,2},{7,0},{8,15},{9,13},{10,... | collective-permute-start | bytes 638984 | tf_op jit(solution)/shard_map/ppermute | solution.py:27
  11.6 2.8 %collective-permute-start.2 = (f32[104,512]{1,0:T(8,128)S(1)}, f32[104,512]{1,0:T(8,128)S(1)}, u32[]{:S(2)}, u32[]{:S(2)}) collective-permute-start(f32[104,512]{1,0:T(8,128)S(1)} %get-tuple-element.13), channel_id=1, source_target_pairs={{0,11},{1,9},{2,10},{3,8},{4,15},{5,13},{6,14},{7,12},{8,3},{9,1},... | collective-permute-start | bytes 638984 | tf_op jit(solution)/shard_map/ppermute | solution.py:27
  14.4 0.6 collective-permute-start.3
  15.0 11.6 %collective-permute-done.refs_0_ = f32[104,512]{1,0:T(8,128)S(1)} collective-permute-done((f32[104,512]{1,0:T(8,128)S(1)}, f32[104,512]{1,0:T(8,128)S(1)}, u32[]{:S(2)}, u32[]{:S(2)}) %collective-permute-start) | collective-permute-done | bytes 213024 | tf_op jit(solution)/shard_map/ppermute | solution.py:27
  26.6 0.0 collective-permute-start.4
  26.6 0.0 collective-permute-done.1.refs_1_
  26.6 0.5 collective-permute-start.5
  27.1 2.4 %collective-permute-done.2.refs_2_ = f32[104,512]{1,0:T(8,128)S(1)} collective-permute-done((f32[104,512]{1,0:T(8,128)S(1)}, f32[104,512]{1,0:T(8,128)S(1)}, u32[]{:S(2)}, u32[]{:S(2)}) %collective-permute-start.2) | collective-permute-done | bytes 213024 | tf_op jit(solution)/shard_map/ppermute | solution.py:27
  29.5 0.0 collective-permute-start.6
  29.5 0.0 collective-permute-done.3.refs_3_
  29.5 0.5 collective-permute-start.7
  30.0 0.0 collective-permute-done.4.refs_4_
  30.0 0.0 collective-permute-done.5.refs_5_
  30.0 0.9 %collective-permute-done.6.refs_6_ = f32[104,512]{1,0:T(8,128)S(1)} collective-permute-done((f32[104,512]{1,0:T(8,128)S(1)}, f32[104,512]{1,0:T(8,128)S(1)}, u32[]{:S(2)}, u32[]{:S(2)}) %collective-permute-start.6) | collective-permute-done | bytes 213024 | tf_op jit(solution)/shard_map/ppermute | solution.py:27
  31.0 0.3 collective-permute-done.7.refs_7_
  31.3 0.0 collective-permute-done.8.refs_8_
  31.3 2.0 %shard_map.87.own_ref = f32[512,512]{1,0:T(8,128)S(1)} custom-call(f32[104,512]{1,0:T(8,128)S(1)} %collective-permute-done.refs_0_, f32[104,512]{1,0:T(8,128)S(1)} %collective-permute-done.1.refs_1_, f32[104,512]{1,0:T(8,128)S(1)} %collective-permute-done.2.refs_2_, f32[104,512]{1,0:T(8,128)S(1)} %collective-permute-done.3.refs_3_, ...), custom_call_target="tpu_custom_call" | custom-call | flops 1342177280 | bytes 3801088 | tf_op jit(solution)/shard_map/pallas_call | solution.py:73
  33.3 0.3 collective-permute-start.9
  33.5 2.5 %collective-permute-done.9.other_ref = f32[512,512]{1,0:T(8,128)S(1)} collective-permute-done((f32[512,512]{1,0:T(8,128)S(1)}, f32[512,512]{1,0:T(8,128)S(1)}, u32[]{:S(2)}, u32[]{:S(2)}) %collective-permute-start.9) | collective-permute-done | bytes 1048608 | tf_op jit(solution)/shard_map/ppermute | solution.py:27
  36.0 1.0 %shard_map.88 = (f32[512,512]{1,0:T(8,128)S(1)}, f32[128,512]{1,0:T(8,128)S(1)}, f32[128,512]{1,0:T(8,128)S(1)}) custom-call(f32[512,512]{1,0:T(8,128)S(1)} %shard_map.87.own_ref, f32[512,512]{1,0:T(8,128)S(1)} %collective-permute-done.9.other_ref), custom_call_target="tpu_custom_call" | custom-call | flops 805306368 | bytes 3670016 | tf_op jit(solution)/shard_map/pallas_call | solution.py:73
  37.0 3.0 %collective-permute-start.12 = (f32[128,512]{1,0:T(8,128)S(1)}, f32[128,512]{1,0:T(8,128)S(1)}, u32[]{:S(2)}, u32[]{:S(2)}) collective-permute-start(f32[128,512]{1,0:T(8,128)S(1)} %get-tuple-element.17), channel_id=1, source_target_pairs={{0,4},{1,5},{2,6},{3,7},{4,0},{5,1},{6,2},{7,3},{8,12},{9,13},{10,... | collective-permute-start | bytes 786440 | tf_op jit(solution)/shard_map/ppermute | solution.py:27
  40.1 0.1 collective-permute-start.10
  40.1 7.1 %collective-permute-done.12.near_ref = f32[128,512]{1,0:T(8,128)S(1)} collective-permute-done((f32[128,512]{1,0:T(8,128)S(1)}, f32[128,512]{1,0:T(8,128)S(1)}, u32[]{:S(2)}, u32[]{:S(2)}) %collective-permute-start.12) | collective-permute-done | bytes 262176 | tf_op jit(solution)/shard_map/ppermute | solution.py:27
  47.2 0.6 shard_map.90.refs_1_
  47.9 0.1 collective-permute-start.14
  48.0 0.7 collective-permute-start.15
  48.6 3.6 %collective-permute-done.10.near_ref = f32[128,512]{1,0:T(8,128)S(1)} collective-permute-done((f32[128,512]{1,0:T(8,128)S(1)}, f32[128,512]{1,0:T(8,128)S(1)}, u32[]{:S(2)}, u32[]{:S(2)}) %collective-permute-start.10) | collective-permute-done | bytes 262176 | tf_op jit(solution)/shard_map/ppermute | solution.py:27
  52.3 0.6 shard_map.89.refs_0_
  52.9 0.1 collective-permute-start.13
  53.0 0.7 collective-permute-start.11
  53.7 0.0 collective-permute-done.14.refs_3_
  53.7 0.0 collective-permute-done.15.near_ref
  53.7 0.8 collective-permute-done.13.refs_2_
  54.5 0.7 shard_map.92.refs_1_
  55.2 0.1 collective-permute-start.19
  55.3 0.0 collective-permute-done.11.near_ref
  55.3 0.7 shard_map.91.refs_0_
  56.0 2.1 %collective-permute-start.18 = (f32[128,512]{1,0:T(8,128)S(1)}, f32[128,512]{1,0:T(8,128)S(1)}, u32[]{:S(2)}, u32[]{:S(2)}) collective-permute-start(f32[128,512]{1,0:T(8,128)S(1)} %shard_map.91.refs_0_), channel_id=1, source_target_pairs={{0,2},{1,3},{2,0},{3,1},{4,6},{5,7},{6,4},{7,5},{8,10},{9,11},{10,... | collective-permute-start | bytes 786440 | tf_op jit(solution)/shard_map/ppermute | solution.py:27
  58.0 0.0 collective-permute-start.17
  58.0 0.5 collective-permute-start.16
  58.5 5.9 %collective-permute-done.19.refs_5_ = f32[128,512]{1,0:T(8,128)S(1)} collective-permute-done((f32[128,512]{1,0:T(8,128)S(1)}, f32[128,512]{1,0:T(8,128)S(1)}, u32[]{:S(2)}, u32[]{:S(2)}) %collective-permute-start.19) | collective-permute-done | bytes 262176 | tf_op jit(solution)/shard_map/ppermute | solution.py:27
  64.5 0.0 collective-permute-start.21
  64.5 4.8 %collective-permute-done.18.refs_4_ = f32[128,512]{1,0:T(8,128)S(1)} collective-permute-done((f32[128,512]{1,0:T(8,128)S(1)}, f32[128,512]{1,0:T(8,128)S(1)}, u32[]{:S(2)}, u32[]{:S(2)}) %collective-permute-start.18) | collective-permute-done | bytes 262176 | tf_op jit(solution)/shard_map/ppermute | solution.py:27
  69.2 0.0 collective-permute-start.20
  69.2 0.0 collective-permute-done.17.refs_3_
  69.2 0.0 collective-permute-done.16.refs_2_
  69.2 0.0 collective-permute-done.21.refs_7_
  69.3 1.5 %collective-permute-done.20.refs_6_ = f32[128,512]{1,0:T(8,128)S(1)} collective-permute-done((f32[128,512]{1,0:T(8,128)S(1)}, f32[128,512]{1,0:T(8,128)S(1)}, u32[]{:S(2)}, u32[]{:S(2)}) %collective-permute-start.20) | collective-permute-done | bytes 262176 | tf_op jit(solution)/shard_map/ppermute | solution.py:27
  70.8 1.5 %shard_map.93 = (f32[64,256]{1,0:T(8,128)S(1)}, f32[72,256]{1,0:T(8,128)S(1)}) custom-call(f32[128,512]{1,0:T(8,128)S(1)} %shard_map.91.refs_0_, f32[128,512]{1,0:T(8,128)S(1)} %shard_map.92.refs_1_, f32[128,512]{1,0:T(8,128)S(1)} %collective-permute-done.16.refs_2_, f32[128,512]{1,0:T(8,128)S(1)} %collective-permute-done.17.refs_3_, ...), custom_call_target="tpu_custom_call" | custom-call | flops 805306368 | bytes 2236416 | tf_op jit(solution)/shard_map/pallas_call | solution.py:73
  72.3 5.6 %collective-permute-start.22 = (f32[72,256]{1,0:T(8,128)S(1)}, f32[72,256]{1,0:T(8,128)S(1)}, u32[]{:S(2)}, u32[]{:S(2)}) collective-permute-start(f32[72,256]{1,0:T(8,128)S(1)} %get-tuple-element.19), channel_id=1, source_target_pairs={{0,4},{1,5},{2,6},{3,7},{4,0},{5,1},{6,2},{7,3},{8,12},{9,13},{10,... | collective-permute-start | bytes 221192 | tf_op jit(solution)/shard_map/ppermute | solution.py:27
  77.9 0.5 slice.10
  78.4 2.1 %collective-permute-done.22 = f32[72,256]{1,0:T(8,128)S(1)} collective-permute-done((f32[72,256]{1,0:T(8,128)S(1)}, f32[72,256]{1,0:T(8,128)S(1)}, u32[]{:S(2)}, u32[]{:S(2)}) %collective-permute-start.22) | collective-permute-done | bytes 73760 | tf_op jit(solution)/shard_map/ppermute | solution.py:27
  80.5 0.5 slice.13
  82.3 0.6 slice_select_fusion
Async XLA Ops:
  0.6 30.7 %collective-permute-start.8 = (f32[512,512]{1,0:T(8,128)}, f32[512,512]{1,0:T(8,128)S(1)}, u32[]{:S(2)}, u32[]{:S(2)}) collective-permute-start(f32[512,512]{1,0:T(8,128)} %param.11), channel_id=1, source_target_pairs={{0,3},{1,1},{2,2},{3,0},{4,7},{5,5},{6,6},{7,4},{8,11},{9,9},{10,1... | collective-permute-start | bytes 3145736 | tf_op jit(solution)/shard_map/ppermute | solution.py:27
  6.8 19.8 %collective-permute-start = (f32[104,512]{1,0:T(8,128)S(1)}, f32[104,512]{1,0:T(8,128)S(1)}, u32[]{:S(2)}, u32[]{:S(2)}) collective-permute-start(f32[104,512]{1,0:T(8,128)S(1)} %get-tuple-element.11), channel_id=1, source_target_pairs={{0,3},{1,1},{2,2},{3,0},{4,7},{5,5},{6,6},{7,4},{8,11},{9,9},{10,1... | collective-permute-start | bytes 638984 | tf_op jit(solution)/shard_map/ppermute | solution.py:27
  8.8 17.9 %collective-permute-start.1 = (f32[104,512]{1,0:T(8,128)S(1)}, f32[104,512]{1,0:T(8,128)S(1)}, u32[]{:S(2)}, u32[]{:S(2)}) collective-permute-start(f32[104,512]{1,0:T(8,128)S(1)} %get-tuple-element.12), channel_id=1, source_target_pairs={{0,7},{1,5},{2,6},{3,4},{4,3},{5,1},{6,2},{7,0},{8,15},{9,13},{10,... | collective-permute-start | bytes 638984 | tf_op jit(solution)/shard_map/ppermute | solution.py:27
  11.6 17.9 %collective-permute-start.2 = (f32[104,512]{1,0:T(8,128)S(1)}, f32[104,512]{1,0:T(8,128)S(1)}, u32[]{:S(2)}, u32[]{:S(2)}) collective-permute-start(f32[104,512]{1,0:T(8,128)S(1)} %get-tuple-element.13), channel_id=1, source_target_pairs={{0,11},{1,9},{2,10},{3,8},{4,15},{5,13},{6,14},{7,12},{8,3},{9,1},... | collective-permute-start | bytes 638984 | tf_op jit(solution)/shard_map/ppermute | solution.py:27
  14.4 15.1 %collective-permute-start.3 = (f32[104,512]{1,0:T(8,128)S(1)}, f32[104,512]{1,0:T(8,128)S(1)}, u32[]{:S(2)}, u32[]{:S(2)}) collective-permute-start(f32[104,512]{1,0:T(8,128)S(1)} %get-tuple-element.14), channel_id=1, source_target_pairs={{0,15},{1,13},{2,14},{3,12},{4,11},{5,9},{6,10},{7,8},{8,7},{9,5},... | collective-permute-start | bytes 638984 | tf_op jit(solution)/shard_map/ppermute | solution.py:27
  26.6 3.4 %collective-permute-start.4 = (f32[104,512]{1,0:T(8,128)S(1)}, f32[104,512]{1,0:T(8,128)S(1)}, u32[]{:S(2)}, u32[]{:S(2)}) collective-permute-start(f32[104,512]{1,0:T(8,128)S(1)} %collective-permute-done.refs_0_), channel_id=1, source_target_pairs={{0,1},{1,0},{2,3},{3,2},{4,5},{5,4},{6,7},{7,6},{8,9},{9,8},{10,11... | collective-permute-start | bytes 638984 | tf_op jit(solution)/shard_map/ppermute | solution.py:27
  26.6 3.4 %collective-permute-start.5 = (f32[104,512]{1,0:T(8,128)S(1)}, f32[104,512]{1,0:T(8,128)S(1)}, u32[]{:S(2)}, u32[]{:S(2)}) collective-permute-start(f32[104,512]{1,0:T(8,128)S(1)} %collective-permute-done.1.refs_1_), channel_id=1, source_target_pairs={{0,1},{1,0},{2,3},{3,2},{4,5},{5,4},{6,7},{7,6},{8,9},{9,8},{10,11... | collective-permute-start | bytes 638984 | tf_op jit(solution)/shard_map/ppermute | solution.py:27
  29.5 1.5 %collective-permute-start.6 = (f32[104,512]{1,0:T(8,128)S(1)}, f32[104,512]{1,0:T(8,128)S(1)}, u32[]{:S(2)}, u32[]{:S(2)}) collective-permute-start(f32[104,512]{1,0:T(8,128)S(1)} %collective-permute-done.2.refs_2_), channel_id=1, source_target_pairs={{0,1},{1,0},{2,3},{3,2},{4,5},{5,4},{6,7},{7,6},{8,9},{9,8},{10,11... | collective-permute-start | bytes 638984 | tf_op jit(solution)/shard_map/ppermute | solution.py:27
  29.5 1.8 %collective-permute-start.7 = (f32[104,512]{1,0:T(8,128)S(1)}, f32[104,512]{1,0:T(8,128)S(1)}, u32[]{:S(2)}, u32[]{:S(2)}) collective-permute-start(f32[104,512]{1,0:T(8,128)S(1)} %collective-permute-done.3.refs_3_), channel_id=1, source_target_pairs={{0,1},{1,0},{2,3},{3,2},{4,5},{5,4},{6,7},{7,6},{8,9},{9,8},{10,11... | collective-permute-start | bytes 638984 | tf_op jit(solution)/shard_map/ppermute | solution.py:27
  33.3 2.7 %collective-permute-start.9 = (f32[512,512]{1,0:T(8,128)S(1)}, f32[512,512]{1,0:T(8,128)S(1)}, u32[]{:S(2)}, u32[]{:S(2)}) collective-permute-start(f32[512,512]{1,0:T(8,128)S(1)} %shard_map.87.own_ref), channel_id=1, source_target_pairs={{0,1},{1,0},{2,3},{3,2},{4,5},{5,4},{6,7},{7,6},{8,9},{9,8},{10,11... | collective-permute-start | bytes 3145736 | tf_op jit(solution)/shard_map/ppermute | solution.py:27
  37.0 10.2 %collective-permute-start.12 = (f32[128,512]{1,0:T(8,128)S(1)}, f32[128,512]{1,0:T(8,128)S(1)}, u32[]{:S(2)}, u32[]{:S(2)}) collective-permute-start(f32[128,512]{1,0:T(8,128)S(1)} %get-tuple-element.17), channel_id=1, source_target_pairs={{0,4},{1,5},{2,6},{3,7},{4,0},{5,1},{6,2},{7,3},{8,12},{9,13},{10,... | collective-permute-start | bytes 786440 | tf_op jit(solution)/shard_map/ppermute | solution.py:27
  40.1 12.2 %collective-permute-start.10 = (f32[128,512]{1,0:T(8,128)S(1)}, f32[128,512]{1,0:T(8,128)S(1)}, u32[]{:S(2)}, u32[]{:S(2)}) collective-permute-start(f32[128,512]{1,0:T(8,128)S(1)} %get-tuple-element.15), channel_id=1, source_target_pairs={{0,4},{1,5},{2,6},{3,7},{4,0},{5,1},{6,2},{7,3},{8,12},{9,13},{10,... | collective-permute-start | bytes 786440 | tf_op jit(solution)/shard_map/ppermute | solution.py:27
  47.9 5.8 %collective-permute-start.14 = (f32[128,512]{1,0:T(8,128)S(1)}, f32[128,512]{1,0:T(8,128)S(1)}, u32[]{:S(2)}, u32[]{:S(2)}) collective-permute-start(f32[128,512]{1,0:T(8,128)S(1)} %shard_map.90.refs_1_), channel_id=1, source_target_pairs={{0,1},{1,0},{2,3},{3,2},{4,5},{5,4},{6,7},{7,6},{8,9},{9,8},{10,11... | collective-permute-start | bytes 786440 | tf_op jit(solution)/shard_map/ppermute | solution.py:27
  48.0 5.8 %collective-permute-start.15 = (f32[128,512]{1,0:T(8,128)S(1)}, f32[128,512]{1,0:T(8,128)S(1)}, u32[]{:S(2)}, u32[]{:S(2)}) collective-permute-start(f32[128,512]{1,0:T(8,128)S(1)} %shard_map.90.refs_1_), channel_id=1, source_target_pairs={{0,0},{1,1},{2,2},{3,3},{4,8},{5,9},{6,10},{7,11},{8,4},{9,5},{10,... | collective-permute-start | bytes 786440 | tf_op jit(solution)/shard_map/ppermute | solution.py:27
  52.9 1.6 %collective-permute-start.13 = (f32[128,512]{1,0:T(8,128)S(1)}, f32[128,512]{1,0:T(8,128)S(1)}, u32[]{:S(2)}, u32[]{:S(2)}) collective-permute-start(f32[128,512]{1,0:T(8,128)S(1)} %shard_map.89.refs_0_), channel_id=1, source_target_pairs={{0,1},{1,0},{2,3},{3,2},{4,5},{5,4},{6,7},{7,6},{8,9},{9,8},{10,11... | collective-permute-start | bytes 786440 | tf_op jit(solution)/shard_map/ppermute | solution.py:27
  53.0 2.3 %collective-permute-start.11 = (f32[128,512]{1,0:T(8,128)S(1)}, f32[128,512]{1,0:T(8,128)S(1)}, u32[]{:S(2)}, u32[]{:S(2)}) collective-permute-start(f32[128,512]{1,0:T(8,128)S(1)} %shard_map.89.refs_0_), channel_id=1, source_target_pairs={{0,0},{1,1},{2,2},{3,3},{4,8},{5,9},{6,10},{7,11},{8,4},{9,5},{10,... | collective-permute-start | bytes 786440 | tf_op jit(solution)/shard_map/ppermute | solution.py:27
  55.2 9.2 %collective-permute-start.19 = (f32[128,512]{1,0:T(8,128)S(1)}, f32[128,512]{1,0:T(8,128)S(1)}, u32[]{:S(2)}, u32[]{:S(2)}) collective-permute-start(f32[128,512]{1,0:T(8,128)S(1)} %shard_map.92.refs_1_), channel_id=1, source_target_pairs={{0,2},{1,3},{2,0},{3,1},{4,6},{5,7},{6,4},{7,5},{8,10},{9,11},{10,... | collective-permute-start | bytes 786440 | tf_op jit(solution)/shard_map/ppermute | solution.py:27
  56.0 13.3 %collective-permute-start.18 = (f32[128,512]{1,0:T(8,128)S(1)}, f32[128,512]{1,0:T(8,128)S(1)}, u32[]{:S(2)}, u32[]{:S(2)}) collective-permute-start(f32[128,512]{1,0:T(8,128)S(1)} %shard_map.91.refs_0_), channel_id=1, source_target_pairs={{0,2},{1,3},{2,0},{3,1},{4,6},{5,7},{6,4},{7,5},{8,10},{9,11},{10,... | collective-permute-start | bytes 786440 | tf_op jit(solution)/shard_map/ppermute | solution.py:27
  58.0 11.2 %collective-permute-start.17 = (f32[128,512]{1,0:T(8,128)S(1)}, f32[128,512]{1,0:T(8,128)S(1)}, u32[]{:S(2)}, u32[]{:S(2)}) collective-permute-start(f32[128,512]{1,0:T(8,128)S(1)} %shard_map.92.refs_1_), channel_id=1, source_target_pairs={{0,1},{1,0},{2,3},{3,2},{4,5},{5,4},{6,7},{7,6},{8,9},{9,8},{10,11... | collective-permute-start | bytes 786440 | tf_op jit(solution)/shard_map/ppermute | solution.py:27
  58.0 11.2 %collective-permute-start.16 = (f32[128,512]{1,0:T(8,128)S(1)}, f32[128,512]{1,0:T(8,128)S(1)}, u32[]{:S(2)}, u32[]{:S(2)}) collective-permute-start(f32[128,512]{1,0:T(8,128)S(1)} %shard_map.91.refs_0_), channel_id=1, source_target_pairs={{0,1},{1,0},{2,3},{3,2},{4,5},{5,4},{6,7},{7,6},{8,9},{9,8},{10,11... | collective-permute-start | bytes 786440 | tf_op jit(solution)/shard_map/ppermute | solution.py:27
  64.5 4.8 %collective-permute-start.21 = (f32[128,512]{1,0:T(8,128)S(1)}, f32[128,512]{1,0:T(8,128)S(1)}, u32[]{:S(2)}, u32[]{:S(2)}) collective-permute-start(f32[128,512]{1,0:T(8,128)S(1)} %collective-permute-done.19.refs_5_), channel_id=1, source_target_pairs={{0,1},{1,0},{2,3},{3,2},{4,5},{5,4},{6,7},{7,6},{8,9},{9,8},{10,11... | collective-permute-start | bytes 786440 | tf_op jit(solution)/shard_map/ppermute | solution.py:27
  69.2 1.5 %collective-permute-start.20 = (f32[128,512]{1,0:T(8,128)S(1)}, f32[128,512]{1,0:T(8,128)S(1)}, u32[]{:S(2)}, u32[]{:S(2)}) collective-permute-start(f32[128,512]{1,0:T(8,128)S(1)} %collective-permute-done.18.refs_4_), channel_id=1, source_target_pairs={{0,1},{1,0},{2,3},{3,2},{4,5},{5,4},{6,7},{7,6},{8,9},{9,8},{10,11... | collective-permute-start | bytes 786440 | tf_op jit(solution)/shard_map/ppermute | solution.py:27
  72.3 8.2 %collective-permute-start.22 = (f32[72,256]{1,0:T(8,128)S(1)}, f32[72,256]{1,0:T(8,128)S(1)}, u32[]{:S(2)}, u32[]{:S(2)}) collective-permute-start(f32[72,256]{1,0:T(8,128)S(1)} %get-tuple-element.19), channel_id=1, source_target_pairs={{0,4},{1,5},{2,6},{3,7},{4,0},{5,1},{6,2},{7,3},{8,12},{9,13},{10,... | collective-permute-start | bytes 221192 | tf_op jit(solution)/shard_map/ppermute | solution.py:27

commit v4 on v3

--- a/solution.py
+++ b/solution.py
@@ -7,32 +7,55 @@
 from jax.experimental.pallas import tpu as pltpu
 from jax.sharding import PartitionSpec as P
 
-AXES = ("tile", "cuts")
+
+AXES = ("groups", "tile", "cuts")
 VMEM = pl.BlockSpec(memory_space=pltpu.VMEM)
 BF, F32 = jnp.bfloat16, jnp.float32
 PAD = 8
 GRANT = 16 << 20
 
 
-def pairs(tiles, place):
+def pairs(groups, tiles, place):
     out = []
-    for t in range(tiles):
-        for c in range(2):
-            to, core = place(t, c)
-            out.append((t * 2 + c, to * 2 + core))
+    for g in range(groups):
+        for t in range(tiles):
+            for c in range(2):
+                to, core, *cross = place(t, c)
+                group = g ^ 1 if cross and (g ^ 1) < groups else g
+                out.append(((g * tiles + t) * 2 + c, (group * tiles + to) * 2 + core))
     return out
 
 
 def moved(x, place):
-    return lax.ppermute(x, AXES, pairs(lax.axis_size("tile"), place))
-
-
-def routed(m):
+    return lax.ppermute(x, AXES, pairs(lax.axis_size("groups"), lax.axis_size("tile"), place))
+
+
+def native():
+    return (lax.axis_index("tile") & 1) != lax.axis_index("cuts")
+
+
+def swapped(t, c):
+    return (t ^ 1, c ^ 1) if (t & 1) == c else (t, c, True)
+
+
+def turned(group, sets):
+    return 3 if sets == 4 and group in (1, 2) else 0
+
+
+def routed(m, sets):
     def place(t, c):
-        to = t ^ (m << 1)
+        step = m ^ turned(t >> 1, sets)
+        if step == 0:
+            return swapped(t, c)
+        to = t ^ (step << 1)
         return (to ^ 1, c ^ 1) if (t & 1) == c else (to, c)
 
     return place
+
+
+def is_inner(sets):
+    group = lax.axis_index("tile") >> 1
+    return ((group == 1) | (group == 2)) if sets == 4 else group < 0
 
 
 def other_core(t, c):
@@ -87,13 +110,16 @@
 
 def pack_kernel(tiles, cap, rows_ref, owner_ref, leaf_ref, exp_ref, order_ref, sign_ref, *outs):
     count = rows_ref.shape[0]
+    lanes = rows_ref.shape[1] // 128
+    last = lanes * 2 * cap
     tile = lax.axis_index("tile")
     own = owner_ref[...]
     hits = own == lax.broadcasted_iota(jnp.int32, (tiles, count), 0)
     earlier = lax.broadcasted_iota(jnp.int32, (count, count), 0) < lax.broadcasted_iota(jnp.int32, (count, count), 1)
     before = mul(jnp.where(hits, 1.0, 0.0).astype(BF), jnp.where(earlier, 1.0, 0.0).astype(BF))
     position = jnp.sum(jnp.where(hits, before, 0.0), axis=0, keepdims=True).astype(jnp.int32)
-    placed = (own ^ tile) * cap + position
+    flip = jnp.where(is_inner(len(outs)), 6, 0)
+    placed = (own ^ tile ^ flip) * cap + position
     power = exp_ref[...]
     factor = jnp.where(power == -1, 0.5, jnp.where(power == 1, 2.0, 1.0))
     row = leaf_ref[...] + 1
@@ -104,41 +130,67 @@
         slots = lax.broadcasted_iota(jnp.int32, (2 * cap, count), 0) + m * 2 * cap
         hot = slots == placed
         pick = jnp.where(hot, factor, 0.0).astype(BF)
-        out[0 : 2 * cap, :] = mul(pick, hi) + (mul(pick, mid) + mul(pick, lo))
-        out[2 * cap : 2 * cap + PAD, :] = jnp.zeros((PAD, out.shape[1]), F32)
-        out[2 * cap : 2 * cap + PAD, 0 : 2 * cap] = mul(digits, jnp.where(hot, 1.0, 0.0).astype(BF), ((1,), (1,)))
-    signs = 1 - 2 * sign_ref[...]
-    outs[0][2 * cap + 2 : 2 * cap + 3, :] = ((order_ref[...] + 1) * signs).astype(F32)
-
-
-def leaf_kernel(cap, count, *refs):
-    near, far, env_ref, leaf_ref = refs[:count], refs[count : 2 * count], refs[2 * count], refs[2 * count + 1]
-    width = env_ref.shape[1]
-    eh, el = split2(env_ref[...])
+        rows = mul(pick, hi) + (mul(pick, mid) + mul(pick, lo))
+        for j in range(lanes):
+            out[j * 2 * cap : (j + 1) * 2 * cap, :] = rows[:, j * 128 : (j + 1) * 128]
+        out[last : last + PAD, :] = jnp.zeros((PAD, 128), F32)
+        out[last : last + PAD, 0 : 2 * cap] = mul(digits, jnp.where(hot, 1.0, 0.0).astype(BF), ((1,), (1,)))
+    code = ((order_ref[...] + 1) * (1 - 2 * sign_ref[...])).astype(F32)
+    for out in (outs[0], outs[-1]):
+        for j in range(lanes):
+            out[last + 2 + j : last + 3 + j, :] = code[:, j * 128 : (j + 1) * 128]
+
+
+def spread_rows(cap, blocks, eh, el):
+    width = eh.shape[1]
+    last = width // 128 * 2 * cap
     lane = lax.broadcasted_iota(jnp.int32, (1, 128), 1)
     targets = lax.broadcasted_iota(jnp.int32, (width, 128), 0) + 1
-    total = None
-    for m in range(0, count, 2):
-        spread, chosen = [], []
-        for i in (m, m + 1):
-            block = jnp.concatenate([near[i][0:cap, :], far[i][cap : 2 * cap, :]], axis=0)
-            bh, bl = split2(block)
-            spread.append(mul(bh, eh) + (mul(bh, el) + mul(bl, eh)))
-            spread.append(jnp.zeros((128 - 2 * cap, width), F32))
-            digits = jnp.where(lane < cap, near[i][2 * cap : 2 * cap + PAD, 0:128], far[i][2 * cap : 2 * cap + PAD, 0:128])
-            to = (digits[0:1, :] * 16.0 + digits[1:2, :]).astype(jnp.int32)
-            to = jnp.where(lane < 2 * cap, to, 0)
-            chosen.append(jnp.where(targets == to, 1.0, 0.0).astype(BF))
-        sh, sl = split2(jnp.concatenate(spread, axis=0))
-        pick = jnp.concatenate(chosen, axis=1)
-        part = mul(pick, sh) + mul(pick, sl)
-        total = part if total is None else total + part
-    code = near[0][2 * cap : 2 * cap + PAD, :]
-    column = jnp.transpose(code)[:, 2:3]
+    spread, chosen = [], []
+    for near, far in blocks:
+        columns = [
+            jnp.concatenate([near[at : at + cap, :], far[at + cap : at + 2 * cap, :]], axis=0)
+            for at in range(0, last, 2 * cap)
+        ]
+        bh, bl = split2(jnp.concatenate(columns, axis=1))
+        spread.append(mul(bh, eh) + (mul(bh, el) + mul(bl, eh)))
+        spread.append(jnp.zeros((128 - 2 * cap, width), F32))
+        digits = jnp.where(lane < cap, near[last : last + PAD, :], far[last : last + PAD, :])
+        to = (digits[0:1, :] * 16.0 + digits[1:2, :]).astype(jnp.int32)
+        to = jnp.where(lane < 2 * cap, to, 0)
+        chosen.append(jnp.where(targets == to, 1.0, 0.0).astype(BF))
+    sh, sl = split2(jnp.concatenate(spread, axis=0))
+    pick = jnp.concatenate(chosen, axis=1)
+    return mul(pick, sh) + mul(pick, sl)
+
+
+def early_leaf_kernel(cap, sets, *refs):
+    env_own_ref, env_got_ref, part_ref, high_ref, low_ref = refs[8:]
+    keep, inner = native(), is_inner(sets)
+    eh, el = split2(jnp.where(keep, env_own_ref[...], env_got_ref[...]))
+    high_ref[...] = eh
+    low_ref[...] = el
+    blocks = []
+    for (own, got, far_own, far_got), stays in ((refs[:4], jnp.logical_not(inner)), (refs[4:8], inner)):
+        near = jnp.where(keep & stays, own[...], got[...])
+        far = jnp.where(jnp.logical_not(keep) & stays, far_own[...], far_got[...])
+        blocks.append((near, far))
+    width = eh.shape[1]
+    lanes = width // 128
+    last = lanes * 2 * cap
+    code = jnp.transpose(jnp.where(inner, blocks[1][0][last : last + PAD, :], blocks[0][0][last : last + PAD, :]))
+    column = jnp.concatenate([code[:, 2 + j : 3 + j] for j in range(lanes)], axis=0)
     bond = (jnp.abs(column) - 1.0).astype(jnp.int32)
     sign = jnp.where(column < 0.0, -1.0, 1.0)
     spots = lax.broadcasted_iota(jnp.int32, (width, width), 1)
-    leaf_ref[...] = total + jnp.where(spots == bond, sign, 0.0)
+    signed = jnp.where(spots == bond, sign, 0.0)
+    part_ref[...] = signed + spread_rows(cap, blocks, eh, el)
+
+
+def late_leaf_kernel(cap, count, *refs):
+    near, far = refs[:count], refs[count : 2 * count]
+    high_ref, low_ref, part_ref, leaf_ref = refs[2 * count :]
+    leaf_ref[...] = part_ref[...] + spread_rows(cap, list(zip(near, far)), high_ref[...], low_ref[...])
 
 
 def half_of(core, value, half_ref):
@@ -224,10 +276,11 @@
     def _():
         out_ref[...] = jnp.transpose(out_ref[...])
 
-    rows = parts[0].shape[0]
-    start = core * (rows * len(parts))
-    for p, part in enumerate(parts):
-        part[...] = out_ref[pl.ds(pl.multiple_of(start + p * rows, 8), rows), :]
+    start = core * (out_ref.shape[0] // 2)
+    for part in parts:
+        rows = part.shape[0]
+        part[...] = out_ref[pl.ds(pl.multiple_of(start, 8), rows), :]
+        start = start + rows
 
 
 def fold_kernel(near_ref, own_ref, out_ref):
@@ -251,12 +304,13 @@
     block_ref, send_ref, own_ref, got_ref, whole_ref = refs[4 * count :]
     core, tile = lax.axis_index("cuts"), lax.axis_index("tile")
     side, column, group = (tile >> 2) & 1, tile & 1, tile >> 1
-    rows = own[0].shape[0]
     for ref, near, far in ((own_ref, own, own_far), (got_ref, got, got_far)):
         for at, part in ((core, near), (1 - core, far)):
-            for p, piece in enumerate(part):
-                start = pl.multiple_of(at * (rows * count) + p * rows, 8)
-                ref[pl.ds(start, rows), :] = piece[...]
+            start = at * (ref.shape[0] // 2)
+            for piece in part:
+                rows = piece.shape[0]
+                ref[pl.ds(pl.multiple_of(start, 8), rows), :] = piece[...]
+                start = start + rows
 
     @pl.when(side == column)
     def _():
@@ -284,6 +338,14 @@
 
         ref[0:high, :] = got_ref[pl.ds(pl.multiple_of(column * high, 8), high), 0:cols] / spread
     send_ref[high : high + PAD, :] = jnp.broadcast_to(jnp.log(spread), (PAD, cols))
+
+
+def choose_kernel(block_ref, send_ref, got_ref, out_ref, log_ref):
+    group = lax.axis_index("tile") >> 1
+    inner = (group == 1) | (group == 2)
+    high = out_ref.shape[0]
+    out_ref[...] = jnp.where(inner, block_ref[...], got_ref[0:high, :])
+    log_ref[...] = jnp.where(inner, send_ref[high : high + 1, 0:1], got_ref[high : high + 1, 0:1])
 
 
 def plain_leaf(slice_rows, row_owner, leaf_row, exponent, environment, ordering, sign_mask, tiles, cap):
@@ -303,30 +365,42 @@
     columns = jnp.arange(width, dtype=jnp.int32)
     signs = 1.0 - 2.0 * sign_mask[0].astype(F32)
     leaf = contracted + (ordering[0][:, None] == columns[None, :]).astype(F32) * signs[:, None]
-    return moved(leaf, routed(0))
+    return jnp.where(native(), leaf, moved(leaf, swapped))
 
 
 def packed_leaf(slice_rows, row_owner, leaf_row, exponent, environment, ordering, sign_mask, tiles, cap):
     count, width = slice_rows.shape
     sets = tiles // 2
-    env = moved(environment, routed(0))
+    env = moved(environment, swapped)
     line = lambda a: a.reshape(1, count)
     outgoing = call(
         functools.partial(pack_kernel, tiles, cap),
-        [like(2 * cap + PAD, width)] * sets,
+        [like(2 * cap * (width // 128) + PAD, 128)] * sets,
         (slice_rows, line(row_owner), line(leaf_row), line(exponent), ordering, sign_mask),
         flops=6 * tiles * cap * count * width,
         held=False,
     )
-    near = [None] * sets
-    for m in sorted(range(sets), key=lambda m: -m):
-        near[m] = moved(outgoing[m], routed(m))
-    far = [moved(block, other_core) for block in near]
+    near, far = [None] * sets, [None] * sets
+    ends = (0, sets - 1)
+    for m in (sets - 1, 0, *range(sets - 2, 0, -1)):
+        near[m] = moved(outgoing[m], routed(m, sets))
+    for m in range(sets):
+        far[m] = moved(near[m], other_core)
+    far_own = {m: moved(outgoing[m], other_core) for m in ends}
+    split = jax.ShapeDtypeStruct((width, width), BF)
+    part, high, low = call(
+        functools.partial(early_leaf_kernel, cap, sets),
+        [like(width, width), split, split],
+        [x for m in ends for x in (outgoing[m], near[m], far_own[m], far[m])] + [environment, env],
+        flops=5 * width**3,
+    )
+    if sets == 2:
+        return part
     (leaf,) = call(
-        functools.partial(leaf_kernel, cap, sets),
+        functools.partial(late_leaf_kernel, cap, sets - 2),
         [like(width, width)],
-        (*near, *far, env),
-        flops=10 * width**3,
+        (*near[1:-1], *far[1:-1], high, low, part),
+        flops=5 * width**3,
     )
     return leaf
 
@@ -335,7 +409,7 @@
     tiles = lax.axis_size("tile")
     count, width = slice_rows.shape
     cap = max(2, (3 * count + 2 * tiles - 1) // (2 * tiles))
-    narrow = cap % 8 == 0 and 2 * cap <= 128 and 2 <= tiles // 2 <= 8 and width % 128 == 0
+    narrow = cap % 8 == 0 and 2 * cap <= 128 and tiles // 2 in (2, 4, 8) and width % 128 == 0 and width <= 768
     make_leaf = packed_leaf if narrow else plain_leaf
     leaf = make_leaf(slice_rows, row_owner, leaf_row, exponent, environment, ordering, sign_mask, tiles, cap)
     if tiles == 8 and width % 512 == 0:
@@ -344,27 +418,32 @@
 
 
 def center(t, c):
-    return (t ^ 6 if t >> 1 in (1, 2) else t), c
+    return (t ^ 6, c) if t >> 1 in (1, 2) else (t, c ^ 1)
+
+
+def piece_rows(size):
+    long = 3 * size // 8
+    return long, long, size - 2 * long
 
 
 def center_tree(leaf, tiles, width):
-    count = 2
-    rows = width // 2 // count
+    sizes = piece_rows(width // 2)
+    count = len(sizes)
     cost = 6 * width**2
-    whole, piece = like(width, width), like(rows, width)
+    pieces = [like(rows, width) for rows in sizes]
     own, *parts = call(
-        fold_pair_kernel, [whole] + [piece] * count, (leaf, moved(leaf, other_core)), flops=cost * width
+        fold_pair_kernel, [like(width, width)] + pieces, (leaf, moved(leaf, other_core)), flops=cost * width
     )
     near = [moved(part, across(1)) for part in parts]
     first, first_far, got = [], [], []
     for p in range(count):
-        (done,) = call(fold_kernel, [piece], (near[p], own), flops=cost * rows)
+        (done,) = call(fold_kernel, [pieces[p]], (near[p], own), flops=cost * sizes[p])
         first.append(done)
         got.append(moved(done, center))
         first_far.append(moved(done, other_core))
     mine, mine_far, theirs, theirs_far = [], [], [], []
     for p in range(count):
-        (done,) = call(fold_wide_kernel, [piece], (got[p], *first, *first_far), flops=cost * rows)
+        (done,) = call(fold_wide_kernel, [pieces[p]], (got[p], *first, *first_far), flops=cost * sizes[p])
         mine.append(done)
         theirs.append(moved(done, across(0)))
         mine_far.append(moved(done, other_core))
@@ -377,11 +456,10 @@
         scratch=[pltpu.VMEM((width, width), F32)] * 3,
         flops=cost * width,
     )
-    got = moved(send, across(1))
-    group = lax.axis_index("tile") >> 1
-    inner = (group == 1) | (group == 2)
-    log = jnp.where(inner, send[high, 0], got[high, 0])
-    return jnp.where(inner, block, got[:high]), log.reshape(1)
+    out, log = call(
+        choose_kernel, [like(high, cols), like(1, 1)], (block, send, moved(send, across(1))), kept=False
+    )
+    return out, log.reshape(1)
 
 
 def plain_tree(leaf, tiles, width):

time: 84.3 us -> 82.7 us (0.981)
  between operations: 3.23 us -> 0.79 us
  Pallas kernels: 9.02 us -> 11 us
  waiting for transfers between devices: 43.5 us -> 44.8 us
  local copies, waits for them, and re-layouts: 1.02 us -> 0.01 us
    pallas_call x8 -> x12, Pallas kernels: 9.02 us -> 11 us  [call(): pl.pallas_call(kernel, out_shape=tuple((pltpu.VMEM(o.shape, o.dtype) if k...]
    ppermute x23 -> x31, waiting for transfers between devices: 43.5 us -> 44.8 us  [moved(): lax.ppermute(x, AXES, pairs(lax.axis_size('groups'), lax.axis_size('tile'...]
    slice x2 -> x0, local copies, waits for them, and re-layouts: 1.02 us -> none  [center_tree(): log = jnp.where(inner, send[high, 0], got[high, 0])]
    ppermute x23 -> x31, starting transfers between devices: 26.6 us -> 25.9 us  [moved(): lax.ppermute(x, AXES, pairs(lax.axis_size('groups'), lax.axis_size('tile'...]
  transfers between devices with their start and end apart: 23 -> 31, of which waited for: 12 -> 13; matrix products, arithmetic and copies ran while one was open for 1% -> 0% of each run, Pallas kernels for 5% -> 8%
where the time goes in v4:
time: 82.7 us; the launch traced here: 82.5 us
  waiting for transfers between devices  44.8 us (54%)
  starting transfers between devices  25.9 us (31%)
  Pallas kernels  11 us (13%)
    ppermute x31, waiting for transfers between devices, moved(): lax.ppermute(x, AXES, pairs(lax.axis_size('groups'), lax.axis_size('tile'...  44.8 us
    ppermute x31, starting transfers between devices, moved(): lax.ppermute(x, AXES, pairs(lax.axis_size('groups'), lax.axis_size('tile'...  25.9 us
    pallas_call x12, Pallas kernels, call(): pl.pallas_call(kernel, out_shape=tuple((pltpu.VMEM(o.shape, o.dtype) if k...  11 us
  transfers between devices with their start and end apart: 31, of which 13 were waited for; matrix products, arithmetic and copies ran while one was open for 0% of the time, Pallas kernels for 8%

profile of v4, /device:TPU:0, one launch (start us, length us, event | category | flops | bytes accessed | tf_op | source)
XLA Modules:
  0.0 82.5 jit_solution(9472233383877699189)
XLA Ops:
  0.6 2.5 %collective-permute-start.10 = (f32[512,512]{1,0:T(8,128)}, f32[512,512]{1,0:T(8,128)S(1)}, u32[]{:S(2)}, u32[]{:S(2)}) collective-permute-start(f32[512,512]{1,0:T(8,128)} %refs_8_.1), channel_id=1, source_target_pairs={{0,3},{1,17},{2,18},{3,0},{4,7},{5,21},{6,22},{7,4},{8,11},{9,25},... | collective-permute-start | bytes 3145736 | tf_op jit(solution)/shard_map/ppermute | solution.py:30
  3.1 1.9 %shard_map.86 = (f32[392,128]{1,0:T(8,128)S(1)}, f32[392,128]{1,0:T(8,128)S(1)}, f32[392,128]{1,0:T(8,128)S(1)}, f32[392,128]{1,0:T(8,128)S(1)}) custom-call(f32[256,512]{1,0:T(8,128)} %rows_ref.1, s32[1,256]{1,0:T(1,128)} %bitcast.4, s32[1,256]{1,0:T(1,128)} %bitcast.5, s32[1,256]{1,0:T(1,128)} %bitcast.6, s32[1,512]{1,0:T(1,128)} %order_ref.1, ...), custom_call_target="tpu_custom_call" | custom-call | flops 301989888 | bytes 1334272 | tf_op jit(solution)/shard_map/pallas_call | solution.py:96
  5.0 0.1 collective-permute-start.4
  5.1 4.7 %collective-permute-start.7 = (f32[392,128]{1,0:T(8,128)S(1)}, f32[392,128]{1,0:T(8,128)S(1)}, u32[]{:S(2)}, u32[]{:S(2)}) collective-permute-start(f32[392,128]{1,0:T(8,128)S(1)} %get-tuple-element.20.refs_4_), channel_id=1, source_target_pairs={{0,15},{1,13},{2,14},{3,12},{4,7},{5,21},{6,22},{7,4},{8,11},{9,25... | collective-permute-start | bytes 602120 | tf_op jit(solution)/shard_map/ppermute | solution.py:30
  9.8 0.0 collective-permute-start.5
  9.8 0.5 collective-permute-start.8
  10.4 9.8 %collective-permute-done.4.refs_1_ = f32[392,128]{1,0:T(8,128)S(1)} collective-permute-done((f32[392,128]{1,0:T(8,128)S(1)}, f32[392,128]{1,0:T(8,128)S(1)}, u32[]{:S(2)}, u32[]{:S(2)}) %collective-permute-start.4) | collective-permute-done | bytes 200736 | tf_op jit(solution)/shard_map/ppermute | solution.py:30
  20.1 0.0 collective-permute-start
  20.1 0.0 collective-permute-done.7.refs_5_
  20.1 3.8 %collective-permute-start.1 = (f32[392,128]{1,0:T(8,128)S(1)}, f32[392,128]{1,0:T(8,128)S(1)}, u32[]{:S(2)}, u32[]{:S(2)}) collective-permute-start(f32[392,128]{1,0:T(8,128)S(1)} %get-tuple-element.18), channel_id=1, source_target_pairs={{0,11},{1,9},{2,10},{3,8},{4,3},{5,1},{6,2},{7,0},{8,15},{9,13},{1... | collective-permute-start | bytes 602120 | tf_op jit(solution)/shard_map/ppermute | solution.py:30
  23.9 0.0 collective-permute-done.5.refs_2_
  23.9 0.0 collective-permute-start.6
  23.9 0.0 collective-permute-done.8.refs_6_
  23.9 0.5 collective-permute-start.9
  24.4 4.8 %collective-permute-done.refs_0_ = f32[392,128]{1,0:T(8,128)S(1)} collective-permute-done((f32[392,128]{1,0:T(8,128)S(1)}, f32[392,128]{1,0:T(8,128)S(1)}, u32[]{:S(2)}, u32[]{:S(2)}) %collective-permute-start) | collective-permute-done | bytes 200736 | tf_op jit(solution)/shard_map/ppermute | solution.py:30
  29.2 0.0 collective-permute-start.2
  29.2 4.2 %collective-permute-done.1.refs_1_ = f32[392,128]{1,0:T(8,128)S(1)} collective-permute-done((f32[392,128]{1,0:T(8,128)S(1)}, f32[392,128]{1,0:T(8,128)S(1)}, u32[]{:S(2)}, u32[]{:S(2)}) %collective-permute-start.1) | collective-permute-done | bytes 200736 | tf_op jit(solution)/shard_map/ppermute | solution.py:30
  33.3 0.0 collective-permute-start.3
  33.3 0.0 collective-permute-done.6.refs_3_
  33.3 0.0 collective-permute-done.9.refs_7_
  33.3 0.0 collective-permute-done.10.refs_9_
  33.4 1.2 %shard_map.87 = (f32[512,512]{1,0:T(8,128)S(1)}, bf16[512,512]{1,0:T(8,128)(2,1)S(1)}, bf16[512,512]{1,0:T(8,128)(2,1)S(1)}) custom-call(f32[392,128]{1,0:T(8,128)S(1)} %get-tuple-element.19.refs_0_, f32[392,128]{1,0:T(8,128)S(1)} %collective-permute-done.4.refs_1_, f32[392,128]{1,0:T(8,128)S(1)} %collective-permute-done.5.refs_2_, ...), custom_call_target="tpu_custom_call" | custom-call | flops 671088640 | bytes 6848512 | tf_op jit(solution)/shard_map/pallas_call | solution.py:96
  34.6 0.2 collective-permute-done.3.refs_3_
  34.8 1.1 %shard_map.88.own_ref = f32[512,512]{1,0:T(8,128)S(1)} custom-call(f32[392,128]{1,0:T(8,128)S(1)} %collective-permute-done.refs_0_, f32[392,128]{1,0:T(8,128)S(1)} %collective-permute-done.1.refs_1_, f32[392,128]{1,0:T(8,128)S(1)} %collective-permute-done.2.refs_2_, f32[392,128]{1,0:T(8,128)S(1)} %collective-permute-done.3.refs_3_, ...), custom_call_target="tpu_custom_call" | custom-call | flops 671088640 | bytes 4997120 | tf_op jit(solution)/shard_map/pallas_call | solution.py:96
  35.8 0.4 collective-permute-start.11
  36.2 2.3 %collective-permute-done.11.other_ref = f32[512,512]{1,0:T(8,128)S(1)} collective-permute-done((f32[512,512]{1,0:T(8,128)S(1)}, f32[512,512]{1,0:T(8,128)S(1)}, u32[]{:S(2)}, u32[]{:S(2)}) %collective-permute-start.11) | collective-permute-done | bytes 1048608 | tf_op jit(solution)/shard_map/ppermute | solution.py:30
  38.6 1.0 %shard_map.89 = (f32[512,512]{1,0:T(8,128)S(1)}, f32[96,512]{1,0:T(8,128)S(1)}, f32[96,512]{1,0:T(8,128)S(1)}, f32[64,512]{1,0:T(8,128)S(1)}) custom-call(f32[512,512]{1,0:T(8,128)S(1)} %shard_map.88.own_ref, f32[512,512]{1,0:T(8,128)S(1)} %collective-permute-done.11.other_ref), custom_call_target="tpu_custom_call" | custom-call | flops 805306368 | bytes 3670016 | tf_op jit(solution)/shard_map/pallas_call | solution.py:96
  39.6 1.6 %collective-permute-start.14 = (f32[96,512]{1,0:T(8,128)S(1)}, f32[96,512]{1,0:T(8,128)S(1)}, u32[]{:S(2)}, u32[]{:S(2)}) collective-permute-start(f32[96,512]{1,0:T(8,128)S(1)} %get-tuple-element.26), channel_id=1, source_target_pairs={{0,4},{1,5},{2,6},{3,7},{4,0},{5,1},{6,2},{7,3},{8,12},{9,13},{10,... | collective-permute-start | bytes 589832 | tf_op jit(solution)/shard_map/ppermute | solution.py:30
  41.2 0.5 collective-permute-start.12
  41.7 1.6 %collective-permute-start.15 = (f32[64,512]{1,0:T(8,128)S(1)}, f32[64,512]{1,0:T(8,128)S(1)}, u32[]{:S(2)}, u32[]{:S(2)}) collective-permute-start(f32[64,512]{1,0:T(8,128)S(1)} %get-tuple-element.27), channel_id=1, source_target_pairs={{0,4},{1,5},{2,6},{3,7},{4,0},{5,1},{6,2},{7,3},{8,12},{9,13},{10,... | collective-permute-start | bytes 393224 | tf_op jit(solution)/shard_map/ppermute | solution.py:30
  43.3 4.2 %collective-permute-done.14.near_ref = f32[96,512]{1,0:T(8,128)S(1)} collective-permute-done((f32[96,512]{1,0:T(8,128)S(1)}, f32[96,512]{1,0:T(8,128)S(1)}, u32[]{:S(2)}, u32[]{:S(2)}) %collective-permute-start.14) | collective-permute-done | bytes 196640 | tf_op jit(solution)/shard_map/ppermute | solution.py:30
  47.4 0.6 shard_map.91.refs_1_
  48.1 0.1 collective-permute-start.17
  48.1 3.5 %collective-permute-done.12.near_ref = f32[96,512]{1,0:T(8,128)S(1)} collective-permute-done((f32[96,512]{1,0:T(8,128)S(1)}, f32[96,512]{1,0:T(8,128)S(1)}, u32[]{:S(2)}, u32[]{:S(2)}) %collective-permute-start.12) | collective-permute-done | bytes 196640 | tf_op jit(solution)/shard_map/ppermute | solution.py:30
  51.7 0.6 shard_map.90.refs_0_
  52.3 0.1 collective-permute-start.16
  52.4 0.5 collective-permute-start.19
  52.9 0.1 collective-permute-start.13
  52.9 0.9 %collective-permute-done.15.near_ref = f32[64,512]{1,0:T(8,128)S(1)} collective-permute-done((f32[64,512]{1,0:T(8,128)S(1)}, f32[64,512]{1,0:T(8,128)S(1)}, u32[]{:S(2)}, u32[]{:S(2)}) %collective-permute-start.15) | collective-permute-done | bytes 131104 | tf_op jit(solution)/shard_map/ppermute | solution.py:30
  53.8 0.6 shard_map.92.refs_2_
  54.4 0.1 collective-permute-start.18
  54.5 1.3 %collective-permute-done.18.refs_5_ = f32[64,512]{1,0:T(8,128)S(1)} collective-permute-done((f32[64,512]{1,0:T(8,128)S(1)}, f32[64,512]{1,0:T(8,128)S(1)}, u32[]{:S(2)}, u32[]{:S(2)}) %collective-permute-start.18) | collective-permute-done | bytes 131104 | tf_op jit(solution)/shard_map/ppermute | solution.py:30
  55.8 0.1 collective-permute-start.20
  56.0 0.6 shard_map.94.refs_1_
  56.6 0.5 collective-permute-start.25
  57.1 0.0 collective-permute-done.13.near_ref
  57.1 0.6 shard_map.93.refs_0_
  57.8 1.6 %collective-permute-start.24 = (f32[96,512]{1,0:T(8,128)S(1)}, f32[96,512]{1,0:T(8,128)S(1)}, u32[]{:S(2)}, u32[]{:S(2)}) collective-permute-start(f32[96,512]{1,0:T(8,128)S(1)} %shard_map.93.refs_0_), channel_id=1, source_target_pairs={{0,2},{1,3},{2,0},{3,1},{4,6},{5,7},{6,4},{7,5},{8,10},{9,11},{10,... | collective-permute-start | bytes 589832 | tf_op jit(solution)/shard_map/ppermute | solution.py:30
  59.4 0.0 collective-permute-done.20.near_ref
  59.4 0.6 shard_map.95.refs_2_
  60.0 0.5 collective-permute-start.26
  60.5 0.0 collective-permute-start.23
  60.5 0.5 collective-permute-start.22
  61.0 9.8 %collective-permute-done.26.refs_8_ = f32[64,512]{1,0:T(8,128)S(1)} collective-permute-done((f32[64,512]{1,0:T(8,128)S(1)}, f32[64,512]{1,0:T(8,128)S(1)}, u32[]{:S(2)}, u32[]{:S(2)}) %collective-permute-start.26) | collective-permute-done | bytes 131104 | tf_op jit(solution)/shard_map/ppermute | solution.py:30
  70.9 0.5 collective-permute-start.28
  71.4 0.1 collective-permute-start.27
  71.5 0.4 collective-permute-start.29
  71.9 0.4 collective-permute-done.21.refs_3_
  72.3 0.7 collective-permute-done.29.refs_11_
  73.1 0.0 collective-permute-done.28.refs_10_
  73.1 1.5 %shard_map.96 = (f32[64,256]{1,0:T(8,128)S(1)}, f32[72,256]{1,0:T(8,128)S(1)}) custom-call(f32[96,512]{1,0:T(8,128)S(1)} %shard_map.93.refs_0_, f32[96,512]{1,0:T(8,128)S(1)} %shard_map.94.refs_1_, f32[64,512]{1,0:T(8,128)S(1)} %shard_map.95.refs_2_, f32[96,512]{1,0:T(8,128)S(1)} %collective-permute-done.21.refs_3_, ...), custom_call_target="tpu_custom_call" | custom-call | flops 805306368 | bytes 2236416 | tf_op jit(solution)/shard_map/pallas_call | solution.py:96
  74.6 4.6 %collective-permute-start.30 = (f32[72,256]{1,0:T(8,128)S(1)}, f32[72,256]{1,0:T(8,128)S(1)}, u32[]{:S(2)}, u32[]{:S(2)}) collective-permute-start(f32[72,256]{1,0:T(8,128)S(1)} %get-tuple-element.29.send_ref), channel_id=1, source_target_pairs={{0,4},{1,5},{2,6},{3,7},{4,0},{5,1},{6,2},{7,3},{8,12},{9,13},{10,... | collective-permute-start | bytes 221192 | tf_op jit(solution)/shard_map/ppermute | solution.py:30
  79.2 2.7 %collective-permute-done.30.got_ref = f32[72,256]{1,0:T(8,128)S(1)} collective-permute-done((f32[72,256]{1,0:T(8,128)S(1)}, f32[72,256]{1,0:T(8,128)S(1)}, u32[]{:S(2)}, u32[]{:S(2)}) %collective-permute-start.30) | collective-permute-done | bytes 73760 | tf_op jit(solution)/shard_map/ppermute | solution.py:30
  81.9 0.6 shard_map.97
  (12 shorter events, 0.0 us)
Async XLA Ops:
  0.6 32.7 %copy-start = (f32[512,512]{1,0:T(8,128)S(1)}, f32[512,512]{1,0:T(8,128)}, u32[]{:S(2)}) copy-start(f32[512,512]{1,0:T(8,128)} %refs_8_.1) | copy-start | bytes 3145732
  0.6 32.7 %collective-permute-start.10 = (f32[512,512]{1,0:T(8,128)}, f32[512,512]{1,0:T(8,128)S(1)}, u32[]{:S(2)}, u32[]{:S(2)}) collective-permute-start(f32[512,512]{1,0:T(8,128)} %refs_8_.1), channel_id=1, source_target_pairs={{0,3},{1,17},{2,18},{3,0},{4,7},{5,21},{6,22},{7,4},{8,11},{9,25},... | collective-permute-start | bytes 3145736 | tf_op jit(solution)/shard_map/ppermute | solution.py:30
  5.0 15.1 %collective-permute-start.4 = (f32[392,128]{1,0:T(8,128)S(1)}, f32[392,128]{1,0:T(8,128)S(1)}, u32[]{:S(2)}, u32[]{:S(2)}) collective-permute-start(f32[392,128]{1,0:T(8,128)S(1)} %get-tuple-element.19.refs_0_), channel_id=1, source_target_pairs={{0,3},{1,17},{2,18},{3,0},{4,11},{5,9},{6,10},{7,8},{8,7},{9,5},{1... | collective-permute-start | bytes 602120 | tf_op jit(solution)/shard_map/ppermute | solution.py:30
  5.1 15.0 %collective-permute-start.7 = (f32[392,128]{1,0:T(8,128)S(1)}, f32[392,128]{1,0:T(8,128)S(1)}, u32[]{:S(2)}, u32[]{:S(2)}) collective-permute-start(f32[392,128]{1,0:T(8,128)S(1)} %get-tuple-element.20.refs_4_), channel_id=1, source_target_pairs={{0,15},{1,13},{2,14},{3,12},{4,7},{5,21},{6,22},{7,4},{8,11},{9,25... | collective-permute-start | bytes 602120 | tf_op jit(solution)/shard_map/ppermute | solution.py:30
  9.8 14.0 %collective-permute-start.5 = (f32[392,128]{1,0:T(8,128)S(1)}, f32[392,128]{1,0:T(8,128)S(1)}, u32[]{:S(2)}, u32[]{:S(2)}) collective-permute-start(f32[392,128]{1,0:T(8,128)S(1)} %get-tuple-element.19.refs_0_), channel_id=1, source_target_pairs={{0,1},{1,0},{2,3},{3,2},{4,5},{5,4},{6,7},{7,6},{8,9},{9,8},{10,11... | collective-permute-start | bytes 602120 | tf_op jit(solution)/shard_map/ppermute | solution.py:30
  9.8 14.0 %collective-permute-start.8 = (f32[392,128]{1,0:T(8,128)S(1)}, f32[392,128]{1,0:T(8,128)S(1)}, u32[]{:S(2)}, u32[]{:S(2)}) collective-permute-start(f32[392,128]{1,0:T(8,128)S(1)} %get-tuple-element.20.refs_4_), channel_id=1, source_target_pairs={{0,1},{1,0},{2,3},{3,2},{4,5},{5,4},{6,7},{7,6},{8,9},{9,8},{10,11... | collective-permute-start | bytes 602120 | tf_op jit(solution)/shard_map/ppermute | solution.py:30
  20.1 9.0 %collective-permute-start = (f32[392,128]{1,0:T(8,128)S(1)}, f32[392,128]{1,0:T(8,128)S(1)}, u32[]{:S(2)}, u32[]{:S(2)}) collective-permute-start(f32[392,128]{1,0:T(8,128)S(1)} %get-tuple-element.17), channel_id=1, source_target_pairs={{0,7},{1,5},{2,6},{3,4},{4,15},{5,13},{6,14},{7,12},{8,3},{9,1},{1... | collective-permute-start | bytes 602120 | tf_op jit(solution)/shard_map/ppermute | solution.py:30
  20.1 13.2 %collective-permute-start.1 = (f32[392,128]{1,0:T(8,128)S(1)}, f32[392,128]{1,0:T(8,128)S(1)}, u32[]{:S(2)}, u32[]{:S(2)}) collective-permute-start(f32[392,128]{1,0:T(8,128)S(1)} %get-tuple-element.18), channel_id=1, source_target_pairs={{0,11},{1,9},{2,10},{3,8},{4,3},{5,1},{6,2},{7,0},{8,15},{9,13},{1... | collective-permute-start | bytes 602120 | tf_op jit(solution)/shard_map/ppermute | solution.py:30
  23.9 9.5 %collective-permute-start.6 = (f32[392,128]{1,0:T(8,128)S(1)}, f32[392,128]{1,0:T(8,128)S(1)}, u32[]{:S(2)}, u32[]{:S(2)}) collective-permute-start(f32[392,128]{1,0:T(8,128)S(1)} %collective-permute-done.4.refs_1_), channel_id=1, source_target_pairs={{0,1},{1,0},{2,3},{3,2},{4,5},{5,4},{6,7},{7,6},{8,9},{9,8},{10,11... | collective-permute-start | bytes 602120 | tf_op jit(solution)/shard_map/ppermute | solution.py:30
  23.9 9.5 %collective-permute-start.9 = (f32[392,128]{1,0:T(8,128)S(1)}, f32[392,128]{1,0:T(8,128)S(1)}, u32[]{:S(2)}, u32[]{:S(2)}) collective-permute-start(f32[392,128]{1,0:T(8,128)S(1)} %collective-permute-done.7.refs_5_), channel_id=1, source_target_pairs={{0,1},{1,0},{2,3},{3,2},{4,5},{5,4},{6,7},{7,6},{8,9},{9,8},{10,11... | collective-permute-start | bytes 602120 | tf_op jit(solution)/shard_map/ppermute | solution.py:30
  29.2 5.4 %collective-permute-start.2 = (f32[392,128]{1,0:T(8,128)S(1)}, f32[392,128]{1,0:T(8,128)S(1)}, u32[]{:S(2)}, u32[]{:S(2)}) collective-permute-start(f32[392,128]{1,0:T(8,128)S(1)} %collective-permute-done.refs_0_), channel_id=1, source_target_pairs={{0,1},{1,0},{2,3},{3,2},{4,5},{5,4},{6,7},{7,6},{8,9},{9,8},{10,11... | collective-permute-start | bytes 602120 | tf_op jit(solution)/shard_map/ppermute | solution.py:30
  33.3 1.4 %collective-permute-start.3 = (f32[392,128]{1,0:T(8,128)S(1)}, f32[392,128]{1,0:T(8,128)S(1)}, u32[]{:S(2)}, u32[]{:S(2)}) collective-permute-start(f32[392,128]{1,0:T(8,128)S(1)} %collective-permute-done.1.refs_1_), channel_id=1, source_target_pairs={{0,1},{1,0},{2,3},{3,2},{4,5},{5,4},{6,7},{7,6},{8,9},{9,8},{10,11... | collective-permute-start | bytes 602120 | tf_op jit(solution)/shard_map/ppermute | solution.py:30
  35.8 2.7 %collective-permute-start.11 = (f32[512,512]{1,0:T(8,128)S(1)}, f32[512,512]{1,0:T(8,128)S(1)}, u32[]{:S(2)}, u32[]{:S(2)}) collective-permute-start(f32[512,512]{1,0:T(8,128)S(1)} %shard_map.88.own_ref), channel_id=1, source_target_pairs={{0,1},{1,0},{2,3},{3,2},{4,5},{5,4},{6,7},{7,6},{8,9},{9,8},{10,11... | collective-permute-start | bytes 3145736 | tf_op jit(solution)/shard_map/ppermute | solution.py:30
  39.6 7.8 %collective-permute-start.14 = (f32[96,512]{1,0:T(8,128)S(1)}, f32[96,512]{1,0:T(8,128)S(1)}, u32[]{:S(2)}, u32[]{:S(2)}) collective-permute-start(f32[96,512]{1,0:T(8,128)S(1)} %get-tuple-element.26), channel_id=1, source_target_pairs={{0,4},{1,5},{2,6},{3,7},{4,0},{5,1},{6,2},{7,3},{8,12},{9,13},{10,... | collective-permute-start | bytes 589832 | tf_op jit(solution)/shard_map/ppermute | solution.py:30
  41.2 10.4 %collective-permute-start.12 = (f32[96,512]{1,0:T(8,128)S(1)}, f32[96,512]{1,0:T(8,128)S(1)}, u32[]{:S(2)}, u32[]{:S(2)}) collective-permute-start(f32[96,512]{1,0:T(8,128)S(1)} %get-tuple-element.24), channel_id=1, source_target_pairs={{0,4},{1,5},{2,6},{3,7},{4,0},{5,1},{6,2},{7,3},{8,12},{9,13},{10,... | collective-permute-start | bytes 589832 | tf_op jit(solution)/shard_map/ppermute | solution.py:30
  41.7 12.1 %collective-permute-start.15 = (f32[64,512]{1,0:T(8,128)S(1)}, f32[64,512]{1,0:T(8,128)S(1)}, u32[]{:S(2)}, u32[]{:S(2)}) collective-permute-start(f32[64,512]{1,0:T(8,128)S(1)} %get-tuple-element.27), channel_id=1, source_target_pairs={{0,4},{1,5},{2,6},{3,7},{4,0},{5,1},{6,2},{7,3},{8,12},{9,13},{10,... | collective-permute-start | bytes 393224 | tf_op jit(solution)/shard_map/ppermute | solution.py:30
  48.1 7.9 %collective-permute-start.17 = (f32[96,512]{1,0:T(8,128)S(1)}, f32[96,512]{1,0:T(8,128)S(1)}, u32[]{:S(2)}, u32[]{:S(2)}) collective-permute-start(f32[96,512]{1,0:T(8,128)S(1)} %shard_map.91.refs_1_), channel_id=1, source_target_pairs={{0,1},{1,0},{2,3},{3,2},{4,5},{5,4},{6,7},{7,6},{8,9},{9,8},{10,11... | collective-permute-start | bytes 589832 | tf_op jit(solution)/shard_map/ppermute | solution.py:30
  52.3 3.7 %collective-permute-start.16 = (f32[96,512]{1,0:T(8,128)S(1)}, f32[96,512]{1,0:T(8,128)S(1)}, u32[]{:S(2)}, u32[]{:S(2)}) collective-permute-start(f32[96,512]{1,0:T(8,128)S(1)} %shard_map.90.refs_0_), channel_id=1, source_target_pairs={{0,1},{1,0},{2,3},{3,2},{4,5},{5,4},{6,7},{7,6},{8,9},{9,8},{10,11... | collective-permute-start | bytes 589832 | tf_op jit(solution)/shard_map/ppermute | solution.py:30
  52.4 3.6 %collective-permute-start.19 = (f32[96,512]{1,0:T(8,128)S(1)}, f32[96,512]{1,0:T(8,128)S(1)}, u32[]{:S(2)}, u32[]{:S(2)}) collective-permute-start(f32[96,512]{1,0:T(8,128)S(1)} %shard_map.91.refs_1_), channel_id=1, source_target_pairs={{0,1},{1,0},{2,3},{3,2},{4,8},{5,9},{6,10},{7,11},{8,4},{9,5},{10,... | collective-permute-start | bytes 589832 | tf_op jit(solution)/shard_map/ppermute | solution.py:30
  52.9 4.3 %collective-permute-start.13 = (f32[96,512]{1,0:T(8,128)S(1)}, f32[96,512]{1,0:T(8,128)S(1)}, u32[]{:S(2)}, u32[]{:S(2)}) collective-permute-start(f32[96,512]{1,0:T(8,128)S(1)} %shard_map.90.refs_0_), channel_id=1, source_target_pairs={{0,1},{1,0},{2,3},{3,2},{4,8},{5,9},{6,10},{7,11},{8,4},{9,5},{10,... | collective-permute-start | bytes 589832 | tf_op jit(solution)/shard_map/ppermute | solution.py:30
  54.4 1.4 %collective-permute-start.18 = (f32[64,512]{1,0:T(8,128)S(1)}, f32[64,512]{1,0:T(8,128)S(1)}, u32[]{:S(2)}, u32[]{:S(2)}) collective-permute-start(f32[64,512]{1,0:T(8,128)S(1)} %shard_map.92.refs_2_), channel_id=1, source_target_pairs={{0,1},{1,0},{2,3},{3,2},{4,5},{5,4},{6,7},{7,6},{8,9},{9,8},{10,11... | collective-permute-start | bytes 393224 | tf_op jit(solution)/shard_map/ppermute | solution.py:30
  55.8 3.6 %collective-permute-start.20 = (f32[64,512]{1,0:T(8,128)S(1)}, f32[64,512]{1,0:T(8,128)S(1)}, u32[]{:S(2)}, u32[]{:S(2)}) collective-permute-start(f32[64,512]{1,0:T(8,128)S(1)} %shard_map.92.refs_2_), channel_id=1, source_target_pairs={{0,1},{1,0},{2,3},{3,2},{4,8},{5,9},{6,10},{7,11},{8,4},{9,5},{10,... | collective-permute-start | bytes 393224 | tf_op jit(solution)/shard_map/ppermute | solution.py:30
  56.6 14.3 %collective-permute-start.25 = (f32[96,512]{1,0:T(8,128)S(1)}, f32[96,512]{1,0:T(8,128)S(1)}, u32[]{:S(2)}, u32[]{:S(2)}) collective-permute-start(f32[96,512]{1,0:T(8,128)S(1)} %shard_map.94.refs_1_), channel_id=1, source_target_pairs={{0,2},{1,3},{2,0},{3,1},{4,6},{5,7},{6,4},{7,5},{8,10},{9,11},{10,... | collective-permute-start | bytes 589832 | tf_op jit(solution)/shard_map/ppermute | solution.py:30
  57.8 13.6 %collective-permute-start.24 = (f32[96,512]{1,0:T(8,128)S(1)}, f32[96,512]{1,0:T(8,128)S(1)}, u32[]{:S(2)}, u32[]{:S(2)}) collective-permute-start(f32[96,512]{1,0:T(8,128)S(1)} %shard_map.93.refs_0_), channel_id=1, source_target_pairs={{0,2},{1,3},{2,0},{3,1},{4,6},{5,7},{6,4},{7,5},{8,10},{9,11},{10,... | collective-permute-start | bytes 589832 | tf_op jit(solution)/shard_map/ppermute | solution.py:30
  60.0 10.9 %collective-permute-start.26 = (f32[64,512]{1,0:T(8,128)S(1)}, f32[64,512]{1,0:T(8,128)S(1)}, u32[]{:S(2)}, u32[]{:S(2)}) collective-permute-start(f32[64,512]{1,0:T(8,128)S(1)} %shard_map.95.refs_2_), channel_id=1, source_target_pairs={{0,2},{1,3},{2,0},{3,1},{4,6},{5,7},{6,4},{7,5},{8,10},{9,11},{10,... | collective-permute-start | bytes 393224 | tf_op jit(solution)/shard_map/ppermute | solution.py:30
  60.5 10.9 %collective-permute-start.23 = (f32[64,512]{1,0:T(8,128)S(1)}, f32[64,512]{1,0:T(8,128)S(1)}, u32[]{:S(2)}, u32[]{:S(2)}) collective-permute-start(f32[64,512]{1,0:T(8,128)S(1)} %shard_map.95.refs_2_), channel_id=1, source_target_pairs={{0,1},{1,0},{2,3},{3,2},{4,5},{5,4},{6,7},{7,6},{8,9},{9,8},{10,11... | collective-permute-start | bytes 393224 | tf_op jit(solution)/shard_map/ppermute | solution.py:30
  60.5 11.4 %collective-permute-start.22 = (f32[96,512]{1,0:T(8,128)S(1)}, f32[96,512]{1,0:T(8,128)S(1)}, u32[]{:S(2)}, u32[]{:S(2)}) collective-permute-start(f32[96,512]{1,0:T(8,128)S(1)} %shard_map.94.refs_1_), channel_id=1, source_target_pairs={{0,1},{1,0},{2,3},{3,2},{4,5},{5,4},{6,7},{7,6},{8,9},{9,8},{10,11... | collective-permute-start | bytes 589832 | tf_op jit(solution)/shard_map/ppermute | solution.py:30
  70.9 1.4 %collective-permute-start.21 = (f32[96,512]{1,0:T(8,128)S(1)}, f32[96,512]{1,0:T(8,128)S(1)}, u32[]{:S(2)}, u32[]{:S(2)}) collective-permute-start(f32[96,512]{1,0:T(8,128)S(1)} %shard_map.93.refs_0_), channel_id=1, source_target_pairs={{0,1},{1,0},{2,3},{3,2},{4,5},{5,4},{6,7},{7,6},{8,9},{9,8},{10,11... | collective-permute-start | bytes 589832 | tf_op jit(solution)/shard_map/ppermute | solution.py:30
  70.9 2.2 %collective-permute-start.28 = (f32[96,512]{1,0:T(8,128)S(1)}, f32[96,512]{1,0:T(8,128)S(1)}, u32[]{:S(2)}, u32[]{:S(2)}) collective-permute-start(f32[96,512]{1,0:T(8,128)S(1)} %collective-permute-done.25.refs_7_), channel_id=1, source_target_pairs={{0,1},{1,0},{2,3},{3,2},{4,5},{5,4},{6,7},{7,6},{8,9},{9,8},{10,11... | collective-permute-start | bytes 589832 | tf_op jit(solution)/shard_map/ppermute | solution.py:30
  71.4 1.7 %collective-permute-start.27 = (f32[96,512]{1,0:T(8,128)S(1)}, f32[96,512]{1,0:T(8,128)S(1)}, u32[]{:S(2)}, u32[]{:S(2)}) collective-permute-start(f32[96,512]{1,0:T(8,128)S(1)} %collective-permute-done.24.refs_6_), channel_id=1, source_target_pairs={{0,1},{1,0},{2,3},{3,2},{4,5},{5,4},{6,7},{7,6},{8,9},{9,8},{10,11... | collective-permute-start | bytes 589832 | tf_op jit(solution)/shard_map/ppermute | solution.py:30
  71.5 1.6 %collective-permute-start.29 = (f32[64,512]{1,0:T(8,128)S(1)}, f32[64,512]{1,0:T(8,128)S(1)}, u32[]{:S(2)}, u32[]{:S(2)}) collective-permute-start(f32[64,512]{1,0:T(8,128)S(1)} %collective-permute-done.26.refs_8_), channel_id=1, source_target_pairs={{0,1},{1,0},{2,3},{3,2},{4,5},{5,4},{6,7},{7,6},{8,9},{9,8},{10,11... | collective-permute-start | bytes 393224 | tf_op jit(solution)/shard_map/ppermute | solution.py:30
  74.6 7.3 %collective-permute-start.30 = (f32[72,256]{1,0:T(8,128)S(1)}, f32[72,256]{1,0:T(8,128)S(1)}, u32[]{:S(2)}, u32[]{:S(2)}) collective-permute-start(f32[72,256]{1,0:T(8,128)S(1)} %get-tuple-element.29.send_ref), channel_id=1, source_target_pairs={{0,4},{1,5},{2,6},{3,7},{4,0},{5,1},{6,2},{7,3},{8,12},{9,13},{10,... | collective-permute-start | bytes 221192 | tf_op jit(solution)/shard_map/ppermute | solution.py:30

commit v5 on v4

--- a/solution.py
+++ b/solution.py
@@ -262,63 +262,109 @@
     return mul(ah, bh, last) + (mul(ah, bl, last) + mul(al, bh, last))
 
 
-def fold_pair_kernel(own_ref, other_ref, out_ref, *parts):
+def fold_half(flip, own_ref, other_ref, half_ref):
     core = lax.axis_index("cuts")
-    odd = (lax.axis_index("tile") >> 1) & 1
+    side = (lax.axis_index("tile") >> 2) & 1
+    size = half_ref.shape[0]
+    for k in range(2):
+        left, right = (own_ref, other_ref) if k else (other_ref, own_ref)
+        at = slice((k ^ flip) * size, ((k ^ flip) + 1) * size)
+
+        @pl.when((core == k) & (side == 0))
+        def _(left=left, right=right, at=at):
+            half_ref[...] = product(left[at, :], right[...])
+
+        @pl.when((core == k) & (side == 1))
+        def _(left=left, right=right, at=at):
+            half_ref[...] = jnp.transpose(product(left[...], right[:, at]))
+
+
+def fold_own_kernel(own_ref, other_ref, high_ref, low_ref, *refs):
+    half_ref, parts = refs[-1], refs[:-1]
+    fold_half(0, own_ref, other_ref, half_ref)
+    start = 0
+    for part in parts:
+        part[...] = half_ref[start : start + part.shape[0], :]
+        start += part.shape[0]
+    high_ref[...], low_ref[...] = split2(half_ref[...])
+
+
+def fold_rest_kernel(own_ref, other_ref, high_ref, low_ref, half_ref):
+    fold_half(1, own_ref, other_ref, half_ref)
+    high_ref[...], low_ref[...] = split2(half_ref[...])
+
+
+def fold_kernel(near_ref, high_ref, low_ref, rest_high_ref, rest_low_ref, out_ref):
+    core = lax.axis_index("cuts")
+    size = high_ref.shape[0]
+    total = None
+    for at, high, low in ((core, high_ref, low_ref), (1 - core, rest_high_ref, rest_low_ref)):
+        ah, al = split2(near_ref[:, pl.ds(pl.multiple_of(at * size, 128), size)])
+        part = mul(ah, high[...]) + (mul(ah, low[...]) + mul(al, high[...]))
+        total = part if total is None else total + part
+    out_ref[...] = total
+
+
+def fold_wide_kernel(*refs):
+    out_ref, groups = refs[-1], refs[0]
+    at, used = 0, 1
+    for count in groups:
+        near, pieces = refs[used][...], refs[used + 1 : used + 1 + count]
+        rows = jnp.concatenate([piece[...] for piece in pieces], axis=0)
+        out_ref[:, at : at + rows.shape[0]] = product_nt(near, rows)
+        at += rows.shape[0]
+        used += 1 + count
+
+
+def gather_pieces(mine, ref, pieces):
+    first, second, third = pieces
+    size = ref.shape[0] // 2
+    long = first.shape[0]
+    body = 2 * long
+    tail = size - body
+    own, other = mine * size, (1 - mine) * size
+    at = own
+    for piece, low, high in ((first, second, 4 * long + 2 * tail), (second, second, 4 * long), (third, third, 4 * long)):
+        rows = slice(at, at + piece.shape[0])
+        ref[rows, own : own + body] = piece[:, 0:body]
+        ref[rows, other : other + body] = piece[:, body : 2 * body]
+        ref[rows, own + body : own + size] = low[:, high : high + tail]
+        ref[rows, other + body : other + size] = low[:, high + tail : high + 2 * tail]
+        at += piece.shape[0]
+
+
+def gather_both(near, far, ref):
+    core = lax.axis_index("cuts")
     for k in range(2):
 
         @pl.when(core == k)
         def _(k=k):
-            left, right = (own_ref, other_ref) if k else (other_ref, own_ref)
-            out_ref[...] = product(left[...], right[...])
-
-    @pl.when(odd == 1)
-    def _():
-        out_ref[...] = jnp.transpose(out_ref[...])
-
-    start = core * (out_ref.shape[0] // 2)
-    for part in parts:
-        rows = part.shape[0]
-        part[...] = out_ref[pl.ds(pl.multiple_of(start, 8), rows), :]
-        start = start + rows
-
-
-def fold_kernel(near_ref, own_ref, out_ref):
-    out_ref[...] = product_nt(near_ref[...], own_ref[...])
-
-
-def fold_wide_kernel(near_ref, *refs):
-    out_ref, pieces = refs[-1], refs[:-1]
-    core = lax.axis_index("cuts")
-    half = len(pieces) // 2
-    size = out_ref.shape[1] // 2
-    near = near_ref[...]
-    for at, group in ((core, pieces[:half]), (1 - core, pieces[half:])):
-        rows = jnp.concatenate([piece[...] for piece in group], axis=0)
-        out_ref[:, pl.ds(pl.multiple_of(at * size, 128), size)] = product_nt(near, rows)
+            gather_pieces(k, ref, near)
+            gather_pieces(1 - k, ref, far)
+
+
+def fold_ready_kernel(count, *refs):
+    near, far, (high_ref, low_ref, own_ref) = refs[:count], refs[count : 2 * count], refs[2 * count :]
+    gather_both(near, far, own_ref)
+    high_ref[...], low_ref[...] = split2(own_ref[...])
 
 
 def fold_last_kernel(count, *refs):
-    own, own_far = refs[:count], refs[count : 2 * count]
-    got, got_far = refs[2 * count : 3 * count], refs[3 * count : 4 * count]
-    block_ref, send_ref, own_ref, got_ref, whole_ref = refs[4 * count :]
+    high_ref, low_ref, *refs = refs
+    block_ref, send_ref, got_ref, whole_ref = refs[2 * count :]
+    gather_both(refs[:count], refs[count : 2 * count], got_ref)
     core, tile = lax.axis_index("cuts"), lax.axis_index("tile")
     side, column, group = (tile >> 2) & 1, tile & 1, tile >> 1
-    for ref, near, far in ((own_ref, own, own_far), (got_ref, got, got_far)):
-        for at, part in ((core, near), (1 - core, far)):
-            start = at * (ref.shape[0] // 2)
-            for piece in part:
-                rows = piece.shape[0]
-                ref[pl.ds(pl.multiple_of(start, 8), rows), :] = piece[...]
-                start = start + rows
 
     @pl.when(side == column)
     def _():
-        whole_ref[...] = product(own_ref[...], got_ref[...])
+        gh, gl = split2(got_ref[...])
+        whole_ref[...] = mul(high_ref[...], gh) + (mul(high_ref[...], gl) + mul(low_ref[...], gh))
 
     @pl.when(side != column)
     def _():
-        whole_ref[...] = product(got_ref[...], own_ref[...])
+        gh, gl = split2(got_ref[...])
+        whole_ref[...] = mul(gh, high_ref[...]) + (mul(gl, high_ref[...]) + mul(gh, low_ref[...]))
 
     whole = whole_ref[...]
     square = jnp.sum(jnp.sum(whole * whole, axis=0, keepdims=True), axis=1, keepdims=True)
@@ -431,33 +477,49 @@
     count = len(sizes)
     cost = 6 * width**2
     pieces = [like(rows, width) for rows in sizes]
-    own, *parts = call(
-        fold_pair_kernel, [like(width, width)] + pieces, (leaf, moved(leaf, other_core)), flops=cost * width
-    )
+    half = jax.ShapeDtypeStruct((width // 2, width), BF)
+    scratch = [pltpu.VMEM((width // 2, width), F32)]
+    other = moved(leaf, other_core)
+    high, low, *parts = call(
+        fold_own_kernel, [half, half] + pieces, (leaf, other), scratch=scratch, flops=cost * width // 2
+    )
+    rest = call(fold_rest_kernel, [half, half], (leaf, other), scratch=scratch, flops=cost * width // 2)
     near = [moved(part, across(1)) for part in parts]
     first, first_far, got = [], [], []
     for p in range(count):
-        (done,) = call(fold_kernel, [pieces[p]], (near[p], own), flops=cost * sizes[p])
+        (done,) = call(fold_kernel, [pieces[p]], (near[p], high, low, *rest), flops=cost * sizes[p])
         first.append(done)
         got.append(moved(done, center))
         first_far.append(moved(done, other_core))
-    mine, mine_far, theirs, theirs_far = [], [], [], []
-    for p in range(count):
-        (done,) = call(fold_wide_kernel, [pieces[p]], (got[p], *first, *first_far), flops=cost * sizes[p])
+    mine, mine_far, theirs = [], [], []
+    long, last = first[:2] + first_far[:2], [first[2], first_far[2]]
+    for p, groups in enumerate(([(0, long)], [(1, long + last), (0, last)], [(2, long + last)])):
+        columns = [sum(piece.shape[0] for piece in pieces_in) for _, pieces_in in groups]
+        args = [x for q, pieces_in in groups for x in (got[q], *pieces_in)]
+        kernel = functools.partial(fold_wide_kernel, [len(pieces_in) for _, pieces_in in groups])
+        (done,) = call(kernel, [like(sizes[p], sum(columns))], args, flops=6 * width * sizes[p] * sum(columns))
         mine.append(done)
         theirs.append(moved(done, across(0)))
         mine_far.append(moved(done, other_core))
     theirs_far = [moved(part, other_core) for part in theirs]
-    high, cols = width // tiles, width // 2
+    tall, cols = width // tiles, width // 2
+    split = jax.ShapeDtypeStruct((width, width), BF)
+    own = call(
+        functools.partial(fold_ready_kernel, count),
+        [split, split],
+        (*mine, *mine_far),
+        scratch=[pltpu.VMEM((width, width), F32)],
+        flops=width * width,
+    )
     block, send = call(
         functools.partial(fold_last_kernel, count),
-        [like(high, cols), like(high + PAD, cols)],
-        (*mine, *mine_far, *theirs, *theirs_far),
-        scratch=[pltpu.VMEM((width, width), F32)] * 3,
+        [like(tall, cols), like(tall + PAD, cols)],
+        (*own, *theirs, *theirs_far),
+        scratch=[pltpu.VMEM((width, width), F32)] * 2,
         flops=cost * width,
     )
     out, log = call(
-        choose_kernel, [like(high, cols), like(1, 1)], (block, send, moved(send, across(1))), kept=False
+        choose_kernel, [like(tall, cols), like(1, 1)], (block, send, moved(send, across(1))), kept=False
     )
     return out, log.reshape(1)
 

time: 82.7 us -> 85.5 us (1.034)
  starting transfers between devices: 25.9 us -> 29.3 us
  waiting for transfers between devices: 44.8 us -> 43.9 us
    ppermute x31, starting transfers between devices: 25.9 us -> 29.3 us  [moved(): lax.ppermute(x, AXES, pairs(lax.axis_size('groups'), lax.axis_size('tile'...]
    ppermute x31, waiting for transfers between devices: 44.8 us -> 43.9 us  [moved(): lax.ppermute(x, AXES, pairs(lax.axis_size('groups'), lax.axis_size('tile'...]
    pallas_call x12 -> x14, Pallas kernels: 11 us -> 11.3 us  [call(): pl.pallas_call(kernel, out_shape=tuple((pltpu.VMEM(o.shape, o.dtype) if k...]
  transfers between devices with their start and end apart: 31 -> 31, of which waited for: 13 -> 14; matrix products, arithmetic and copies ran while one was open for 0% -> 0% of each run, Pallas kernels for 8% -> 8%
where the time goes in v5:
time: 85.5 us; the launch traced here: 85.3 us
  waiting for transfers between devices  43.9 us (51%)
  starting transfers between devices  29.3 us (34%)
  Pallas kernels  11.3 us (13%)
    ppermute x31, waiting for transfers between devices, moved(): lax.ppermute(x, AXES, pairs(lax.axis_size('groups'), lax.axis_size('tile'...  43.9 us
    ppermute x31, starting transfers between devices, moved(): lax.ppermute(x, AXES, pairs(lax.axis_size('groups'), lax.axis_size('tile'...  29.3 us
    pallas_call x14, Pallas kernels, call(): pl.pallas_call(kernel, out_shape=tuple((pltpu.VMEM(o.shape, o.dtype) if k...  11.3 us
  transfers between devices with their start and end apart: 31, of which 14 were waited for; matrix products, arithmetic and copies ran while one was open for 0% of the time, Pallas kernels for 8%

profile of v5, /device:TPU:0, one launch (start us, length us, event | category | flops | bytes accessed | tf_op | source)
XLA Modules:
  0.0 85.3 jit_solution(9149355476227496648)
XLA Ops:
  0.6 2.5 %collective-permute-start.10 = (f32[512,512]{1,0:T(8,128)}, f32[512,512]{1,0:T(8,128)S(1)}, u32[]{:S(2)}, u32[]{:S(2)}) collective-permute-start(f32[512,512]{1,0:T(8,128)} %refs_8_.1), channel_id=1, source_target_pairs={{0,3},{1,17},{2,18},{3,0},{4,7},{5,21},{6,22},{7,4},{8,11},{9,25},... | collective-permute-start | bytes 3145736 | tf_op jit(solution)/shard_map/ppermute | solution.py:30
  3.1 1.9 %shard_map.86 = (f32[392,128]{1,0:T(8,128)S(1)}, f32[392,128]{1,0:T(8,128)S(1)}, f32[392,128]{1,0:T(8,128)S(1)}, f32[392,128]{1,0:T(8,128)S(1)}) custom-call(f32[256,512]{1,0:T(8,128)} %rows_ref.1, s32[1,256]{1,0:T(1,128)} %bitcast.4, s32[1,256]{1,0:T(1,128)} %bitcast.5, s32[1,256]{1,0:T(1,128)} %bitcast.6, s32[1,512]{1,0:T(1,128)} %order_ref.1, ...), custom_call_target="tpu_custom_call" | custom-call | flops 301989888 | bytes 1334272 | tf_op jit(solution)/shard_map/pallas_call | solution.py:96
  5.0 0.1 collective-permute-start.4
  5.1 4.7 %collective-permute-start.7 = (f32[392,128]{1,0:T(8,128)S(1)}, f32[392,128]{1,0:T(8,128)S(1)}, u32[]{:S(2)}, u32[]{:S(2)}) collective-permute-start(f32[392,128]{1,0:T(8,128)S(1)} %get-tuple-element.25.refs_4_), channel_id=1, source_target_pairs={{0,15},{1,13},{2,14},{3,12},{4,7},{5,21},{6,22},{7,4},{8,11},{9,25... | collective-permute-start | bytes 602120 | tf_op jit(solution)/shard_map/ppermute | solution.py:30
  9.8 0.0 collective-permute-start.5
  9.8 0.5 collective-permute-start.8
  10.4 9.8 %collective-permute-done.4.refs_1_ = f32[392,128]{1,0:T(8,128)S(1)} collective-permute-done((f32[392,128]{1,0:T(8,128)S(1)}, f32[392,128]{1,0:T(8,128)S(1)}, u32[]{:S(2)}, u32[]{:S(2)}) %collective-permute-start.4) | collective-permute-done | bytes 200736 | tf_op jit(solution)/shard_map/ppermute | solution.py:30
  20.1 0.0 collective-permute-done.7.refs_5_
  20.1 3.8 %collective-permute-start.1 = (f32[392,128]{1,0:T(8,128)S(1)}, f32[392,128]{1,0:T(8,128)S(1)}, u32[]{:S(2)}, u32[]{:S(2)}) collective-permute-start(f32[392,128]{1,0:T(8,128)S(1)} %get-tuple-element.23), channel_id=1, source_target_pairs={{0,11},{1,9},{2,10},{3,8},{4,3},{5,1},{6,2},{7,0},{8,15},{9,13},{1... | collective-permute-start | bytes 602120 | tf_op jit(solution)/shard_map/ppermute | solution.py:30
  23.9 0.0 collective-permute-done.5.refs_2_
  23.9 0.0 collective-permute-start.6
  23.9 0.0 collective-permute-done.8.refs_6_
  23.9 0.5 collective-permute-start.9
  24.4 4.8 %collective-permute-done.refs_0_ = f32[392,128]{1,0:T(8,128)S(1)} collective-permute-done((f32[392,128]{1,0:T(8,128)S(1)}, f32[392,128]{1,0:T(8,128)S(1)}, u32[]{:S(2)}, u32[]{:S(2)}) %collective-permute-start) | collective-permute-done | bytes 200736 | tf_op jit(solution)/shard_map/ppermute | solution.py:30
  29.2 0.0 collective-permute-start.2
  29.2 4.2 %collective-permute-done.1.refs_1_ = f32[392,128]{1,0:T(8,128)S(1)} collective-permute-done((f32[392,128]{1,0:T(8,128)S(1)}, f32[392,128]{1,0:T(8,128)S(1)}, u32[]{:S(2)}, u32[]{:S(2)}) %collective-permute-start.1) | collective-permute-done | bytes 200736 | tf_op jit(solution)/shard_map/ppermute | solution.py:30
  33.3 0.0 collective-permute-start.3
  33.3 0.0 collective-permute-done.6.refs_3_
  33.3 0.0 collective-permute-done.9.refs_7_
  33.4 1.2 %shard_map.87 = (f32[512,512]{1,0:T(8,128)S(1)}, bf16[512,512]{1,0:T(8,128)(2,1)S(1)}, bf16[512,512]{1,0:T(8,128)(2,1)S(1)}) custom-call(f32[392,128]{1,0:T(8,128)S(1)} %get-tuple-element.24.refs_0_, f32[392,128]{1,0:T(8,128)S(1)} %collective-permute-done.4.refs_1_, f32[392,128]{1,0:T(8,128)S(1)} %collective-permute-done.5.refs_2_, ...), custom_call_target="tpu_custom_call" | custom-call | flops 671088640 | bytes 6848512 | tf_op jit(solution)/shard_map/pallas_call | solution.py:96
  34.6 0.2 collective-permute-done.3.refs_3_
  34.8 1.0 %shard_map.88.own_ref = f32[512,512]{1,0:T(8,128)S(1)} custom-call(f32[392,128]{1,0:T(8,128)S(1)} %collective-permute-done.refs_0_, f32[392,128]{1,0:T(8,128)S(1)} %collective-permute-done.1.refs_1_, f32[392,128]{1,0:T(8,128)S(1)} %collective-permute-done.2.refs_2_, f32[392,128]{1,0:T(8,128)S(1)} %collective-permute-done.3.refs_3_, ...), custom_call_target="tpu_custom_call" | custom-call | flops 671088640 | bytes 4997120 | tf_op jit(solution)/shard_map/pallas_call | solution.py:96
  35.8 0.4 collective-permute-start.11
  36.2 2.3 %collective-permute-done.11.other_ref = f32[512,512]{1,0:T(8,128)S(1)} collective-permute-done((f32[512,512]{1,0:T(8,128)S(1)}, f32[512,512]{1,0:T(8,128)S(1)}, u32[]{:S(2)}, u32[]{:S(2)}) %collective-permute-start.11) | collective-permute-done | bytes 1048608 | tf_op jit(solution)/shard_map/ppermute | solution.py:30
  38.6 0.7 shard_map.89
  39.3 1.3 %collective-permute-start.14 = (f32[96,512]{1,0:T(8,128)S(1)}, f32[96,512]{1,0:T(8,128)S(1)}, u32[]{:S(2)}, u32[]{:S(2)}) collective-permute-start(f32[96,512]{1,0:T(8,128)S(1)} %get-tuple-element.34), channel_id=1, source_target_pairs={{0,4},{1,5},{2,6},{3,7},{4,0},{5,1},{6,2},{7,3},{8,12},{9,13},{10,... | collective-permute-start | bytes 589832 | tf_op jit(solution)/shard_map/ppermute | solution.py:30
  40.6 0.8 collective-permute-start.12
  41.4 1.2 %collective-permute-start.18 = (f32[64,512]{1,0:T(8,128)S(1)}, f32[64,512]{1,0:T(8,128)S(1)}, u32[]{:S(2)}, u32[]{:S(2)}) collective-permute-start(f32[64,512]{1,0:T(8,128)S(1)} %get-tuple-element.35), channel_id=1, source_target_pairs={{0,4},{1,5},{2,6},{3,7},{4,0},{5,1},{6,2},{7,3},{8,12},{9,13},{10,... | collective-permute-start | bytes 393224 | tf_op jit(solution)/shard_map/ppermute | solution.py:30
  42.6 0.7 shard_map.90
  43.3 3.8 %collective-permute-done.14.near_ref = f32[96,512]{1,0:T(8,128)S(1)} collective-permute-done((f32[96,512]{1,0:T(8,128)S(1)}, f32[96,512]{1,0:T(8,128)S(1)}, u32[]{:S(2)}, u32[]{:S(2)}) %collective-permute-start.14) | collective-permute-done | bytes 196640 | tf_op jit(solution)/shard_map/ppermute | solution.py:30
  47.1 0.4 shard_map.92.refs_2_
  47.5 0.1 collective-permute-start.16
  47.6 3.8 %collective-permute-done.12.near_ref = f32[96,512]{1,0:T(8,128)S(1)} collective-permute-done((f32[96,512]{1,0:T(8,128)S(1)}, f32[96,512]{1,0:T(8,128)S(1)}, u32[]{:S(2)}, u32[]{:S(2)}) %collective-permute-start.12) | collective-permute-done | bytes 196640 | tf_op jit(solution)/shard_map/ppermute | solution.py:30
  51.4 0.4 shard_map.91.refs_1_
  51.7 0.1 collective-permute-start.15
  51.8 0.5 collective-permute-start.17
  52.3 0.1 collective-permute-start.13
  52.4 1.1 %collective-permute-done.18.near_ref = f32[64,512]{1,0:T(8,128)S(1)} collective-permute-done((f32[64,512]{1,0:T(8,128)S(1)}, f32[64,512]{1,0:T(8,128)S(1)}, u32[]{:S(2)}, u32[]{:S(2)}) %collective-permute-start.18) | collective-permute-done | bytes 131104 | tf_op jit(solution)/shard_map/ppermute | solution.py:30
  53.5 0.4 shard_map.94.refs_5_.refs_8_
  53.9 0.1 collective-permute-start.19
  54.0 1.3 %collective-permute-done.19.refs_6_.refs_9_ = f32[64,512]{1,0:T(8,128)S(1)} collective-permute-done((f32[64,512]{1,0:T(8,128)S(1)}, f32[64,512]{1,0:T(8,128)S(1)}, u32[]{:S(2)}, u32[]{:S(2)}) %collective-permute-start.19) | collective-permute-done | bytes 131104 | tf_op jit(solution)/shard_map/ppermute | solution.py:30
  55.3 0.0 collective-permute-done.15.refs_3_
  55.3 0.0 collective-permute-done.17.refs_0_
  55.3 0.0 collective-permute-done.13.refs_0_.refs_7_
  55.3 0.7 shard_map.95.refs_1_
  56.1 0.5 collective-permute-start.25
  56.6 0.5 shard_map.93.refs_0_
  57.1 1.6 %collective-permute-start.24 = (f32[96,384]{1,0:T(8,128)S(1)}, f32[96,384]{1,0:T(8,128)S(1)}, u32[]{:S(2)}, u32[]{:S(2)}) collective-permute-start(f32[96,384]{1,0:T(8,128)S(1)} %shard_map.93.refs_0_), channel_id=1, source_target_pairs={{0,2},{1,3},{2,0},{3,1},{4,6},{5,7},{6,4},{7,5},{8,10},{9,11},{10,... | collective-permute-start | bytes 442376 | tf_op jit(solution)/shard_map/ppermute | solution.py:30
  58.7 0.6 shard_map.96.refs_2_
  59.3 0.3 collective-permute-start.23
  59.6 0.7 collective-permute-start.26
  60.3 0.1 collective-permute-start.22
  60.4 4.6 %collective-permute-done.25.refs_3_ = f32[96,640]{1,0:T(8,128)S(1)} collective-permute-done((f32[96,640]{1,0:T(8,128)S(1)}, f32[96,640]{1,0:T(8,128)S(1)}, u32[]{:S(2)}, u32[]{:S(2)}) %collective-permute-start.25) | collective-permute-done | bytes 245792 | tf_op jit(solution)/shard_map/ppermute | solution.py:30
  65.0 0.0 collective-permute-start.28
  65.0 0.5 collective-permute-start.21
  65.5 2.6 %collective-permute-done.24.refs_2_ = f32[96,384]{1,0:T(8,128)S(1)} collective-permute-done((f32[96,384]{1,0:T(8,128)S(1)}, f32[96,384]{1,0:T(8,128)S(1)}, u32[]{:S(2)}, u32[]{:S(2)}) %collective-permute-start.24) | collective-permute-done | bytes 147488 | tf_op jit(solution)/shard_map/ppermute | solution.py:30
  68.1 0.0 collective-permute-start.27
  68.1 2.0 %collective-permute-done.26.refs_4_ = f32[64,512]{1,0:T(8,128)S(1)} collective-permute-done((f32[64,512]{1,0:T(8,128)S(1)}, f32[64,512]{1,0:T(8,128)S(1)}, u32[]{:S(2)}, u32[]{:S(2)}) %collective-permute-start.26) | collective-permute-done | bytes 131104 | tf_op jit(solution)/shard_map/ppermute | solution.py:30
  70.1 0.4 shard_map.97
  70.6 0.9 %collective-permute-done.29.refs_7_ = f32[64,512]{1,0:T(8,128)S(1)} collective-permute-done((f32[64,512]{1,0:T(8,128)S(1)}, f32[64,512]{1,0:T(8,128)S(1)}, u32[]{:S(2)}, u32[]{:S(2)}) %collective-permute-start.29) | collective-permute-done | bytes 131104 | tf_op jit(solution)/shard_map/ppermute | solution.py:30
  71.5 1.7 %shard_map.98 = (f32[64,256]{1,0:T(8,128)S(1)}, f32[72,256]{1,0:T(8,128)S(1)}) custom-call(bf16[512,512]{1,0:T(8,128)(2,1)S(1)} %get-tuple-element.36.refs_0_, bf16[512,512]{1,0:T(8,128)(2,1)S(1)} %get-tuple-element.37.refs_1_, f32[96,384]{1,0:T(8,128)S(1)} %collective-permute-done.24.refs_2_, f32[96,640]{1,0:T(8,128)S(1)} %collective-permute-done.25.refs_3_, ...), custom_call_target="tpu_custom_call" | custom-call | flops 805306368 | bytes 3284992 | tf_op jit(solution)/shard_map/pallas_call | solution.py:96
  73.1 8.9 %collective-permute-start.30 = (f32[72,256]{1,0:T(8,128)S(1)}, f32[72,256]{1,0:T(8,128)S(1)}, u32[]{:S(2)}, u32[]{:S(2)}) collective-permute-start(f32[72,256]{1,0:T(8,128)S(1)} %get-tuple-element.39.send_ref), channel_id=1, source_target_pairs={{0,4},{1,5},{2,6},{3,7},{4,0},{5,1},{6,2},{7,3},{8,12},{9,13},{10,... | collective-permute-start | bytes 221192 | tf_op jit(solution)/shard_map/ppermute | solution.py:30
  82.1 2.6 %collective-permute-done.30.got_ref = f32[72,256]{1,0:T(8,128)S(1)} collective-permute-done((f32[72,256]{1,0:T(8,128)S(1)}, f32[72,256]{1,0:T(8,128)S(1)}, u32[]{:S(2)}, u32[]{:S(2)}) %collective-permute-start.30) | collective-permute-done | bytes 73760 | tf_op jit(solution)/shard_map/ppermute | solution.py:30
  84.7 0.6 shard_map.99
  (14 shorter events, 0.0 us)
Async XLA Ops:
  0.6 32.7 %copy-start = (f32[512,512]{1,0:T(8,128)S(1)}, f32[512,512]{1,0:T(8,128)}, u32[]{:S(2)}) copy-start(f32[512,512]{1,0:T(8,128)} %refs_8_.1) | copy-start | bytes 3145732
  0.6 32.7 %collective-permute-start.10 = (f32[512,512]{1,0:T(8,128)}, f32[512,512]{1,0:T(8,128)S(1)}, u32[]{:S(2)}, u32[]{:S(2)}) collective-permute-start(f32[512,512]{1,0:T(8,128)} %refs_8_.1), channel_id=1, source_target_pairs={{0,3},{1,17},{2,18},{3,0},{4,7},{5,21},{6,22},{7,4},{8,11},{9,25},... | collective-permute-start | bytes 3145736 | tf_op jit(solution)/shard_map/ppermute | solution.py:30
  5.0 15.1 %collective-permute-start.4 = (f32[392,128]{1,0:T(8,128)S(1)}, f32[392,128]{1,0:T(8,128)S(1)}, u32[]{:S(2)}, u32[]{:S(2)}) collective-permute-start(f32[392,128]{1,0:T(8,128)S(1)} %get-tuple-element.24.refs_0_), channel_id=1, source_target_pairs={{0,3},{1,17},{2,18},{3,0},{4,11},{5,9},{6,10},{7,8},{8,7},{9,5},{1... | collective-permute-start | bytes 602120 | tf_op jit(solution)/shard_map/ppermute | solution.py:30
  5.1 15.0 %collective-permute-start.7 = (f32[392,128]{1,0:T(8,128)S(1)}, f32[392,128]{1,0:T(8,128)S(1)}, u32[]{:S(2)}, u32[]{:S(2)}) collective-permute-start(f32[392,128]{1,0:T(8,128)S(1)} %get-tuple-element.25.refs_4_), channel_id=1, source_target_pairs={{0,15},{1,13},{2,14},{3,12},{4,7},{5,21},{6,22},{7,4},{8,11},{9,25... | collective-permute-start | bytes 602120 | tf_op jit(solution)/shard_map/ppermute | solution.py:30
  9.8 14.0 %collective-permute-start.5 = (f32[392,128]{1,0:T(8,128)S(1)}, f32[392,128]{1,0:T(8,128)S(1)}, u32[]{:S(2)}, u32[]{:S(2)}) collective-permute-start(f32[392,128]{1,0:T(8,128)S(1)} %get-tuple-element.24.refs_0_), channel_id=1, source_target_pairs={{0,1},{1,0},{2,3},{3,2},{4,5},{5,4},{6,7},{7,6},{8,9},{9,8},{10,11... | collective-permute-start | bytes 602120 | tf_op jit(solution)/shard_map/ppermute | solution.py:30
  9.8 14.0 %collective-permute-start.8 = (f32[392,128]{1,0:T(8,128)S(1)}, f32[392,128]{1,0:T(8,128)S(1)}, u32[]{:S(2)}, u32[]{:S(2)}) collective-permute-start(f32[392,128]{1,0:T(8,128)S(1)} %get-tuple-element.25.refs_4_), channel_id=1, source_target_pairs={{0,1},{1,0},{2,3},{3,2},{4,5},{5,4},{6,7},{7,6},{8,9},{9,8},{10,11... | collective-permute-start | bytes 602120 | tf_op jit(solution)/shard_map/ppermute | solution.py:30
  20.1 9.0 %collective-permute-start = (f32[392,128]{1,0:T(8,128)S(1)}, f32[392,128]{1,0:T(8,128)S(1)}, u32[]{:S(2)}, u32[]{:S(2)}) collective-permute-start(f32[392,128]{1,0:T(8,128)S(1)} %get-tuple-element.22), channel_id=1, source_target_pairs={{0,7},{1,5},{2,6},{3,4},{4,15},{5,13},{6,14},{7,12},{8,3},{9,1},{1... | collective-permute-start | bytes 602120 | tf_op jit(solution)/shard_map/ppermute | solution.py:30
  20.1 13.2 %collective-permute-start.1 = (f32[392,128]{1,0:T(8,128)S(1)}, f32[392,128]{1,0:T(8,128)S(1)}, u32[]{:S(2)}, u32[]{:S(2)}) collective-permute-start(f32[392,128]{1,0:T(8,128)S(1)} %get-tuple-element.23), channel_id=1, source_target_pairs={{0,11},{1,9},{2,10},{3,8},{4,3},{5,1},{6,2},{7,0},{8,15},{9,13},{1... | collective-permute-start | bytes 602120 | tf_op jit(solution)/shard_map/ppermute | solution.py:30
  23.9 9.5 %collective-permute-start.6 = (f32[392,128]{1,0:T(8,128)S(1)}, f32[392,128]{1,0:T(8,128)S(1)}, u32[]{:S(2)}, u32[]{:S(2)}) collective-permute-start(f32[392,128]{1,0:T(8,128)S(1)} %collective-permute-done.4.refs_1_), channel_id=1, source_target_pairs={{0,1},{1,0},{2,3},{3,2},{4,5},{5,4},{6,7},{7,6},{8,9},{9,8},{10,11... | collective-permute-start | bytes 602120 | tf_op jit(solution)/shard_map/ppermute | solution.py:30
  23.9 9.5 %collective-permute-start.9 = (f32[392,128]{1,0:T(8,128)S(1)}, f32[392,128]{1,0:T(8,128)S(1)}, u32[]{:S(2)}, u32[]{:S(2)}) collective-permute-start(f32[392,128]{1,0:T(8,128)S(1)} %collective-permute-done.7.refs_5_), channel_id=1, source_target_pairs={{0,1},{1,0},{2,3},{3,2},{4,5},{5,4},{6,7},{7,6},{8,9},{9,8},{10,11... | collective-permute-start | bytes 602120 | tf_op jit(solution)/shard_map/ppermute | solution.py:30
  29.2 5.4 %collective-permute-start.2 = (f32[392,128]{1,0:T(8,128)S(1)}, f32[392,128]{1,0:T(8,128)S(1)}, u32[]{:S(2)}, u32[]{:S(2)}) collective-permute-start(f32[392,128]{1,0:T(8,128)S(1)} %collective-permute-done.refs_0_), channel_id=1, source_target_pairs={{0,1},{1,0},{2,3},{3,2},{4,5},{5,4},{6,7},{7,6},{8,9},{9,8},{10,11... | collective-permute-start | bytes 602120 | tf_op jit(solution)/shard_map/ppermute | solution.py:30
  33.3 1.4 %collective-permute-start.3 = (f32[392,128]{1,0:T(8,128)S(1)}, f32[392,128]{1,0:T(8,128)S(1)}, u32[]{:S(2)}, u32[]{:S(2)}) collective-permute-start(f32[392,128]{1,0:T(8,128)S(1)} %collective-permute-done.1.refs_1_), channel_id=1, source_target_pairs={{0,1},{1,0},{2,3},{3,2},{4,5},{5,4},{6,7},{7,6},{8,9},{9,8},{10,11... | collective-permute-start | bytes 602120 | tf_op jit(solution)/shard_map/ppermute | solution.py:30
  35.8 2.7 %collective-permute-start.11 = (f32[512,512]{1,0:T(8,128)S(1)}, f32[512,512]{1,0:T(8,128)S(1)}, u32[]{:S(2)}, u32[]{:S(2)}) collective-permute-start(f32[512,512]{1,0:T(8,128)S(1)} %shard_map.88.own_ref), channel_id=1, source_target_pairs={{0,1},{1,0},{2,3},{3,2},{4,5},{5,4},{6,7},{7,6},{8,9},{9,8},{10,11... | collective-permute-start | bytes 3145736 | tf_op jit(solution)/shard_map/ppermute | solution.py:30
  39.3 7.8 %collective-permute-start.14 = (f32[96,512]{1,0:T(8,128)S(1)}, f32[96,512]{1,0:T(8,128)S(1)}, u32[]{:S(2)}, u32[]{:S(2)}) collective-permute-start(f32[96,512]{1,0:T(8,128)S(1)} %get-tuple-element.34), channel_id=1, source_target_pairs={{0,4},{1,5},{2,6},{3,7},{4,0},{5,1},{6,2},{7,3},{8,12},{9,13},{10,... | collective-permute-start | bytes 589832 | tf_op jit(solution)/shard_map/ppermute | solution.py:30
  40.6 10.7 %collective-permute-start.12 = (f32[96,512]{1,0:T(8,128)S(1)}, f32[96,512]{1,0:T(8,128)S(1)}, u32[]{:S(2)}, u32[]{:S(2)}) collective-permute-start(f32[96,512]{1,0:T(8,128)S(1)} %get-tuple-element.29), channel_id=1, source_target_pairs={{0,4},{1,5},{2,6},{3,7},{4,0},{5,1},{6,2},{7,3},{8,12},{9,13},{10,... | collective-permute-start | bytes 589832 | tf_op jit(solution)/shard_map/ppermute | solution.py:30
  41.4 12.1 %collective-permute-start.18 = (f32[64,512]{1,0:T(8,128)S(1)}, f32[64,512]{1,0:T(8,128)S(1)}, u32[]{:S(2)}, u32[]{:S(2)}) collective-permute-start(f32[64,512]{1,0:T(8,128)S(1)} %get-tuple-element.35), channel_id=1, source_target_pairs={{0,4},{1,5},{2,6},{3,7},{4,0},{5,1},{6,2},{7,3},{8,12},{9,13},{10,... | collective-permute-start | bytes 393224 | tf_op jit(solution)/shard_map/ppermute | solution.py:30
  47.5 7.8 %collective-permute-start.16 = (f32[96,512]{1,0:T(8,128)S(1)}, f32[96,512]{1,0:T(8,128)S(1)}, u32[]{:S(2)}, u32[]{:S(2)}) collective-permute-start(f32[96,512]{1,0:T(8,128)S(1)} %shard_map.92.refs_2_), channel_id=1, source_target_pairs={{0,1},{1,0},{2,3},{3,2},{4,5},{5,4},{6,7},{7,6},{8,9},{9,8},{10,11... | collective-permute-start | bytes 589832 | tf_op jit(solution)/shard_map/ppermute | solution.py:30
  51.7 3.6 %collective-permute-start.15 = (f32[96,512]{1,0:T(8,128)S(1)}, f32[96,512]{1,0:T(8,128)S(1)}, u32[]{:S(2)}, u32[]{:S(2)}) collective-permute-start(f32[96,512]{1,0:T(8,128)S(1)} %shard_map.91.refs_1_), channel_id=1, source_target_pairs={{0,1},{1,0},{2,3},{3,2},{4,5},{5,4},{6,7},{7,6},{8,9},{9,8},{10,11... | collective-permute-start | bytes 589832 | tf_op jit(solution)/shard_map/ppermute | solution.py:30
  51.8 3.5 %collective-permute-start.17 = (f32[96,512]{1,0:T(8,128)S(1)}, f32[96,512]{1,0:T(8,128)S(1)}, u32[]{:S(2)}, u32[]{:S(2)}) collective-permute-start(f32[96,512]{1,0:T(8,128)S(1)} %shard_map.92.refs_2_), channel_id=1, source_target_pairs={{0,1},{1,0},{2,3},{3,2},{4,8},{5,9},{6,10},{7,11},{8,4},{9,5},{10,... | collective-permute-start | bytes 589832 | tf_op jit(solution)/shard_map/ppermute | solution.py:30
  52.3 3.0 %collective-permute-start.13 = (f32[96,512]{1,0:T(8,128)S(1)}, f32[96,512]{1,0:T(8,128)S(1)}, u32[]{:S(2)}, u32[]{:S(2)}) collective-permute-start(f32[96,512]{1,0:T(8,128)S(1)} %shard_map.91.refs_1_), channel_id=1, source_target_pairs={{0,1},{1,0},{2,3},{3,2},{4,8},{5,9},{6,10},{7,11},{8,4},{9,5},{10,... | collective-permute-start | bytes 589832 | tf_op jit(solution)/shard_map/ppermute | solution.py:30
  53.9 1.4 %collective-permute-start.19 = (f32[64,512]{1,0:T(8,128)S(1)}, f32[64,512]{1,0:T(8,128)S(1)}, u32[]{:S(2)}, u32[]{:S(2)}) collective-permute-start(f32[64,512]{1,0:T(8,128)S(1)} %shard_map.94.refs_5_.refs_8_), channel_id=1, source_target_pairs={{0,1},{1,0},{2,3},{3,2},{4,5},{5,4},{6,7},{7,6},{8,9},{9,8},{10,11... | collective-permute-start | bytes 393224 | tf_op jit(solution)/shard_map/ppermute | solution.py:30
  56.1 8.9 %collective-permute-start.25 = (f32[96,640]{1,0:T(8,128)S(1)}, f32[96,640]{1,0:T(8,128)S(1)}, u32[]{:S(2)}, u32[]{:S(2)}) collective-permute-start(f32[96,640]{1,0:T(8,128)S(1)} %shard_map.95.refs_1_), channel_id=1, source_target_pairs={{0,2},{1,3},{2,0},{3,1},{4,6},{5,7},{6,4},{7,5},{8,10},{9,11},{10,... | collective-permute-start | bytes 737288 | tf_op jit(solution)/shard_map/ppermute | solution.py:30
  56.6 2.1 %collective-permute-start.20 = (f32[64,512]{1,0:T(8,128)S(1)}, f32[64,512]{1,0:T(8,128)S(1)}, u32[]{:S(2)}, u32[]{:S(2)}) collective-permute-start(f32[64,512]{1,0:T(8,128)S(1)} %shard_map.94.refs_5_.refs_8_), channel_id=1, source_target_pairs={{0,1},{1,0},{2,3},{3,2},{4,8},{5,9},{6,10},{7,11},{8,4},{9,5},{10,... | collective-permute-start | bytes 393224 | tf_op jit(solution)/shard_map/ppermute | solution.py:30
  57.1 11.0 %collective-permute-start.24 = (f32[96,384]{1,0:T(8,128)S(1)}, f32[96,384]{1,0:T(8,128)S(1)}, u32[]{:S(2)}, u32[]{:S(2)}) collective-permute-start(f32[96,384]{1,0:T(8,128)S(1)} %shard_map.93.refs_0_), channel_id=1, source_target_pairs={{0,2},{1,3},{2,0},{3,1},{4,6},{5,7},{6,4},{7,5},{8,10},{9,11},{10,... | collective-permute-start | bytes 442376 | tf_op jit(solution)/shard_map/ppermute | solution.py:30
  59.3 5.6 %collective-permute-start.23 = (f32[64,512]{1,0:T(8,128)S(1)}, f32[64,512]{1,0:T(8,128)S(1)}, u32[]{:S(2)}, u32[]{:S(2)}) collective-permute-start(f32[64,512]{1,0:T(8,128)S(1)} %shard_map.96.refs_2_), channel_id=1, source_target_pairs={{0,1},{1,0},{2,3},{3,2},{4,5},{5,4},{6,7},{7,6},{8,9},{9,8},{10,11... | collective-permute-start | bytes 393224 | tf_op jit(solution)/shard_map/ppermute | solution.py:30
  59.6 10.5 %collective-permute-start.26 = (f32[64,512]{1,0:T(8,128)S(1)}, f32[64,512]{1,0:T(8,128)S(1)}, u32[]{:S(2)}, u32[]{:S(2)}) collective-permute-start(f32[64,512]{1,0:T(8,128)S(1)} %shard_map.96.refs_2_), channel_id=1, source_target_pairs={{0,2},{1,3},{2,0},{3,1},{4,6},{5,7},{6,4},{7,5},{8,10},{9,11},{10,... | collective-permute-start | bytes 393224 | tf_op jit(solution)/shard_map/ppermute | solution.py:30
  60.3 9.8 %collective-permute-start.22 = (f32[96,640]{1,0:T(8,128)S(1)}, f32[96,640]{1,0:T(8,128)S(1)}, u32[]{:S(2)}, u32[]{:S(2)}) collective-permute-start(f32[96,640]{1,0:T(8,128)S(1)} %shard_map.95.refs_1_), channel_id=1, source_target_pairs={{0,1},{1,0},{2,3},{3,2},{4,5},{5,4},{6,7},{7,6},{8,9},{9,8},{10,11... | collective-permute-start | bytes 737288 | tf_op jit(solution)/shard_map/ppermute | solution.py:30
  65.0 6.5 %collective-permute-start.28 = (f32[96,640]{1,0:T(8,128)S(1)}, f32[96,640]{1,0:T(8,128)S(1)}, u32[]{:S(2)}, u32[]{:S(2)}) collective-permute-start(f32[96,640]{1,0:T(8,128)S(1)} %collective-permute-done.25.refs_3_), channel_id=1, source_target_pairs={{0,1},{1,0},{2,3},{3,2},{4,5},{5,4},{6,7},{7,6},{8,9},{9,8},{10,11... | collective-permute-start | bytes 737288 | tf_op jit(solution)/shard_map/ppermute | solution.py:30
  65.0 5.2 %collective-permute-start.21 = (f32[96,384]{1,0:T(8,128)S(1)}, f32[96,384]{1,0:T(8,128)S(1)}, u32[]{:S(2)}, u32[]{:S(2)}) collective-permute-start(f32[96,384]{1,0:T(8,128)S(1)} %shard_map.93.refs_0_), channel_id=1, source_target_pairs={{0,1},{1,0},{2,3},{3,2},{4,5},{5,4},{6,7},{7,6},{8,9},{9,8},{10,11... | collective-permute-start | bytes 442376 | tf_op jit(solution)/shard_map/ppermute | solution.py:30
  68.1 3.3 %collective-permute-start.27 = (f32[96,384]{1,0:T(8,128)S(1)}, f32[96,384]{1,0:T(8,128)S(1)}, u32[]{:S(2)}, u32[]{:S(2)}) collective-permute-start(f32[96,384]{1,0:T(8,128)S(1)} %collective-permute-done.24.refs_2_), channel_id=1, source_target_pairs={{0,1},{1,0},{2,3},{3,2},{4,5},{5,4},{6,7},{7,6},{8,9},{9,8},{10,11... | collective-permute-start | bytes 442376 | tf_op jit(solution)/shard_map/ppermute | solution.py:30
  70.1 1.3 %collective-permute-start.29 = (f32[64,512]{1,0:T(8,128)S(1)}, f32[64,512]{1,0:T(8,128)S(1)}, u32[]{:S(2)}, u32[]{:S(2)}) collective-permute-start(f32[64,512]{1,0:T(8,128)S(1)} %collective-permute-done.26.refs_4_), channel_id=1, source_target_pairs={{0,1},{1,0},{2,3},{3,2},{4,5},{5,4},{6,7},{7,6},{8,9},{9,8},{10,11... | collective-permute-start | bytes 393224 | tf_op jit(solution)/shard_map/ppermute | solution.py:30
  73.1 11.5 %collective-permute-start.30 = (f32[72,256]{1,0:T(8,128)S(1)}, f32[72,256]{1,0:T(8,128)S(1)}, u32[]{:S(2)}, u32[]{:S(2)}) collective-permute-start(f32[72,256]{1,0:T(8,128)S(1)} %get-tuple-element.39.send_ref), channel_id=1, source_target_pairs={{0,4},{1,5},{2,6},{3,7},{4,0},{5,1},{6,2},{7,3},{8,12},{9,13},{10,... | collective-permute-start | bytes 221192 | tf_op jit(solution)/shard_map/ppermute | solution.py:30

commit v6 on v5

--- a/solution.py
+++ b/solution.py
@@ -141,56 +141,58 @@
             out[last + 2 + j : last + 3 + j, :] = code[:, j * 128 : (j + 1) * 128]
 
 
-def spread_rows(cap, blocks, eh, el):
+def spread_rows(cap, half, blocks, eh, el):
     width = eh.shape[1]
     last = width // 128 * 2 * cap
     lane = lax.broadcasted_iota(jnp.int32, (1, 128), 1)
     targets = lax.broadcasted_iota(jnp.int32, (width, 128), 0) + 1
-    spread, chosen = [], []
-    for near, far in blocks:
-        columns = [
-            jnp.concatenate([near[at : at + cap, :], far[at + cap : at + 2 * cap, :]], axis=0)
-            for at in range(0, last, 2 * cap)
-        ]
-        bh, bl = split2(jnp.concatenate(columns, axis=1))
-        spread.append(mul(bh, eh) + (mul(bh, el) + mul(bl, eh)))
-        spread.append(jnp.zeros((128 - 2 * cap, width), F32))
-        digits = jnp.where(lane < cap, near[last : last + PAD, :], far[last : last + PAD, :])
-        to = (digits[0:1, :] * 16.0 + digits[1:2, :]).astype(jnp.int32)
-        to = jnp.where(lane < 2 * cap, to, 0)
-        chosen.append(jnp.where(targets == to, 1.0, 0.0).astype(BF))
-    sh, sl = split2(jnp.concatenate(spread, axis=0))
+    gap = jnp.zeros((64 - cap, width), F32)
+    rows, chosen = [], []
+    for first, second in zip(blocks[::2], blocks[1::2]):
+        for block in (first, second):
+            columns = [block[at + half * cap : at + (half + 1) * cap, :] for at in range(0, last, 2 * cap)]
+            rows += [jnp.concatenate(columns, axis=1), gap]
+        ends = [block[last : last + PAD, :] for block in (first, second)]
+        to = [(end[0:1, :] * 16.0 + end[1:2, :]).astype(jnp.int32) for end in ends]
+        at = [pltpu.roll(jnp.broadcast_to(t, (PAD, 128)), (j * 64 - half * cap) % 128, 1)[0:1, :] for j, t in enumerate(to)]
+        both = jnp.where(lane < 64, jnp.where(lane < cap, at[0], 0), jnp.where(lane < 64 + cap, at[1], 0))
+        chosen.append(jnp.where(targets == both, 1.0, 0.0).astype(BF))
+    rh, rl = split2(jnp.concatenate(rows, axis=0))
+    sh, sl = split2(mul(rh, eh) + (mul(rh, el) + mul(rl, eh)))
     pick = jnp.concatenate(chosen, axis=1)
     return mul(pick, sh) + mul(pick, sl)
 
 
 def early_leaf_kernel(cap, sets, *refs):
-    env_own_ref, env_got_ref, part_ref, high_ref, low_ref = refs[8:]
+    packed_first, packed_last, env_own_ref, env_got_ref, *refs = refs
+    near, (part_ref, high_ref, low_ref) = refs[:sets], refs[sets:]
     keep, inner = native(), is_inner(sets)
     eh, el = split2(jnp.where(keep, env_own_ref[...], env_got_ref[...]))
     high_ref[...] = eh
     low_ref[...] = el
-    blocks = []
-    for (own, got, far_own, far_got), stays in ((refs[:4], jnp.logical_not(inner)), (refs[4:8], inner)):
-        near = jnp.where(keep & stays, own[...], got[...])
-        far = jnp.where(jnp.logical_not(keep) & stays, far_own[...], far_got[...])
-        blocks.append((near, far))
+    blocks = [ref[...] for ref in near]
+    blocks[0] = jnp.where(keep & jnp.logical_not(inner), packed_first[...], blocks[0])
+    blocks[-1] = jnp.where(keep & inner, packed_last[...], blocks[-1])
     width = eh.shape[1]
     lanes = width // 128
     last = lanes * 2 * cap
-    code = jnp.transpose(jnp.where(inner, blocks[1][0][last : last + PAD, :], blocks[0][0][last : last + PAD, :]))
+    code = jnp.transpose(jnp.where(inner, blocks[-1][last : last + PAD, :], blocks[0][last : last + PAD, :]))
     column = jnp.concatenate([code[:, 2 + j : 3 + j] for j in range(lanes)], axis=0)
     bond = (jnp.abs(column) - 1.0).astype(jnp.int32)
     sign = jnp.where(column < 0.0, -1.0, 1.0)
     spots = lax.broadcasted_iota(jnp.int32, (width, width), 1)
     signed = jnp.where(spots == bond, sign, 0.0)
-    part_ref[...] = signed + spread_rows(cap, blocks, eh, el)
-
-
-def late_leaf_kernel(cap, count, *refs):
-    near, far = refs[:count], refs[count : 2 * count]
-    high_ref, low_ref, part_ref, leaf_ref = refs[2 * count :]
-    leaf_ref[...] = part_ref[...] + spread_rows(cap, list(zip(near, far)), high_ref[...], low_ref[...])
+    part_ref[...] = signed + spread_rows(cap, 0, blocks, eh, el)
+
+
+def late_leaf_kernel(cap, sets, *refs):
+    packed_first, packed_last, high_ref, low_ref, part_ref, *refs = refs
+    far, leaf_ref = refs[:sets], refs[sets]
+    drop, inner = jnp.logical_not(native()), is_inner(sets)
+    blocks = [ref[...] for ref in far]
+    blocks[0] = jnp.where(drop & jnp.logical_not(inner), packed_first[...], blocks[0])
+    blocks[-1] = jnp.where(drop & inner, packed_last[...], blocks[-1])
+    leaf_ref[...] = part_ref[...] + spread_rows(cap, 1, blocks, high_ref[...], low_ref[...])
 
 
 def half_of(core, value, half_ref):
@@ -437,15 +439,13 @@
     part, high, low = call(
         functools.partial(early_leaf_kernel, cap, sets),
         [like(width, width), split, split],
-        [x for m in ends for x in (outgoing[m], near[m], far_own[m], far[m])] + [environment, env],
+        (outgoing[0], outgoing[-1], environment, env, *near),
         flops=5 * width**3,
     )
-    if sets == 2:
-        return part
     (leaf,) = call(
-        functools.partial(late_leaf_kernel, cap, sets - 2),
+        functools.partial(late_leaf_kernel, cap, sets),
         [like(width, width)],
-        (*near[1:-1], *far[1:-1], high, low, part),
+        (far_own[0], far_own[sets - 1], high, low, part, *far),
         flops=5 * width**3,
     )
     return leaf
@@ -455,7 +455,7 @@
     tiles = lax.axis_size("tile")
     count, width = slice_rows.shape
     cap = max(2, (3 * count + 2 * tiles - 1) // (2 * tiles))
-    narrow = cap % 8 == 0 and 2 * cap <= 128 and tiles // 2 in (2, 4, 8) and width % 128 == 0 and width <= 768
+    narrow = cap % 8 == 0 and cap <= 64 and tiles // 2 in (2, 4, 8) and width % 128 == 0 and width <= 768
     make_leaf = packed_leaf if narrow else plain_leaf
     leaf = make_leaf(slice_rows, row_owner, leaf_row, exponent, environment, ordering, sign_mask, tiles, cap)
     if tiles == 8 and width % 512 == 0:

time: 85.5 us -> 78.7 us (0.920)
  waiting for transfers between devices: 43.9 us -> 37 us
    ppermute x31, waiting for transfers between devices: 43.9 us -> 37 us  [moved(): lax.ppermute(x, AXES, pairs(lax.axis_size('groups'), lax.axis_size('tile'...]
where the time goes in v6:
time: 78.7 us; the launch traced here: 78.5 us
  waiting for transfers between devices  37 us (47%)
  starting transfers between devices  29.5 us (37%)
  Pallas kernels  11.2 us (14%)
  between operations  0.81 us (1%)
    ppermute x31, waiting for transfers between devices, moved(): lax.ppermute(x, AXES, pairs(lax.axis_size('groups'), lax.axis_size('tile'...  37 us
    ppermute x31, starting transfers between devices, moved(): lax.ppermute(x, AXES, pairs(lax.axis_size('groups'), lax.axis_size('tile'...  29.5 us
    pallas_call x14, Pallas kernels, call(): pl.pallas_call(kernel, out_shape=tuple((pltpu.VMEM(o.shape, o.dtype) if k...  11.2 us
  transfers between devices with their start and end apart: 31, of which 14 were waited for; matrix products, arithmetic and copies ran while one was open for 0% of the time, Pallas kernels for 8%

profile of v6, /device:TPU:0, one launch (start us, length us, event | category | flops | bytes accessed | tf_op | source)
XLA Modules:
  0.0 78.5 jit_solution(5274627781183792268)
XLA Ops:
  0.6 2.5 %collective-permute-start.2 = (f32[512,512]{1,0:T(8,128)}, f32[512,512]{1,0:T(8,128)S(1)}, u32[]{:S(2)}, u32[]{:S(2)}) collective-permute-start(f32[512,512]{1,0:T(8,128)} %refs_2_.1), channel_id=1, source_target_pairs={{0,3},{1,17},{2,18},{3,0},{4,7},{5,21},{6,22},{7,4},{8,11},{9,25},... | collective-permute-start | bytes 3145736 | tf_op jit(solution)/shard_map/ppermute | solution.py:30
  3.1 1.9 %shard_map.86 = (f32[392,128]{1,0:T(8,128)S(1)}, f32[392,128]{1,0:T(8,128)S(1)}, f32[392,128]{1,0:T(8,128)S(1)}, f32[392,128]{1,0:T(8,128)S(1)}) custom-call(f32[256,512]{1,0:T(8,128)} %rows_ref.1, s32[1,256]{1,0:T(1,128)} %bitcast.4, s32[1,256]{1,0:T(1,128)} %bitcast.5, s32[1,256]{1,0:T(1,128)} %bitcast.6, s32[1,512]{1,0:T(1,128)} %order_ref.1, ...), custom_call_target="tpu_custom_call" | custom-call | flops 301989888 | bytes 1334272 | tf_op jit(solution)/shard_map/pallas_call | solution.py:96
  5.0 0.1 collective-permute-start.3
  5.1 4.7 %collective-permute-start.6 = (f32[392,128]{1,0:T(8,128)S(1)}, f32[392,128]{1,0:T(8,128)S(1)}, u32[]{:S(2)}, u32[]{:S(2)}) collective-permute-start(f32[392,128]{1,0:T(8,128)S(1)} %get-tuple-element.23.refs_1_), channel_id=1, source_target_pairs={{0,15},{1,13},{2,14},{3,12},{4,7},{5,21},{6,22},{7,4},{8,11},{9,25... | collective-permute-start | bytes 602120 | tf_op jit(solution)/shard_map/ppermute | solution.py:30
  9.8 0.0 collective-permute-start.4
  9.8 3.5 %collective-permute-start.5 = (f32[392,128]{1,0:T(8,128)S(1)}, f32[392,128]{1,0:T(8,128)S(1)}, u32[]{:S(2)}, u32[]{:S(2)}) collective-permute-start(f32[392,128]{1,0:T(8,128)S(1)} %get-tuple-element.25), channel_id=1, source_target_pairs={{0,11},{1,9},{2,10},{3,8},{4,3},{5,1},{6,2},{7,0},{8,15},{9,13},{1... | collective-permute-start | bytes 602120 | tf_op jit(solution)/shard_map/ppermute | solution.py:30
  13.4 10.1 %collective-permute-done.3.refs_4_ = f32[392,128]{1,0:T(8,128)S(1)} collective-permute-done((f32[392,128]{1,0:T(8,128)S(1)}, f32[392,128]{1,0:T(8,128)S(1)}, u32[]{:S(2)}, u32[]{:S(2)}) %collective-permute-start.3) | collective-permute-done | bytes 200736 | tf_op jit(solution)/shard_map/ppermute | solution.py:30
  23.5 0.5 collective-permute-start.1
  24.0 2.1 %collective-permute-done.4.refs_5_ = f32[392,128]{1,0:T(8,128)S(1)} collective-permute-done((f32[392,128]{1,0:T(8,128)S(1)}, f32[392,128]{1,0:T(8,128)S(1)}, u32[]{:S(2)}, u32[]{:S(2)}) %collective-permute-start.4) | collective-permute-done | bytes 200736 | tf_op jit(solution)/shard_map/ppermute | solution.py:30
  26.1 0.0 collective-permute-done.5.refs_6_
  26.1 0.5 collective-permute-start.7
  26.6 0.0 collective-permute-done.refs_0_
  26.6 0.1 collective-permute-start.8
  26.7 0.4 collective-permute-start.9
  27.1 1.1 %shard_map.87 = (f32[512,512]{1,0:T(8,128)S(1)}, bf16[512,512]{1,0:T(8,128)(2,1)S(1)}, bf16[512,512]{1,0:T(8,128)(2,1)S(1)}) custom-call(f32[392,128]{1,0:T(8,128)S(1)} %get-tuple-element.22.refs_0_, f32[392,128]{1,0:T(8,128)S(1)} %get-tuple-element.23.refs_1_, f32[512,512]{1,0:T(8,128)S(1)} %copy-done, f32[512,512]{1,0:T(8,128)S(1)} %collective-permute-done.2.refs_3_, ...), custom_call_target="tpu_custom_call" | custom-call | flops 671088640 | bytes 6447104 | tf_op jit(solution)/shard_map/pallas_call | solution.py:96
  28.2 0.0 collective-permute-done.10.refs_8_
  28.2 0.0 collective-permute-done.7.refs_5_
  28.3 0.1 collective-permute-done.9.refs_7_
  28.4 1.0 %shard_map.88.own_ref = f32[512,512]{1,0:T(8,128)S(1)} custom-call(f32[392,128]{1,0:T(8,128)S(1)} %collective-permute-done.refs_0_, f32[392,128]{1,0:T(8,128)S(1)} %collective-permute-done.1.refs_1_, bf16[512,512]{1,0:T(8,128)(2,1)S(1)} %get-tuple-element.26.refs_2_, bf16[512,512]{1,0:T(8,128)(2,1)S(1)} %get-tuple-element.27.refs_3_, ...), custom_call_target="tpu_custom_call" | custom-call | flops 671088640 | bytes 5398528 | tf_op jit(solution)/shard_map/pallas_call | solution.py:96
  29.4 0.3 collective-permute-start.11
  29.7 2.4 %collective-permute-done.11.other_ref = f32[512,512]{1,0:T(8,128)S(1)} collective-permute-done((f32[512,512]{1,0:T(8,128)S(1)}, f32[512,512]{1,0:T(8,128)S(1)}, u32[]{:S(2)}, u32[]{:S(2)}) %collective-permute-start.11) | collective-permute-done | bytes 1048608 | tf_op jit(solution)/shard_map/ppermute | solution.py:30
  32.1 0.8 shard_map.89
  32.9 1.1 %collective-permute-start.14 = (f32[96,512]{1,0:T(8,128)S(1)}, f32[96,512]{1,0:T(8,128)S(1)}, u32[]{:S(2)}, u32[]{:S(2)}) collective-permute-start(f32[96,512]{1,0:T(8,128)S(1)} %get-tuple-element.34), channel_id=1, source_target_pairs={{0,4},{1,5},{2,6},{3,7},{4,0},{5,1},{6,2},{7,3},{8,12},{9,13},{10,... | collective-permute-start | bytes 589832 | tf_op jit(solution)/shard_map/ppermute | solution.py:30
  33.9 1.0 %collective-permute-start.12 = (f32[96,512]{1,0:T(8,128)S(1)}, f32[96,512]{1,0:T(8,128)S(1)}, u32[]{:S(2)}, u32[]{:S(2)}) collective-permute-start(f32[96,512]{1,0:T(8,128)S(1)} %get-tuple-element.29), channel_id=1, source_target_pairs={{0,4},{1,5},{2,6},{3,7},{4,0},{5,1},{6,2},{7,3},{8,12},{9,13},{10,... | collective-permute-start | bytes 589832 | tf_op jit(solution)/shard_map/ppermute | solution.py:30
  35.0 1.0 %collective-permute-start.18 = (f32[64,512]{1,0:T(8,128)S(1)}, f32[64,512]{1,0:T(8,128)S(1)}, u32[]{:S(2)}, u32[]{:S(2)}) collective-permute-start(f32[64,512]{1,0:T(8,128)S(1)} %get-tuple-element.35), channel_id=1, source_target_pairs={{0,4},{1,5},{2,6},{3,7},{4,0},{5,1},{6,2},{7,3},{8,12},{9,13},{10,... | collective-permute-start | bytes 393224 | tf_op jit(solution)/shard_map/ppermute | solution.py:30
  36.0 0.7 shard_map.90
  36.7 4.0 %collective-permute-done.14.near_ref = f32[96,512]{1,0:T(8,128)S(1)} collective-permute-done((f32[96,512]{1,0:T(8,128)S(1)}, f32[96,512]{1,0:T(8,128)S(1)}, u32[]{:S(2)}, u32[]{:S(2)}) %collective-permute-start.14) | collective-permute-done | bytes 196640 | tf_op jit(solution)/shard_map/ppermute | solution.py:30
  40.7 0.4 shard_map.92.refs_2_
  41.1 0.1 collective-permute-start.16
  41.2 3.8 %collective-permute-done.12.near_ref = f32[96,512]{1,0:T(8,128)S(1)} collective-permute-done((f32[96,512]{1,0:T(8,128)S(1)}, f32[96,512]{1,0:T(8,128)S(1)}, u32[]{:S(2)}, u32[]{:S(2)}) %collective-permute-start.12) | collective-permute-done | bytes 196640 | tf_op jit(solution)/shard_map/ppermute | solution.py:30
  44.9 0.4 shard_map.91.refs_1_
  45.3 0.1 collective-permute-start.15
  45.4 0.5 collective-permute-start.17
  45.9 0.1 collective-permute-start.13
  46.0 1.0 %collective-permute-done.18.near_ref = f32[64,512]{1,0:T(8,128)S(1)} collective-permute-done((f32[64,512]{1,0:T(8,128)S(1)}, f32[64,512]{1,0:T(8,128)S(1)}, u32[]{:S(2)}, u32[]{:S(2)}) %collective-permute-start.18) | collective-permute-done | bytes 131104 | tf_op jit(solution)/shard_map/ppermute | solution.py:30
  47.0 0.4 shard_map.94.refs_5_.refs_8_
  47.4 0.1 collective-permute-start.19
  47.4 1.3 %collective-permute-done.19.refs_6_.refs_9_ = f32[64,512]{1,0:T(8,128)S(1)} collective-permute-done((f32[64,512]{1,0:T(8,128)S(1)}, f32[64,512]{1,0:T(8,128)S(1)}, u32[]{:S(2)}, u32[]{:S(2)}) %collective-permute-start.19) | collective-permute-done | bytes 131104 | tf_op jit(solution)/shard_map/ppermute | solution.py:30
  48.8 0.0 collective-permute-done.13.refs_0_.refs_7_
  48.8 0.7 shard_map.95.refs_1_
  49.5 1.7 %collective-permute-start.25 = (f32[96,640]{1,0:T(8,128)S(1)}, f32[96,640]{1,0:T(8,128)S(1)}, u32[]{:S(2)}, u32[]{:S(2)}) collective-permute-start(f32[96,640]{1,0:T(8,128)S(1)} %shard_map.95.refs_1_), channel_id=1, source_target_pairs={{0,2},{1,3},{2,0},{3,1},{4,6},{5,7},{6,4},{7,5},{8,10},{9,11},{10,... | collective-permute-start | bytes 737288 | tf_op jit(solution)/shard_map/ppermute | solution.py:30
  51.3 0.0 collective-permute-start.20
  51.3 0.5 shard_map.93.refs_0_
  51.8 0.4 collective-permute-start.24
  52.2 0.4 collective-permute-done.20.refs_0_
  52.6 0.6 shard_map.96.refs_2_
  53.2 0.2 collective-permute-start.23
  53.4 1.3 %collective-permute-start.26 = (f32[64,512]{1,0:T(8,128)S(1)}, f32[64,512]{1,0:T(8,128)S(1)}, u32[]{:S(2)}, u32[]{:S(2)}) collective-permute-start(f32[64,512]{1,0:T(8,128)S(1)} %shard_map.96.refs_2_), channel_id=1, source_target_pairs={{0,2},{1,3},{2,0},{3,1},{4,6},{5,7},{6,4},{7,5},{8,10},{9,11},{10,... | collective-permute-start | bytes 393224 | tf_op jit(solution)/shard_map/ppermute | solution.py:30
  54.8 0.0 collective-permute-start.22
  54.8 3.6 %collective-permute-done.25.refs_3_ = f32[96,640]{1,0:T(8,128)S(1)} collective-permute-done((f32[96,640]{1,0:T(8,128)S(1)}, f32[96,640]{1,0:T(8,128)S(1)}, u32[]{:S(2)}, u32[]{:S(2)}) %collective-permute-start.25) | collective-permute-done | bytes 245792 | tf_op jit(solution)/shard_map/ppermute | solution.py:30
  58.4 0.0 collective-permute-start.28
  58.4 0.0 collective-permute-done.23.refs_5_
  58.4 0.5 collective-permute-start.21
  58.9 2.6 %collective-permute-done.24.refs_2_ = f32[96,384]{1,0:T(8,128)S(1)} collective-permute-done((f32[96,384]{1,0:T(8,128)S(1)}, f32[96,384]{1,0:T(8,128)S(1)}, u32[]{:S(2)}, u32[]{:S(2)}) %collective-permute-start.24) | collective-permute-done | bytes 147488 | tf_op jit(solution)/shard_map/ppermute | solution.py:30
  61.6 0.0 collective-permute-start.27
  61.6 2.0 %collective-permute-done.26.refs_4_ = f32[64,512]{1,0:T(8,128)S(1)} collective-permute-done((f32[64,512]{1,0:T(8,128)S(1)}, f32[64,512]{1,0:T(8,128)S(1)}, u32[]{:S(2)}, u32[]{:S(2)}) %collective-permute-start.26) | collective-permute-done | bytes 131104 | tf_op jit(solution)/shard_map/ppermute | solution.py:30
  63.6 0.0 collective-permute-start.29
  63.6 0.0 collective-permute-done.21.refs_3_
  63.6 0.4 shard_map.97
  64.0 0.9 %collective-permute-done.29.refs_7_ = f32[64,512]{1,0:T(8,128)S(1)} collective-permute-done((f32[64,512]{1,0:T(8,128)S(1)}, f32[64,512]{1,0:T(8,128)S(1)}, u32[]{:S(2)}, u32[]{:S(2)}) %collective-permute-start.29) | collective-permute-done | bytes 131104 | tf_op jit(solution)/shard_map/ppermute | solution.py:30
  64.9 1.7 %shard_map.98 = (f32[64,256]{1,0:T(8,128)S(1)}, f32[72,256]{1,0:T(8,128)S(1)}) custom-call(bf16[512,512]{1,0:T(8,128)(2,1)S(1)} %get-tuple-element.36.refs_0_, bf16[512,512]{1,0:T(8,128)(2,1)S(1)} %get-tuple-element.37.refs_1_, f32[96,384]{1,0:T(8,128)S(1)} %collective-permute-done.24.refs_2_, f32[96,640]{1,0:T(8,128)S(1)} %collective-permute-done.25.refs_3_, ...), custom_call_target="tpu_custom_call" | custom-call | flops 805306368 | bytes 3284992 | tf_op jit(solution)/shard_map/pallas_call | solution.py:96
  66.6 8.7 %collective-permute-start.30 = (f32[72,256]{1,0:T(8,128)S(1)}, f32[72,256]{1,0:T(8,128)S(1)}, u32[]{:S(2)}, u32[]{:S(2)}) collective-permute-start(f32[72,256]{1,0:T(8,128)S(1)} %get-tuple-element.39.send_ref), channel_id=1, source_target_pairs={{0,4},{1,5},{2,6},{3,7},{4,0},{5,1},{6,2},{7,3},{8,12},{9,13},{10,... | collective-permute-start | bytes 221192 | tf_op jit(solution)/shard_map/ppermute | solution.py:30
  75.3 2.6 %collective-permute-done.30.got_ref = f32[72,256]{1,0:T(8,128)S(1)} collective-permute-done((f32[72,256]{1,0:T(8,128)S(1)}, f32[72,256]{1,0:T(8,128)S(1)}, u32[]{:S(2)}, u32[]{:S(2)}) %collective-permute-start.30) | collective-permute-done | bytes 73760 | tf_op jit(solution)/shard_map/ppermute | solution.py:30
  77.9 0.6 shard_map.99
  (14 shorter events, 0.0 us)
Async XLA Ops:
  0.6 26.5 %copy-start = (f32[512,512]{1,0:T(8,128)S(1)}, f32[512,512]{1,0:T(8,128)}, u32[]{:S(2)}) copy-start(f32[512,512]{1,0:T(8,128)} %refs_2_.1) | copy-start | bytes 3145732
  0.6 26.0 %collective-permute-start.2 = (f32[512,512]{1,0:T(8,128)}, f32[512,512]{1,0:T(8,128)S(1)}, u32[]{:S(2)}, u32[]{:S(2)}) collective-permute-start(f32[512,512]{1,0:T(8,128)} %refs_2_.1), channel_id=1, source_target_pairs={{0,3},{1,17},{2,18},{3,0},{4,7},{5,21},{6,22},{7,4},{8,11},{9,25},... | collective-permute-start | bytes 3145736 | tf_op jit(solution)/shard_map/ppermute | solution.py:30
  5.0 18.4 %collective-permute-start.3 = (f32[392,128]{1,0:T(8,128)S(1)}, f32[392,128]{1,0:T(8,128)S(1)}, u32[]{:S(2)}, u32[]{:S(2)}) collective-permute-start(f32[392,128]{1,0:T(8,128)S(1)} %get-tuple-element.22.refs_0_), channel_id=1, source_target_pairs={{0,3},{1,17},{2,18},{3,0},{4,11},{5,9},{6,10},{7,8},{8,7},{9,5},{1... | collective-permute-start | bytes 602120 | tf_op jit(solution)/shard_map/ppermute | solution.py:30
  5.1 18.3 %collective-permute-start.6 = (f32[392,128]{1,0:T(8,128)S(1)}, f32[392,128]{1,0:T(8,128)S(1)}, u32[]{:S(2)}, u32[]{:S(2)}) collective-permute-start(f32[392,128]{1,0:T(8,128)S(1)} %get-tuple-element.23.refs_1_), channel_id=1, source_target_pairs={{0,15},{1,13},{2,14},{3,12},{4,7},{5,21},{6,22},{7,4},{8,11},{9,25... | collective-permute-start | bytes 602120 | tf_op jit(solution)/shard_map/ppermute | solution.py:30
  9.8 16.2 %collective-permute-start.4 = (f32[392,128]{1,0:T(8,128)S(1)}, f32[392,128]{1,0:T(8,128)S(1)}, u32[]{:S(2)}, u32[]{:S(2)}) collective-permute-start(f32[392,128]{1,0:T(8,128)S(1)} %get-tuple-element.24), channel_id=1, source_target_pairs={{0,7},{1,5},{2,6},{3,4},{4,15},{5,13},{6,14},{7,12},{8,3},{9,1},{1... | collective-permute-start | bytes 602120 | tf_op jit(solution)/shard_map/ppermute | solution.py:30
  9.8 16.2 %collective-permute-start.5 = (f32[392,128]{1,0:T(8,128)S(1)}, f32[392,128]{1,0:T(8,128)S(1)}, u32[]{:S(2)}, u32[]{:S(2)}) collective-permute-start(f32[392,128]{1,0:T(8,128)S(1)} %get-tuple-element.25), channel_id=1, source_target_pairs={{0,11},{1,9},{2,10},{3,8},{4,3},{5,1},{6,2},{7,0},{8,15},{9,13},{1... | collective-permute-start | bytes 602120 | tf_op jit(solution)/shard_map/ppermute | solution.py:30
  23.4 3.1 %collective-permute-start = (f32[392,128]{1,0:T(8,128)S(1)}, f32[392,128]{1,0:T(8,128)S(1)}, u32[]{:S(2)}, u32[]{:S(2)}) collective-permute-start(f32[392,128]{1,0:T(8,128)S(1)} %get-tuple-element.22.refs_0_), channel_id=1, source_target_pairs={{0,1},{1,0},{2,3},{3,2},{4,5},{5,4},{6,7},{7,6},{8,9},{9,8},{10,11... | collective-permute-start | bytes 602120 | tf_op jit(solution)/shard_map/ppermute | solution.py:30
  23.5 4.8 %collective-permute-start.1 = (f32[392,128]{1,0:T(8,128)S(1)}, f32[392,128]{1,0:T(8,128)S(1)}, u32[]{:S(2)}, u32[]{:S(2)}) collective-permute-start(f32[392,128]{1,0:T(8,128)S(1)} %get-tuple-element.23.refs_1_), channel_id=1, source_target_pairs={{0,1},{1,0},{2,3},{3,2},{4,5},{5,4},{6,7},{7,6},{8,9},{9,8},{10,11... | collective-permute-start | bytes 602120 | tf_op jit(solution)/shard_map/ppermute | solution.py:30
  26.1 2.2 %collective-permute-start.10 = (f32[392,128]{1,0:T(8,128)S(1)}, f32[392,128]{1,0:T(8,128)S(1)}, u32[]{:S(2)}, u32[]{:S(2)}) collective-permute-start(f32[392,128]{1,0:T(8,128)S(1)} %collective-permute-done.6.refs_7_), channel_id=1, source_target_pairs={{0,1},{1,0},{2,3},{3,2},{4,5},{5,4},{6,7},{7,6},{8,9},{9,8},{10,11... | collective-permute-start | bytes 602120 | tf_op jit(solution)/shard_map/ppermute | solution.py:30
  26.1 2.2 %collective-permute-start.7 = (f32[392,128]{1,0:T(8,128)S(1)}, f32[392,128]{1,0:T(8,128)S(1)}, u32[]{:S(2)}, u32[]{:S(2)}) collective-permute-start(f32[392,128]{1,0:T(8,128)S(1)} %collective-permute-done.3.refs_4_), channel_id=1, source_target_pairs={{0,1},{1,0},{2,3},{3,2},{4,5},{5,4},{6,7},{7,6},{8,9},{9,8},{10,11... | collective-permute-start | bytes 602120 | tf_op jit(solution)/shard_map/ppermute | solution.py:30
  26.6 1.7 %collective-permute-start.8 = (f32[392,128]{1,0:T(8,128)S(1)}, f32[392,128]{1,0:T(8,128)S(1)}, u32[]{:S(2)}, u32[]{:S(2)}) collective-permute-start(f32[392,128]{1,0:T(8,128)S(1)} %collective-permute-done.4.refs_5_), channel_id=1, source_target_pairs={{0,1},{1,0},{2,3},{3,2},{4,5},{5,4},{6,7},{7,6},{8,9},{9,8},{10,11... | collective-permute-start | bytes 602120 | tf_op jit(solution)/shard_map/ppermute | solution.py:30
  26.7 1.7 %collective-permute-start.9 = (f32[392,128]{1,0:T(8,128)S(1)}, f32[392,128]{1,0:T(8,128)S(1)}, u32[]{:S(2)}, u32[]{:S(2)}) collective-permute-start(f32[392,128]{1,0:T(8,128)S(1)} %collective-permute-done.5.refs_6_), channel_id=1, source_target_pairs={{0,1},{1,0},{2,3},{3,2},{4,5},{5,4},{6,7},{7,6},{8,9},{9,8},{10,11... | collective-permute-start | bytes 602120 | tf_op jit(solution)/shard_map/ppermute | solution.py:30
  29.4 2.7 %collective-permute-start.11 = (f32[512,512]{1,0:T(8,128)S(1)}, f32[512,512]{1,0:T(8,128)S(1)}, u32[]{:S(2)}, u32[]{:S(2)}) collective-permute-start(f32[512,512]{1,0:T(8,128)S(1)} %shard_map.88.own_ref), channel_id=1, source_target_pairs={{0,1},{1,0},{2,3},{3,2},{4,5},{5,4},{6,7},{7,6},{8,9},{9,8},{10,11... | collective-permute-start | bytes 3145736 | tf_op jit(solution)/shard_map/ppermute | solution.py:30
  32.9 7.8 %collective-permute-start.14 = (f32[96,512]{1,0:T(8,128)S(1)}, f32[96,512]{1,0:T(8,128)S(1)}, u32[]{:S(2)}, u32[]{:S(2)}) collective-permute-start(f32[96,512]{1,0:T(8,128)S(1)} %get-tuple-element.34), channel_id=1, source_target_pairs={{0,4},{1,5},{2,6},{3,7},{4,0},{5,1},{6,2},{7,3},{8,12},{9,13},{10,... | collective-permute-start | bytes 589832 | tf_op jit(solution)/shard_map/ppermute | solution.py:30
  33.9 11.0 %collective-permute-start.12 = (f32[96,512]{1,0:T(8,128)S(1)}, f32[96,512]{1,0:T(8,128)S(1)}, u32[]{:S(2)}, u32[]{:S(2)}) collective-permute-start(f32[96,512]{1,0:T(8,128)S(1)} %get-tuple-element.29), channel_id=1, source_target_pairs={{0,4},{1,5},{2,6},{3,7},{4,0},{5,1},{6,2},{7,3},{8,12},{9,13},{10,... | collective-permute-start | bytes 589832 | tf_op jit(solution)/shard_map/ppermute | solution.py:30
  35.0 12.0 %collective-permute-start.18 = (f32[64,512]{1,0:T(8,128)S(1)}, f32[64,512]{1,0:T(8,128)S(1)}, u32[]{:S(2)}, u32[]{:S(2)}) collective-permute-start(f32[64,512]{1,0:T(8,128)S(1)} %get-tuple-element.35), channel_id=1, source_target_pairs={{0,4},{1,5},{2,6},{3,7},{4,0},{5,1},{6,2},{7,3},{8,12},{9,13},{10,... | collective-permute-start | bytes 393224 | tf_op jit(solution)/shard_map/ppermute | solution.py:30
  41.1 7.7 %collective-permute-start.16 = (f32[96,512]{1,0:T(8,128)S(1)}, f32[96,512]{1,0:T(8,128)S(1)}, u32[]{:S(2)}, u32[]{:S(2)}) collective-permute-start(f32[96,512]{1,0:T(8,128)S(1)} %shard_map.92.refs_2_), channel_id=1, source_target_pairs={{0,1},{1,0},{2,3},{3,2},{4,5},{5,4},{6,7},{7,6},{8,9},{9,8},{10,11... | collective-permute-start | bytes 589832 | tf_op jit(solution)/shard_map/ppermute | solution.py:30
  45.3 3.5 %collective-permute-start.15 = (f32[96,512]{1,0:T(8,128)S(1)}, f32[96,512]{1,0:T(8,128)S(1)}, u32[]{:S(2)}, u32[]{:S(2)}) collective-permute-start(f32[96,512]{1,0:T(8,128)S(1)} %shard_map.91.refs_1_), channel_id=1, source_target_pairs={{0,1},{1,0},{2,3},{3,2},{4,5},{5,4},{6,7},{7,6},{8,9},{9,8},{10,11... | collective-permute-start | bytes 589832 | tf_op jit(solution)/shard_map/ppermute | solution.py:30
  45.4 3.4 %collective-permute-start.17 = (f32[96,512]{1,0:T(8,128)S(1)}, f32[96,512]{1,0:T(8,128)S(1)}, u32[]{:S(2)}, u32[]{:S(2)}) collective-permute-start(f32[96,512]{1,0:T(8,128)S(1)} %shard_map.92.refs_2_), channel_id=1, source_target_pairs={{0,1},{1,0},{2,3},{3,2},{4,8},{5,9},{6,10},{7,11},{8,4},{9,5},{10,... | collective-permute-start | bytes 589832 | tf_op jit(solution)/shard_map/ppermute | solution.py:30
  45.9 2.9 %collective-permute-start.13 = (f32[96,512]{1,0:T(8,128)S(1)}, f32[96,512]{1,0:T(8,128)S(1)}, u32[]{:S(2)}, u32[]{:S(2)}) collective-permute-start(f32[96,512]{1,0:T(8,128)S(1)} %shard_map.91.refs_1_), channel_id=1, source_target_pairs={{0,1},{1,0},{2,3},{3,2},{4,8},{5,9},{6,10},{7,11},{8,4},{9,5},{10,... | collective-permute-start | bytes 589832 | tf_op jit(solution)/shard_map/ppermute | solution.py:30
  47.4 1.4 %collective-permute-start.19 = (f32[64,512]{1,0:T(8,128)S(1)}, f32[64,512]{1,0:T(8,128)S(1)}, u32[]{:S(2)}, u32[]{:S(2)}) collective-permute-start(f32[64,512]{1,0:T(8,128)S(1)} %shard_map.94.refs_5_.refs_8_), channel_id=1, source_target_pairs={{0,1},{1,0},{2,3},{3,2},{4,5},{5,4},{6,7},{7,6},{8,9},{9,8},{10,11... | collective-permute-start | bytes 393224 | tf_op jit(solution)/shard_map/ppermute | solution.py:30
  49.5 8.9 %collective-permute-start.25 = (f32[96,640]{1,0:T(8,128)S(1)}, f32[96,640]{1,0:T(8,128)S(1)}, u32[]{:S(2)}, u32[]{:S(2)}) collective-permute-start(f32[96,640]{1,0:T(8,128)S(1)} %shard_map.95.refs_1_), channel_id=1, source_target_pairs={{0,2},{1,3},{2,0},{3,1},{4,6},{5,7},{6,4},{7,5},{8,10},{9,11},{10,... | collective-permute-start | bytes 737288 | tf_op jit(solution)/shard_map/ppermute | solution.py:30
  51.3 1.3 %collective-permute-start.20 = (f32[64,512]{1,0:T(8,128)S(1)}, f32[64,512]{1,0:T(8,128)S(1)}, u32[]{:S(2)}, u32[]{:S(2)}) collective-permute-start(f32[64,512]{1,0:T(8,128)S(1)} %shard_map.94.refs_5_.refs_8_), channel_id=1, source_target_pairs={{0,1},{1,0},{2,3},{3,2},{4,8},{5,9},{6,10},{7,11},{8,4},{9,5},{10,... | collective-permute-start | bytes 393224 | tf_op jit(solution)/shard_map/ppermute | solution.py:30
  51.8 9.8 %collective-permute-start.24 = (f32[96,384]{1,0:T(8,128)S(1)}, f32[96,384]{1,0:T(8,128)S(1)}, u32[]{:S(2)}, u32[]{:S(2)}) collective-permute-start(f32[96,384]{1,0:T(8,128)S(1)} %shard_map.93.refs_0_), channel_id=1, source_target_pairs={{0,2},{1,3},{2,0},{3,1},{4,6},{5,7},{6,4},{7,5},{8,10},{9,11},{10,... | collective-permute-start | bytes 442376 | tf_op jit(solution)/shard_map/ppermute | solution.py:30
  53.2 5.2 %collective-permute-start.23 = (f32[64,512]{1,0:T(8,128)S(1)}, f32[64,512]{1,0:T(8,128)S(1)}, u32[]{:S(2)}, u32[]{:S(2)}) collective-permute-start(f32[64,512]{1,0:T(8,128)S(1)} %shard_map.96.refs_2_), channel_id=1, source_target_pairs={{0,1},{1,0},{2,3},{3,2},{4,5},{5,4},{6,7},{7,6},{8,9},{9,8},{10,11... | collective-permute-start | bytes 393224 | tf_op jit(solution)/shard_map/ppermute | solution.py:30
  53.4 10.1 %collective-permute-start.26 = (f32[64,512]{1,0:T(8,128)S(1)}, f32[64,512]{1,0:T(8,128)S(1)}, u32[]{:S(2)}, u32[]{:S(2)}) collective-permute-start(f32[64,512]{1,0:T(8,128)S(1)} %shard_map.96.refs_2_), channel_id=1, source_target_pairs={{0,2},{1,3},{2,0},{3,1},{4,6},{5,7},{6,4},{7,5},{8,10},{9,11},{10,... | collective-permute-start | bytes 393224 | tf_op jit(solution)/shard_map/ppermute | solution.py:30
  54.8 8.8 %collective-permute-start.22 = (f32[96,640]{1,0:T(8,128)S(1)}, f32[96,640]{1,0:T(8,128)S(1)}, u32[]{:S(2)}, u32[]{:S(2)}) collective-permute-start(f32[96,640]{1,0:T(8,128)S(1)} %shard_map.95.refs_1_), channel_id=1, source_target_pairs={{0,1},{1,0},{2,3},{3,2},{4,5},{5,4},{6,7},{7,6},{8,9},{9,8},{10,11... | collective-permute-start | bytes 737288 | tf_op jit(solution)/shard_map/ppermute | solution.py:30
  58.4 6.5 %collective-permute-start.28 = (f32[96,640]{1,0:T(8,128)S(1)}, f32[96,640]{1,0:T(8,128)S(1)}, u32[]{:S(2)}, u32[]{:S(2)}) collective-permute-start(f32[96,640]{1,0:T(8,128)S(1)} %collective-permute-done.25.refs_3_), channel_id=1, source_target_pairs={{0,1},{1,0},{2,3},{3,2},{4,5},{5,4},{6,7},{7,6},{8,9},{9,8},{10,11... | collective-permute-start | bytes 737288 | tf_op jit(solution)/shard_map/ppermute | solution.py:30
  58.4 5.2 %collective-permute-start.21 = (f32[96,384]{1,0:T(8,128)S(1)}, f32[96,384]{1,0:T(8,128)S(1)}, u32[]{:S(2)}, u32[]{:S(2)}) collective-permute-start(f32[96,384]{1,0:T(8,128)S(1)} %shard_map.93.refs_0_), channel_id=1, source_target_pairs={{0,1},{1,0},{2,3},{3,2},{4,5},{5,4},{6,7},{7,6},{8,9},{9,8},{10,11... | collective-permute-start | bytes 442376 | tf_op jit(solution)/shard_map/ppermute | solution.py:30
  61.6 3.3 %collective-permute-start.27 = (f32[96,384]{1,0:T(8,128)S(1)}, f32[96,384]{1,0:T(8,128)S(1)}, u32[]{:S(2)}, u32[]{:S(2)}) collective-permute-start(f32[96,384]{1,0:T(8,128)S(1)} %collective-permute-done.24.refs_2_), channel_id=1, source_target_pairs={{0,1},{1,0},{2,3},{3,2},{4,5},{5,4},{6,7},{7,6},{8,9},{9,8},{10,11... | collective-permute-start | bytes 442376 | tf_op jit(solution)/shard_map/ppermute | solution.py:30
  63.6 1.3 %collective-permute-start.29 = (f32[64,512]{1,0:T(8,128)S(1)}, f32[64,512]{1,0:T(8,128)S(1)}, u32[]{:S(2)}, u32[]{:S(2)}) collective-permute-start(f32[64,512]{1,0:T(8,128)S(1)} %collective-permute-done.26.refs_4_), channel_id=1, source_target_pairs={{0,1},{1,0},{2,3},{3,2},{4,5},{5,4},{6,7},{7,6},{8,9},{9,8},{10,11... | collective-permute-start | bytes 393224 | tf_op jit(solution)/shard_map/ppermute | solution.py:30
  66.6 11.3 %collective-permute-start.30 = (f32[72,256]{1,0:T(8,128)S(1)}, f32[72,256]{1,0:T(8,128)S(1)}, u32[]{:S(2)}, u32[]{:S(2)}) collective-permute-start(f32[72,256]{1,0:T(8,128)S(1)} %get-tuple-element.39.send_ref), channel_id=1, source_target_pairs={{0,4},{1,5},{2,6},{3,7},{4,0},{5,1},{6,2},{7,3},{8,12},{9,13},{10,... | collective-permute-start | bytes 221192 | tf_op jit(solution)/shard_map/ppermute | solution.py:30

commit v7 on v6

--- a/solution.py
+++ b/solution.py
@@ -318,21 +318,28 @@
         used += 1 + count
 
 
+def put_rows(mine, ref, at, piece, ends):
+    size = ref.shape[1] // 2
+    tail = 2 * size // 8
+    body = size - tail
+    own, other = mine * size, (1 - mine) * size
+    rows = slice(at, at + piece.shape[0])
+    ref[rows, own : own + body] = piece[:, 0:body]
+    ref[rows, other : other + body] = piece[:, body : 2 * body]
+    ends_ref, start = ends
+    ref[rows, own + body : own + size] = ends_ref[:, start : start + tail]
+    ref[rows, other + body : other + size] = ends_ref[:, start + tail : start + 2 * tail]
+
+
 def gather_pieces(mine, ref, pieces):
-    first, second, third = pieces
-    size = ref.shape[0] // 2
-    long = first.shape[0]
-    body = 2 * long
-    tail = size - body
-    own, other = mine * size, (1 - mine) * size
-    at = own
-    for piece, low, high in ((first, second, 4 * long + 2 * tail), (second, second, 4 * long), (third, third, 4 * long)):
-        rows = slice(at, at + piece.shape[0])
-        ref[rows, own : own + body] = piece[:, 0:body]
-        ref[rows, other : other + body] = piece[:, body : 2 * body]
-        ref[rows, own + body : own + size] = low[:, high : high + tail]
-        ref[rows, other + body : other + size] = low[:, high + tail : high + 2 * tail]
-        at += piece.shape[0]
+    width = ref.shape[1]
+    first, second = pieces[:2]
+    body = width - width // 4
+    at = mine * (width // 2)
+    put_rows(mine, ref, at, first, (second, width))
+    put_rows(mine, ref, at + first.shape[0], second, (second, body))
+    for third in pieces[2:]:
+        put_rows(mine, ref, at + 2 * first.shape[0], third, (third, body))
 
 
 def gather_both(near, far, ref):
@@ -345,28 +352,75 @@
             gather_pieces(1 - k, ref, far)
 
 
+def is_own_left():
+    tile = lax.axis_index("tile")
+    return ((tile >> 2) & 1) == (tile & 1)
+
+
 def fold_ready_kernel(count, *refs):
     near, far, (high_ref, low_ref, own_ref) = refs[:count], refs[count : 2 * count], refs[2 * count :]
     gather_both(near, far, own_ref)
     high_ref[...], low_ref[...] = split2(own_ref[...])
 
 
-def fold_last_kernel(count, *refs):
-    high_ref, low_ref, *refs = refs
-    block_ref, send_ref, got_ref, whole_ref = refs[2 * count :]
-    gather_both(refs[:count], refs[count : 2 * count], got_ref)
+def fold_ends_kernel(high_ref, low_ref, end_high_ref, end_low_ref):
+    core = lax.axis_index("cuts")
+    size = high_ref.shape[1] // 2
+    tail = end_high_ref.shape[1] // 2
+    for ref, end_ref in ((high_ref, end_high_ref), (low_ref, end_low_ref)):
+        first, second = (ref[:, (j + 1) * size - tail : (j + 1) * size].astype(F32) for j in range(2))
+        both = jnp.where(core == 0, jnp.concatenate([first, second], axis=1), jnp.concatenate([second, first], axis=1))
+        end_ref[...] = both.astype(BF)
+
+
+def fold_partial_kernel(high_ref, low_ref, near0, near1, far0, far1, part_ref, got_ref):
+    size = got_ref.shape[0] // 2
+    tail = size - 2 * near0.shape[0]
+    for j in range(2):
+        got_ref[(j + 1) * size - tail : (j + 1) * size, :] = jnp.zeros((tail, got_ref.shape[1]), F32)
+    gather_both((near0, near1), (far0, far1), got_ref)
+    left = is_own_left()
+
+    @pl.when(left)
+    def _():
+        gh, gl = split2(got_ref[...])
+        part_ref[...] = mul(high_ref[...], gh) + (mul(high_ref[...], gl) + mul(low_ref[...], gh))
+
+    @pl.when(jnp.logical_not(left))
+    def _():
+        gh, gl = split2(got_ref[...])
+        part_ref[...] = mul(gh, high_ref[...]) + (mul(gl, high_ref[...]) + mul(gh, low_ref[...]))
+
+
+def fold_last_kernel(high_ref, low_ref, end_high_ref, end_low_ref, part_ref, near_ref, far_ref, *refs):
+    block_ref, send_ref, got_ref, whole_ref = refs
     core, tile = lax.axis_index("cuts"), lax.axis_index("tile")
     side, column, group = (tile >> 2) & 1, tile & 1, tile >> 1
-
-    @pl.when(side == column)
+    width = whole_ref.shape[1]
+    tail, size = near_ref.shape[0], width // 2
+    body = width - width // 4
+    for k in range(2):
+
+        @pl.when(core == k)
+        def _(k=k):
+            put_rows(k, got_ref, 0, near_ref, (near_ref, body))
+            put_rows(1 - k, got_ref, tail, far_ref, (far_ref, body))
+
+    gh, gl = split2(got_ref[...])
+    left = is_own_left()
+
+    @pl.when(left)
     def _():
-        gh, gl = split2(got_ref[...])
-        whole_ref[...] = mul(high_ref[...], gh) + (mul(high_ref[...], gl) + mul(low_ref[...], gh))
-
-    @pl.when(side != column)
+        more = mul(end_high_ref[...], gh) + (mul(end_high_ref[...], gl) + mul(end_low_ref[...], gh))
+        whole_ref[...] = part_ref[...] + more
+
+    @pl.when(jnp.logical_not(left))
     def _():
-        gh, gl = split2(got_ref[...])
-        whole_ref[...] = mul(gh, high_ref[...]) + (mul(gl, high_ref[...]) + mul(gh, low_ref[...]))
+        rows = mul(gh, high_ref[...]) + (mul(gl, high_ref[...]) + mul(gh, low_ref[...]))
+        whole_ref[...] = part_ref[...]
+        for j, at in enumerate((core, 1 - core)):
+            start = pl.multiple_of(at * size + size - tail, 8)
+            whole_ref[pl.ds(start, tail), :] = rows[j * tail : (j + 1) * tail, :]
 
     whole = whole_ref[...]
     square = jnp.sum(jnp.sum(whole * whole, axis=0, keepdims=True), axis=1, keepdims=True)
@@ -504,19 +558,29 @@
     theirs_far = [moved(part, other_core) for part in theirs]
     tall, cols = width // tiles, width // 2
     split = jax.ShapeDtypeStruct((width, width), BF)
+    ends = jax.ShapeDtypeStruct((width, 2 * sizes[2]), BF)
+    square = [pltpu.VMEM((width, width), F32)]
     own = call(
         functools.partial(fold_ready_kernel, count),
         [split, split],
         (*mine, *mine_far),
-        scratch=[pltpu.VMEM((width, width), F32)],
+        scratch=square,
         flops=width * width,
     )
+    own += call(fold_ends_kernel, [ends, ends], own, flops=width * width)
+    (part,) = call(
+        fold_partial_kernel,
+        [like(width, width)],
+        (*own[:2], *theirs[:2], *theirs_far[:2]),
+        scratch=square,
+        flops=cost * width,
+    )
     block, send = call(
-        functools.partial(fold_last_kernel, count),
+        fold_last_kernel,
         [like(tall, cols), like(tall + PAD, cols)],
-        (*own, *theirs, *theirs_far),
-        scratch=[pltpu.VMEM((width, width), F32)] * 2,
-        flops=cost * width,
+        (*own, part, theirs[2], theirs_far[2]),
+        scratch=[pltpu.VMEM((2 * sizes[2], width), F32)] + square,
+        flops=cost * width // 2,
     )
     out, log = call(
         choose_kernel, [like(tall, cols), like(1, 1)], (block, send, moved(send, across(1))), kept=False

time: 78.7 us -> 80.5 us (1.023)
  Pallas kernels: 11.2 us -> 12.2 us
  starting transfers between devices: 29.5 us -> 30.5 us
    pallas_call x14 -> x16, Pallas kernels: 11.2 us -> 12.2 us  [call(): pl.pallas_call(kernel, out_shape=tuple((pltpu.VMEM(o.shape, o.dtype) if k...]
    ppermute x31, starting transfers between devices: 29.5 us -> 30.5 us  [moved(): lax.ppermute(x, AXES, pairs(lax.axis_size('groups'), lax.axis_size('tile'...]
  transfers between devices with their start and end apart: 31 -> 31, of which waited for: 14 -> 13; matrix products, arithmetic and copies ran while one was open for 0% -> 0% of each run, Pallas kernels for 8% -> 10%
where the time goes in v7:
time: 80.5 us; the launch traced here: 80.4 us
  waiting for transfers between devices  36.8 us (46%)
  starting transfers between devices  30.5 us (38%)
  Pallas kernels  12.2 us (15%)
  between operations  0.86 us (1%)
    ppermute x31, waiting for transfers between devices, moved(): lax.ppermute(x, AXES, pairs(lax.axis_size('groups'), lax.axis_size('tile'...  36.8 us
    ppermute x31, starting transfers between devices, moved(): lax.ppermute(x, AXES, pairs(lax.axis_size('groups'), lax.axis_size('tile'...  30.5 us
    pallas_call x16, Pallas kernels, call(): pl.pallas_call(kernel, out_shape=tuple((pltpu.VMEM(o.shape, o.dtype) if k...  12.2 us
  transfers between devices with their start and end apart: 31, of which 13 were waited for; matrix products, arithmetic and copies ran while one was open for 0% of the time, Pallas kernels for 10%

profile of v7, /device:TPU:0, one launch (start us, length us, event | category | flops | bytes accessed | tf_op | source)
XLA Modules:
  0.0 80.4 jit_solution(5838106904442613243)
XLA Ops:
  0.6 2.5 %collective-permute-start.2 = (f32[512,512]{1,0:T(8,128)}, f32[512,512]{1,0:T(8,128)S(1)}, u32[]{:S(2)}, u32[]{:S(2)}) collective-permute-start(f32[512,512]{1,0:T(8,128)} %refs_2_.1), channel_id=1, source_target_pairs={{0,3},{1,17},{2,18},{3,0},{4,7},{5,21},{6,22},{7,4},{8,11},{9,25},... | collective-permute-start | bytes 3145736 | tf_op jit(solution)/shard_map/ppermute | solution.py:30
  3.1 1.9 %shard_map.86 = (f32[392,128]{1,0:T(8,128)S(1)}, f32[392,128]{1,0:T(8,128)S(1)}, f32[392,128]{1,0:T(8,128)S(1)}, f32[392,128]{1,0:T(8,128)S(1)}) custom-call(f32[256,512]{1,0:T(8,128)} %rows_ref.1, s32[1,256]{1,0:T(1,128)} %bitcast.4, s32[1,256]{1,0:T(1,128)} %bitcast.5, s32[1,256]{1,0:T(1,128)} %bitcast.6, s32[1,512]{1,0:T(1,128)} %order_ref.1, ...), custom_call_target="tpu_custom_call" | custom-call | flops 301989888 | bytes 1334272 | tf_op jit(solution)/shard_map/pallas_call | solution.py:96
  5.0 0.2 collective-permute-start.3
  5.1 4.7 %collective-permute-start.6 = (f32[392,128]{1,0:T(8,128)S(1)}, f32[392,128]{1,0:T(8,128)S(1)}, u32[]{:S(2)}, u32[]{:S(2)}) collective-permute-start(f32[392,128]{1,0:T(8,128)S(1)} %get-tuple-element.25.refs_1_), channel_id=1, source_target_pairs={{0,15},{1,13},{2,14},{3,12},{4,7},{5,21},{6,22},{7,4},{8,11},{9,25... | collective-permute-start | bytes 602120 | tf_op jit(solution)/shard_map/ppermute | solution.py:30
  9.9 3.5 %collective-permute-start.5 = (f32[392,128]{1,0:T(8,128)S(1)}, f32[392,128]{1,0:T(8,128)S(1)}, u32[]{:S(2)}, u32[]{:S(2)}) collective-permute-start(f32[392,128]{1,0:T(8,128)S(1)} %get-tuple-element.27), channel_id=1, source_target_pairs={{0,11},{1,9},{2,10},{3,8},{4,3},{5,1},{6,2},{7,0},{8,15},{9,13},{1... | collective-permute-start | bytes 602120 | tf_op jit(solution)/shard_map/ppermute | solution.py:30
  13.4 10.1 %collective-permute-done.3.refs_4_ = f32[392,128]{1,0:T(8,128)S(1)} collective-permute-done((f32[392,128]{1,0:T(8,128)S(1)}, f32[392,128]{1,0:T(8,128)S(1)}, u32[]{:S(2)}, u32[]{:S(2)}) %collective-permute-start.3) | collective-permute-done | bytes 200736 | tf_op jit(solution)/shard_map/ppermute | solution.py:30
  23.4 0.0 collective-permute-done.6.refs_7_
  23.5 0.5 collective-permute-start.1
  24.0 2.1 %collective-permute-done.4.refs_5_ = f32[392,128]{1,0:T(8,128)S(1)} collective-permute-done((f32[392,128]{1,0:T(8,128)S(1)}, f32[392,128]{1,0:T(8,128)S(1)}, u32[]{:S(2)}, u32[]{:S(2)}) %collective-permute-start.4) | collective-permute-done | bytes 200736 | tf_op jit(solution)/shard_map/ppermute | solution.py:30
  26.1 0.0 collective-permute-start.10
  26.1 0.0 collective-permute-done.5.refs_6_
  26.1 0.5 collective-permute-start.7
  26.6 0.0 collective-permute-done.refs_0_
  26.6 0.1 collective-permute-start.8
  26.7 0.4 collective-permute-start.9
  27.1 1.1 %shard_map.87 = (f32[512,512]{1,0:T(8,128)S(1)}, bf16[512,512]{1,0:T(8,128)(2,1)S(1)}, bf16[512,512]{1,0:T(8,128)(2,1)S(1)}) custom-call(f32[392,128]{1,0:T(8,128)S(1)} %get-tuple-element.24.refs_0_, f32[392,128]{1,0:T(8,128)S(1)} %get-tuple-element.25.refs_1_, f32[512,512]{1,0:T(8,128)S(1)} %copy-done, f32[512,512]{1,0:T(8,128)S(1)} %collective-permute-done.2.refs_3_, ...), custom_call_target="tpu_custom_call" | custom-call | flops 671088640 | bytes 6447104 | tf_op jit(solution)/shard_map/pallas_call | solution.py:96
  28.2 0.0 collective-permute-done.1.refs_1_
  28.2 0.0 collective-permute-done.10.refs_8_
  28.3 0.0 collective-permute-done.8.refs_6_
  28.3 0.1 collective-permute-done.9.refs_7_
  28.4 1.0 %shard_map.88.own_ref = f32[512,512]{1,0:T(8,128)S(1)} custom-call(f32[392,128]{1,0:T(8,128)S(1)} %collective-permute-done.refs_0_, f32[392,128]{1,0:T(8,128)S(1)} %collective-permute-done.1.refs_1_, bf16[512,512]{1,0:T(8,128)(2,1)S(1)} %get-tuple-element.28.refs_2_, bf16[512,512]{1,0:T(8,128)(2,1)S(1)} %get-tuple-element.29.refs_3_, ...), custom_call_target="tpu_custom_call" | custom-call | flops 671088640 | bytes 5398528 | tf_op jit(solution)/shard_map/pallas_call | solution.py:96
  29.4 0.3 collective-permute-start.11
  29.7 2.4 %collective-permute-done.11.other_ref = f32[512,512]{1,0:T(8,128)S(1)} collective-permute-done((f32[512,512]{1,0:T(8,128)S(1)}, f32[512,512]{1,0:T(8,128)S(1)}, u32[]{:S(2)}, u32[]{:S(2)}) %collective-permute-start.11) | collective-permute-done | bytes 1048608 | tf_op jit(solution)/shard_map/ppermute | solution.py:30
  32.1 0.7 shard_map.89
  32.9 1.1 %collective-permute-start.14 = (f32[96,512]{1,0:T(8,128)S(1)}, f32[96,512]{1,0:T(8,128)S(1)}, u32[]{:S(2)}, u32[]{:S(2)}) collective-permute-start(f32[96,512]{1,0:T(8,128)S(1)} %get-tuple-element.36), channel_id=1, source_target_pairs={{0,4},{1,5},{2,6},{3,7},{4,0},{5,1},{6,2},{7,3},{8,12},{9,13},{10,... | collective-permute-start | bytes 589832 | tf_op jit(solution)/shard_map/ppermute | solution.py:30
  34.0 1.0 %collective-permute-start.12 = (f32[96,512]{1,0:T(8,128)S(1)}, f32[96,512]{1,0:T(8,128)S(1)}, u32[]{:S(2)}, u32[]{:S(2)}) collective-permute-start(f32[96,512]{1,0:T(8,128)S(1)} %get-tuple-element.31), channel_id=1, source_target_pairs={{0,4},{1,5},{2,6},{3,7},{4,0},{5,1},{6,2},{7,3},{8,12},{9,13},{10,... | collective-permute-start | bytes 589832 | tf_op jit(solution)/shard_map/ppermute | solution.py:30
  34.9 1.0 %collective-permute-start.18 = (f32[64,512]{1,0:T(8,128)S(1)}, f32[64,512]{1,0:T(8,128)S(1)}, u32[]{:S(2)}, u32[]{:S(2)}) collective-permute-start(f32[64,512]{1,0:T(8,128)S(1)} %get-tuple-element.37), channel_id=1, source_target_pairs={{0,4},{1,5},{2,6},{3,7},{4,0},{5,1},{6,2},{7,3},{8,12},{9,13},{10,... | collective-permute-start | bytes 393224 | tf_op jit(solution)/shard_map/ppermute | solution.py:30
  36.0 0.7 shard_map.90
  36.7 4.0 %collective-permute-done.14.near_ref = f32[96,512]{1,0:T(8,128)S(1)} collective-permute-done((f32[96,512]{1,0:T(8,128)S(1)}, f32[96,512]{1,0:T(8,128)S(1)}, u32[]{:S(2)}, u32[]{:S(2)}) %collective-permute-start.14) | collective-permute-done | bytes 196640 | tf_op jit(solution)/shard_map/ppermute | solution.py:30
  40.7 0.4 shard_map.92.refs_2_
  41.1 0.1 collective-permute-start.16
  41.2 3.8 %collective-permute-done.12.near_ref = f32[96,512]{1,0:T(8,128)S(1)} collective-permute-done((f32[96,512]{1,0:T(8,128)S(1)}, f32[96,512]{1,0:T(8,128)S(1)}, u32[]{:S(2)}, u32[]{:S(2)}) %collective-permute-start.12) | collective-permute-done | bytes 196640 | tf_op jit(solution)/shard_map/ppermute | solution.py:30
  44.9 0.4 shard_map.91.refs_1_
  45.3 0.1 collective-permute-start.15
  45.4 0.5 collective-permute-start.17
  45.9 0.1 collective-permute-start.13
  45.9 1.0 %collective-permute-done.18.near_ref = f32[64,512]{1,0:T(8,128)S(1)} collective-permute-done((f32[64,512]{1,0:T(8,128)S(1)}, f32[64,512]{1,0:T(8,128)S(1)}, u32[]{:S(2)}, u32[]{:S(2)}) %collective-permute-start.18) | collective-permute-done | bytes 131104 | tf_op jit(solution)/shard_map/ppermute | solution.py:30
  47.0 0.4 shard_map.94.refs_5_.refs_8_
  47.4 0.1 collective-permute-start.19
  47.4 1.3 %collective-permute-done.19.refs_6_.refs_9_ = f32[64,512]{1,0:T(8,128)S(1)} collective-permute-done((f32[64,512]{1,0:T(8,128)S(1)}, f32[64,512]{1,0:T(8,128)S(1)}, u32[]{:S(2)}, u32[]{:S(2)}) %collective-permute-start.19) | collective-permute-done | bytes 131104 | tf_op jit(solution)/shard_map/ppermute | solution.py:30
  48.8 0.0 collective-permute-done.13.refs_0_.refs_7_
  48.8 0.7 shard_map.95.refs_1_
  49.5 1.8 %collective-permute-start.25 = (f32[96,640]{1,0:T(8,128)S(1)}, f32[96,640]{1,0:T(8,128)S(1)}, u32[]{:S(2)}, u32[]{:S(2)}) collective-permute-start(f32[96,640]{1,0:T(8,128)S(1)} %shard_map.95.refs_1_), channel_id=1, source_target_pairs={{0,2},{1,3},{2,0},{3,1},{4,6},{5,7},{6,4},{7,5},{8,10},{9,11},{10,... | collective-permute-start | bytes 737288 | tf_op jit(solution)/shard_map/ppermute | solution.py:30
  51.3 0.0 collective-permute-start.20
  51.3 0.5 shard_map.93.refs_0_
  51.8 0.4 collective-permute-start.24
  52.2 0.4 collective-permute-done.20.refs_0_
  52.6 0.6 shard_map.96.refs_2_
  53.2 0.2 collective-permute-start.23
  53.4 0.4 collective-permute-start.22
  53.8 4.6 %collective-permute-done.25.near1 = f32[96,640]{1,0:T(8,128)S(1)} collective-permute-done((f32[96,640]{1,0:T(8,128)S(1)}, f32[96,640]{1,0:T(8,128)S(1)}, u32[]{:S(2)}, u32[]{:S(2)}) %collective-permute-start.25) | collective-permute-done | bytes 245792 | tf_op jit(solution)/shard_map/ppermute | solution.py:30
  58.4 1.7 %collective-permute-start.28 = (f32[64,512]{1,0:T(8,128)S(1)}, f32[64,512]{1,0:T(8,128)S(1)}, u32[]{:S(2)}, u32[]{:S(2)}) collective-permute-start(f32[64,512]{1,0:T(8,128)S(1)} %shard_map.96.refs_2_), channel_id=1, source_target_pairs={{0,2},{1,3},{2,0},{3,1},{4,6},{5,7},{6,4},{7,5},{8,10},{9,11},{10,... | collective-permute-start | bytes 393224 | tf_op jit(solution)/shard_map/ppermute | solution.py:30
  60.1 0.0 collective-permute-done.23.refs_5_
  60.1 0.2 collective-permute-start.21
  60.3 0.4 collective-permute-done.24.near0
  60.8 0.0 collective-permute-start.26
  60.8 3.6 %collective-permute-done.28.near_ref = f32[64,512]{1,0:T(8,128)S(1)} collective-permute-done((f32[64,512]{1,0:T(8,128)S(1)}, f32[64,512]{1,0:T(8,128)S(1)}, u32[]{:S(2)}, u32[]{:S(2)}) %collective-permute-start.28) | collective-permute-done | bytes 131104 | tf_op jit(solution)/shard_map/ppermute | solution.py:30
  64.3 0.4 shard_map.97
  64.8 0.2 shard_map.98
  65.0 1.4 %shard_map.99.part_ref = f32[512,512]{1,0:T(8,128)S(1)} custom-call(bf16[512,512]{1,0:T(8,128)(2,1)S(1)} %get-tuple-element.38.high_ref, bf16[512,512]{1,0:T(8,128)(2,1)S(1)} %get-tuple-element.39.low_ref, f32[96,384]{1,0:T(8,128)S(1)} %collective-permute-done.24.near0, f32[96,640]{1,0:T(8,128)S(1)} %collective-permute-done.25.near1, ...), custom_call_target="tpu_custom_call" | custom-call | flops 805306368 | bytes 3932160 | tf_op jit(solution)/shard_map/pallas_call | solution.py:96
  66.5 1.1 %shard_map.100 = (f32[64,256]{1,0:T(8,128)S(1)}, f32[72,256]{1,0:T(8,128)S(1)}) custom-call(bf16[512,512]{1,0:T(8,128)(2,1)S(1)} %get-tuple-element.38.high_ref, bf16[512,512]{1,0:T(8,128)(2,1)S(1)} %get-tuple-element.39.low_ref, bf16[512,128]{1,0:T(8,128)(2,1)S(1)} %get-tuple-element.40.end_high_ref, bf16[512,128]{1,0:T(8,128)(2,1)S(1)} %get-tuple-element.41.end_low_ref, ...), custom_call_target="tpu_custom_call" | custom-call | flops 402653184 | bytes 4071424 | tf_op jit(solution)/shard_map/pallas_call | solution.py:96
  67.6 9.2 %collective-permute-start.30 = (f32[72,256]{1,0:T(8,128)S(1)}, f32[72,256]{1,0:T(8,128)S(1)}, u32[]{:S(2)}, u32[]{:S(2)}) collective-permute-start(f32[72,256]{1,0:T(8,128)S(1)} %get-tuple-element.43.send_ref), channel_id=1, source_target_pairs={{0,4},{1,5},{2,6},{3,7},{4,0},{5,1},{6,2},{7,3},{8,12},{9,13},{10,... | collective-permute-start | bytes 221192 | tf_op jit(solution)/shard_map/ppermute | solution.py:30
  76.8 2.9 %collective-permute-done.30.got_ref = f32[72,256]{1,0:T(8,128)S(1)} collective-permute-done((f32[72,256]{1,0:T(8,128)S(1)}, f32[72,256]{1,0:T(8,128)S(1)}, u32[]{:S(2)}, u32[]{:S(2)}) %collective-permute-start.30) | collective-permute-done | bytes 73760 | tf_op jit(solution)/shard_map/ppermute | solution.py:30
  79.7 0.6 shard_map.101
  (16 shorter events, 0.0 us)
Async XLA Ops:
  0.6 26.5 %copy-start = (f32[512,512]{1,0:T(8,128)S(1)}, f32[512,512]{1,0:T(8,128)}, u32[]{:S(2)}) copy-start(f32[512,512]{1,0:T(8,128)} %refs_2_.1) | copy-start | bytes 3145732
  0.6 26.0 %collective-permute-start.2 = (f32[512,512]{1,0:T(8,128)}, f32[512,512]{1,0:T(8,128)S(1)}, u32[]{:S(2)}, u32[]{:S(2)}) collective-permute-start(f32[512,512]{1,0:T(8,128)} %refs_2_.1), channel_id=1, source_target_pairs={{0,3},{1,17},{2,18},{3,0},{4,7},{5,21},{6,22},{7,4},{8,11},{9,25},... | collective-permute-start | bytes 3145736 | tf_op jit(solution)/shard_map/ppermute | solution.py:30
  5.0 18.4 %collective-permute-start.3 = (f32[392,128]{1,0:T(8,128)S(1)}, f32[392,128]{1,0:T(8,128)S(1)}, u32[]{:S(2)}, u32[]{:S(2)}) collective-permute-start(f32[392,128]{1,0:T(8,128)S(1)} %get-tuple-element.24.refs_0_), channel_id=1, source_target_pairs={{0,3},{1,17},{2,18},{3,0},{4,11},{5,9},{6,10},{7,8},{8,7},{9,5},{1... | collective-permute-start | bytes 602120 | tf_op jit(solution)/shard_map/ppermute | solution.py:30
  5.1 18.3 %collective-permute-start.6 = (f32[392,128]{1,0:T(8,128)S(1)}, f32[392,128]{1,0:T(8,128)S(1)}, u32[]{:S(2)}, u32[]{:S(2)}) collective-permute-start(f32[392,128]{1,0:T(8,128)S(1)} %get-tuple-element.25.refs_1_), channel_id=1, source_target_pairs={{0,15},{1,13},{2,14},{3,12},{4,7},{5,21},{6,22},{7,4},{8,11},{9,25... | collective-permute-start | bytes 602120 | tf_op jit(solution)/shard_map/ppermute | solution.py:30
  9.8 16.2 %collective-permute-start.4 = (f32[392,128]{1,0:T(8,128)S(1)}, f32[392,128]{1,0:T(8,128)S(1)}, u32[]{:S(2)}, u32[]{:S(2)}) collective-permute-start(f32[392,128]{1,0:T(8,128)S(1)} %get-tuple-element.26), channel_id=1, source_target_pairs={{0,7},{1,5},{2,6},{3,4},{4,15},{5,13},{6,14},{7,12},{8,3},{9,1},{1... | collective-permute-start | bytes 602120 | tf_op jit(solution)/shard_map/ppermute | solution.py:30
  9.9 16.2 %collective-permute-start.5 = (f32[392,128]{1,0:T(8,128)S(1)}, f32[392,128]{1,0:T(8,128)S(1)}, u32[]{:S(2)}, u32[]{:S(2)}) collective-permute-start(f32[392,128]{1,0:T(8,128)S(1)} %get-tuple-element.27), channel_id=1, source_target_pairs={{0,11},{1,9},{2,10},{3,8},{4,3},{5,1},{6,2},{7,0},{8,15},{9,13},{1... | collective-permute-start | bytes 602120 | tf_op jit(solution)/shard_map/ppermute | solution.py:30
  23.4 3.1 %collective-permute-start = (f32[392,128]{1,0:T(8,128)S(1)}, f32[392,128]{1,0:T(8,128)S(1)}, u32[]{:S(2)}, u32[]{:S(2)}) collective-permute-start(f32[392,128]{1,0:T(8,128)S(1)} %get-tuple-element.24.refs_0_), channel_id=1, source_target_pairs={{0,1},{1,0},{2,3},{3,2},{4,5},{5,4},{6,7},{7,6},{8,9},{9,8},{10,11... | collective-permute-start | bytes 602120 | tf_op jit(solution)/shard_map/ppermute | solution.py:30
  23.5 4.8 %collective-permute-start.1 = (f32[392,128]{1,0:T(8,128)S(1)}, f32[392,128]{1,0:T(8,128)S(1)}, u32[]{:S(2)}, u32[]{:S(2)}) collective-permute-start(f32[392,128]{1,0:T(8,128)S(1)} %get-tuple-element.25.refs_1_), channel_id=1, source_target_pairs={{0,1},{1,0},{2,3},{3,2},{4,5},{5,4},{6,7},{7,6},{8,9},{9,8},{10,11... | collective-permute-start | bytes 602120 | tf_op jit(solution)/shard_map/ppermute | solution.py:30
  26.1 2.2 %collective-permute-start.10 = (f32[392,128]{1,0:T(8,128)S(1)}, f32[392,128]{1,0:T(8,128)S(1)}, u32[]{:S(2)}, u32[]{:S(2)}) collective-permute-start(f32[392,128]{1,0:T(8,128)S(1)} %collective-permute-done.6.refs_7_), channel_id=1, source_target_pairs={{0,1},{1,0},{2,3},{3,2},{4,5},{5,4},{6,7},{7,6},{8,9},{9,8},{10,11... | collective-permute-start | bytes 602120 | tf_op jit(solution)/shard_map/ppermute | solution.py:30
  26.1 2.2 %collective-permute-start.7 = (f32[392,128]{1,0:T(8,128)S(1)}, f32[392,128]{1,0:T(8,128)S(1)}, u32[]{:S(2)}, u32[]{:S(2)}) collective-permute-start(f32[392,128]{1,0:T(8,128)S(1)} %collective-permute-done.3.refs_4_), channel_id=1, source_target_pairs={{0,1},{1,0},{2,3},{3,2},{4,5},{5,4},{6,7},{7,6},{8,9},{9,8},{10,11... | collective-permute-start | bytes 602120 | tf_op jit(solution)/shard_map/ppermute | solution.py:30
  26.6 1.7 %collective-permute-start.8 = (f32[392,128]{1,0:T(8,128)S(1)}, f32[392,128]{1,0:T(8,128)S(1)}, u32[]{:S(2)}, u32[]{:S(2)}) collective-permute-start(f32[392,128]{1,0:T(8,128)S(1)} %collective-permute-done.4.refs_5_), channel_id=1, source_target_pairs={{0,1},{1,0},{2,3},{3,2},{4,5},{5,4},{6,7},{7,6},{8,9},{9,8},{10,11... | collective-permute-start | bytes 602120 | tf_op jit(solution)/shard_map/ppermute | solution.py:30
  26.7 1.7 %collective-permute-start.9 = (f32[392,128]{1,0:T(8,128)S(1)}, f32[392,128]{1,0:T(8,128)S(1)}, u32[]{:S(2)}, u32[]{:S(2)}) collective-permute-start(f32[392,128]{1,0:T(8,128)S(1)} %collective-permute-done.5.refs_6_), channel_id=1, source_target_pairs={{0,1},{1,0},{2,3},{3,2},{4,5},{5,4},{6,7},{7,6},{8,9},{9,8},{10,11... | collective-permute-start | bytes 602120 | tf_op jit(solution)/shard_map/ppermute | solution.py:30
  29.4 2.7 %collective-permute-start.11 = (f32[512,512]{1,0:T(8,128)S(1)}, f32[512,512]{1,0:T(8,128)S(1)}, u32[]{:S(2)}, u32[]{:S(2)}) collective-permute-start(f32[512,512]{1,0:T(8,128)S(1)} %shard_map.88.own_ref), channel_id=1, source_target_pairs={{0,1},{1,0},{2,3},{3,2},{4,5},{5,4},{6,7},{7,6},{8,9},{9,8},{10,11... | collective-permute-start | bytes 3145736 | tf_op jit(solution)/shard_map/ppermute | solution.py:30
  32.9 7.8 %collective-permute-start.14 = (f32[96,512]{1,0:T(8,128)S(1)}, f32[96,512]{1,0:T(8,128)S(1)}, u32[]{:S(2)}, u32[]{:S(2)}) collective-permute-start(f32[96,512]{1,0:T(8,128)S(1)} %get-tuple-element.36), channel_id=1, source_target_pairs={{0,4},{1,5},{2,6},{3,7},{4,0},{5,1},{6,2},{7,3},{8,12},{9,13},{10,... | collective-permute-start | bytes 589832 | tf_op jit(solution)/shard_map/ppermute | solution.py:30
  34.0 11.0 %collective-permute-start.12 = (f32[96,512]{1,0:T(8,128)S(1)}, f32[96,512]{1,0:T(8,128)S(1)}, u32[]{:S(2)}, u32[]{:S(2)}) collective-permute-start(f32[96,512]{1,0:T(8,128)S(1)} %get-tuple-element.31), channel_id=1, source_target_pairs={{0,4},{1,5},{2,6},{3,7},{4,0},{5,1},{6,2},{7,3},{8,12},{9,13},{10,... | collective-permute-start | bytes 589832 | tf_op jit(solution)/shard_map/ppermute | solution.py:30
  34.9 12.0 %collective-permute-start.18 = (f32[64,512]{1,0:T(8,128)S(1)}, f32[64,512]{1,0:T(8,128)S(1)}, u32[]{:S(2)}, u32[]{:S(2)}) collective-permute-start(f32[64,512]{1,0:T(8,128)S(1)} %get-tuple-element.37), channel_id=1, source_target_pairs={{0,4},{1,5},{2,6},{3,7},{4,0},{5,1},{6,2},{7,3},{8,12},{9,13},{10,... | collective-permute-start | bytes 393224 | tf_op jit(solution)/shard_map/ppermute | solution.py:30
  41.1 7.7 %collective-permute-start.16 = (f32[96,512]{1,0:T(8,128)S(1)}, f32[96,512]{1,0:T(8,128)S(1)}, u32[]{:S(2)}, u32[]{:S(2)}) collective-permute-start(f32[96,512]{1,0:T(8,128)S(1)} %shard_map.92.refs_2_), channel_id=1, source_target_pairs={{0,1},{1,0},{2,3},{3,2},{4,5},{5,4},{6,7},{7,6},{8,9},{9,8},{10,11... | collective-permute-start | bytes 589832 | tf_op jit(solution)/shard_map/ppermute | solution.py:30
  45.3 3.5 %collective-permute-start.15 = (f32[96,512]{1,0:T(8,128)S(1)}, f32[96,512]{1,0:T(8,128)S(1)}, u32[]{:S(2)}, u32[]{:S(2)}) collective-permute-start(f32[96,512]{1,0:T(8,128)S(1)} %shard_map.91.refs_1_), channel_id=1, source_target_pairs={{0,1},{1,0},{2,3},{3,2},{4,5},{5,4},{6,7},{7,6},{8,9},{9,8},{10,11... | collective-permute-start | bytes 589832 | tf_op jit(solution)/shard_map/ppermute | solution.py:30
  45.4 3.4 %collective-permute-start.17 = (f32[96,512]{1,0:T(8,128)S(1)}, f32[96,512]{1,0:T(8,128)S(1)}, u32[]{:S(2)}, u32[]{:S(2)}) collective-permute-start(f32[96,512]{1,0:T(8,128)S(1)} %shard_map.92.refs_2_), channel_id=1, source_target_pairs={{0,1},{1,0},{2,3},{3,2},{4,8},{5,9},{6,10},{7,11},{8,4},{9,5},{10,... | collective-permute-start | bytes 589832 | tf_op jit(solution)/shard_map/ppermute | solution.py:30
  45.9 2.9 %collective-permute-start.13 = (f32[96,512]{1,0:T(8,128)S(1)}, f32[96,512]{1,0:T(8,128)S(1)}, u32[]{:S(2)}, u32[]{:S(2)}) collective-permute-start(f32[96,512]{1,0:T(8,128)S(1)} %shard_map.91.refs_1_), channel_id=1, source_target_pairs={{0,1},{1,0},{2,3},{3,2},{4,8},{5,9},{6,10},{7,11},{8,4},{9,5},{10,... | collective-permute-start | bytes 589832 | tf_op jit(solution)/shard_map/ppermute | solution.py:30
  47.4 1.4 %collective-permute-start.19 = (f32[64,512]{1,0:T(8,128)S(1)}, f32[64,512]{1,0:T(8,128)S(1)}, u32[]{:S(2)}, u32[]{:S(2)}) collective-permute-start(f32[64,512]{1,0:T(8,128)S(1)} %shard_map.94.refs_5_.refs_8_), channel_id=1, source_target_pairs={{0,1},{1,0},{2,3},{3,2},{4,5},{5,4},{6,7},{7,6},{8,9},{9,8},{10,11... | collective-permute-start | bytes 393224 | tf_op jit(solution)/shard_map/ppermute | solution.py:30
  49.5 8.9 %collective-permute-start.25 = (f32[96,640]{1,0:T(8,128)S(1)}, f32[96,640]{1,0:T(8,128)S(1)}, u32[]{:S(2)}, u32[]{:S(2)}) collective-permute-start(f32[96,640]{1,0:T(8,128)S(1)} %shard_map.95.refs_1_), channel_id=1, source_target_pairs={{0,2},{1,3},{2,0},{3,1},{4,6},{5,7},{6,4},{7,5},{8,10},{9,11},{10,... | collective-permute-start | bytes 737288 | tf_op jit(solution)/shard_map/ppermute | solution.py:30
  51.3 1.3 %collective-permute-start.20 = (f32[64,512]{1,0:T(8,128)S(1)}, f32[64,512]{1,0:T(8,128)S(1)}, u32[]{:S(2)}, u32[]{:S(2)}) collective-permute-start(f32[64,512]{1,0:T(8,128)S(1)} %shard_map.94.refs_5_.refs_8_), channel_id=1, source_target_pairs={{0,1},{1,0},{2,3},{3,2},{4,8},{5,9},{6,10},{7,11},{8,4},{9,5},{10,... | collective-permute-start | bytes 393224 | tf_op jit(solution)/shard_map/ppermute | solution.py:30
  51.8 9.0 %collective-permute-start.24 = (f32[96,384]{1,0:T(8,128)S(1)}, f32[96,384]{1,0:T(8,128)S(1)}, u32[]{:S(2)}, u32[]{:S(2)}) collective-permute-start(f32[96,384]{1,0:T(8,128)S(1)} %shard_map.93.refs_0_), channel_id=1, source_target_pairs={{0,2},{1,3},{2,0},{3,1},{4,6},{5,7},{6,4},{7,5},{8,10},{9,11},{10,... | collective-permute-start | bytes 442376 | tf_op jit(solution)/shard_map/ppermute | solution.py:30
  53.2 6.9 %collective-permute-start.23 = (f32[64,512]{1,0:T(8,128)S(1)}, f32[64,512]{1,0:T(8,128)S(1)}, u32[]{:S(2)}, u32[]{:S(2)}) collective-permute-start(f32[64,512]{1,0:T(8,128)S(1)} %shard_map.96.refs_2_), channel_id=1, source_target_pairs={{0,1},{1,0},{2,3},{3,2},{4,5},{5,4},{6,7},{7,6},{8,9},{9,8},{10,11... | collective-permute-start | bytes 393224 | tf_op jit(solution)/shard_map/ppermute | solution.py:30
  53.4 10.9 %collective-permute-start.22 = (f32[96,640]{1,0:T(8,128)S(1)}, f32[96,640]{1,0:T(8,128)S(1)}, u32[]{:S(2)}, u32[]{:S(2)}) collective-permute-start(f32[96,640]{1,0:T(8,128)S(1)} %shard_map.95.refs_1_), channel_id=1, source_target_pairs={{0,1},{1,0},{2,3},{3,2},{4,5},{5,4},{6,7},{7,6},{8,9},{9,8},{10,11... | collective-permute-start | bytes 737288 | tf_op jit(solution)/shard_map/ppermute | solution.py:30
  58.4 6.6 %collective-permute-start.27 = (f32[96,640]{1,0:T(8,128)S(1)}, f32[96,640]{1,0:T(8,128)S(1)}, u32[]{:S(2)}, u32[]{:S(2)}) collective-permute-start(f32[96,640]{1,0:T(8,128)S(1)} %collective-permute-done.25.near1), channel_id=1, source_target_pairs={{0,1},{1,0},{2,3},{3,2},{4,5},{5,4},{6,7},{7,6},{8,9},{9,8},{10,11... | collective-permute-start | bytes 737288 | tf_op jit(solution)/shard_map/ppermute | solution.py:30
  58.4 5.9 %collective-permute-start.28 = (f32[64,512]{1,0:T(8,128)S(1)}, f32[64,512]{1,0:T(8,128)S(1)}, u32[]{:S(2)}, u32[]{:S(2)}) collective-permute-start(f32[64,512]{1,0:T(8,128)S(1)} %shard_map.96.refs_2_), channel_id=1, source_target_pairs={{0,2},{1,3},{2,0},{3,1},{4,6},{5,7},{6,4},{7,5},{8,10},{9,11},{10,... | collective-permute-start | bytes 393224 | tf_op jit(solution)/shard_map/ppermute | solution.py:30
  60.1 4.2 %collective-permute-start.21 = (f32[96,384]{1,0:T(8,128)S(1)}, f32[96,384]{1,0:T(8,128)S(1)}, u32[]{:S(2)}, u32[]{:S(2)}) collective-permute-start(f32[96,384]{1,0:T(8,128)S(1)} %shard_map.93.refs_0_), channel_id=1, source_target_pairs={{0,1},{1,0},{2,3},{3,2},{4,5},{5,4},{6,7},{7,6},{8,9},{9,8},{10,11... | collective-permute-start | bytes 442376 | tf_op jit(solution)/shard_map/ppermute | solution.py:30
  60.8 4.3 %collective-permute-start.26 = (f32[96,384]{1,0:T(8,128)S(1)}, f32[96,384]{1,0:T(8,128)S(1)}, u32[]{:S(2)}, u32[]{:S(2)}) collective-permute-start(f32[96,384]{1,0:T(8,128)S(1)} %collective-permute-done.24.near0), channel_id=1, source_target_pairs={{0,1},{1,0},{2,3},{3,2},{4,5},{5,4},{6,7},{7,6},{8,9},{9,8},{10,11... | collective-permute-start | bytes 442376 | tf_op jit(solution)/shard_map/ppermute | solution.py:30
  64.3 2.1 %collective-permute-start.29 = (f32[64,512]{1,0:T(8,128)S(1)}, f32[64,512]{1,0:T(8,128)S(1)}, u32[]{:S(2)}, u32[]{:S(2)}) collective-permute-start(f32[64,512]{1,0:T(8,128)S(1)} %collective-permute-done.28.near_ref), channel_id=1, source_target_pairs={{0,1},{1,0},{2,3},{3,2},{4,5},{5,4},{6,7},{7,6},{8,9},{9,8},{10,11... | collective-permute-start | bytes 393224 | tf_op jit(solution)/shard_map/ppermute | solution.py:30
  67.6 12.1 %collective-permute-start.30 = (f32[72,256]{1,0:T(8,128)S(1)}, f32[72,256]{1,0:T(8,128)S(1)}, u32[]{:S(2)}, u32[]{:S(2)}) collective-permute-start(f32[72,256]{1,0:T(8,128)S(1)} %get-tuple-element.43.send_ref), channel_id=1, source_target_pairs={{0,4},{1,5},{2,6},{3,7},{4,0},{5,1},{6,2},{7,3},{8,12},{9,13},{10,... | collective-permute-start | bytes 221192 | tf_op jit(solution)/shard_map/ppermute | solution.py:30
